TPU v7x, 512 devices: a whole 4x8x8 slice. The times are simulated.
512 devices in a mesh: seq: 64 (over y, x, core), head: 8 (over z).
Axes of the slice: x: 4, y: 8, z: 8, core: 2. Of those that a mesh axis runs over, the one named last changes fastest.
Arguments:
- token_values: bfloat16 [24576, 4096], P('seq', 'head'), may hold values from -6 to 6
- b_inputs: bfloat16 [24576, 128], P('seq'), may hold values from -6 to 6
- c_inputs: bfloat16 [24576, 128], P('seq'), may hold values from -6 to 6
- log_decay: float32 [64, 24576], P('head', 'seq'), may hold values from -1 to 0
- grad_out: bfloat16 [24576, 4096], P('seq', 'head'), may hold values from -0.005859375 to 0.005859375
Outputs:
- grad_values: bfloat16 [24576, 4096], P('seq', 'head')
- grad_b: bfloat16 [24576, 128], P('seq')
- grad_c: bfloat16 [24576, 128], P('seq')
All inputs are finite; a program needn't handle non-finite values.
Results may differ from a plain program's by a relative error of at most 0.014.
Values may be sent and summed in bfloat16 or wider, within the bound.
A program may use at most 128 MiB of HBM per device.

v0:
```python
import jax
import jax.numpy as jnp
from jax import lax
from jax.sharding import PartitionSpec as P

PRECISE = lax.Precision.HIGHEST


def entering(part, axis, combine, identity, reverse):
    count = lax.axis_size(axis)
    place = lax.axis_index(axis)
    ahead = count - 1 - place if reverse else place
    gathered = jax.tree.map(lambda a: lax.all_gather(a, axis), part)
    state = jax.tree.map(lambda a, e: jnp.zeros_like(a) + jnp.asarray(e, a.dtype), part, identity)

    def one(lap, state):
        source = count - 1 - lap if reverse else lap
        return combine(
            state, jax.tree.map(lambda a: lax.dynamic_index_in_dim(a, source, 0, False), gathered)
        )

    return lax.fori_loop(0, ahead, one, state)


def spread(values, width):
    return jnp.repeat(values, width)[None, :]


def shards(token_values, b_inputs, c_inputs, log_decay, grad_out):
    length = token_values.shape[0]
    heads_here = log_decay.shape[0]
    head_dim = token_values.shape[1] // heads_here
    state_size = b_inputs.shape[1]
    cumulative = jnp.cumsum(log_decay, axis=1)
    block_log = cumulative[:, -1]
    into_end = jnp.exp(block_log[:, None] - cumulative)
    from_start = jnp.exp(cumulative)
    block_decay = jnp.exp(block_log)
    b_float = b_inputs.astype(jnp.float32)
    c_float = c_inputs.astype(jnp.float32)
    decayed_b = (into_end[:, :, None] * b_float[None]).astype(jnp.bfloat16)
    decayed_c = (from_start[:, :, None] * c_float[None]).astype(jnp.bfloat16)
    x_heads = token_values.reshape(length, heads_here, head_dim)
    dy_heads = grad_out.reshape(length, heads_here, head_dim)
    state_local = jnp.einsum(
        "htn,thp->nhp", decayed_b, x_heads, preferred_element_type=jnp.float32
    ).reshape(state_size, heads_here * head_dim)
    adjoint_local = jnp.einsum(
        "hsn,shp->nhp", decayed_c, dy_heads, preferred_element_type=jnp.float32
    ).reshape(state_size, heads_here * head_dim)

    def forward_combine(earlier, later):
        return (earlier[0] * later[0], spread(later[0], head_dim) * earlier[1] + later[1])

    def backward_combine(earlier, later):
        return (earlier[0] * later[0], later[1] + spread(later[0], head_dim) * earlier[1])

    identity = (jnp.ones((heads_here,), jnp.float32), jnp.zeros_like(state_local))
    carried_decay, state_in = entering(
        (block_decay, state_local), "seq", forward_combine, identity, False
    )
    later_decay, adjoint_out = entering(
        (block_decay, adjoint_local), "seq", backward_combine, identity, True
    )
    scores = lax.dot_general(
        c_inputs, b_inputs, (((1,), (1,)), ((), ())), preferred_element_type=jnp.float32
    )
    entry_indices = lax.iota(jnp.int32, length)
    causal = entry_indices[:, None] >= entry_indices[None, :]

    def head_step(head_idx, carried):
        running, dx_local = carried
        cum_head = lax.dynamic_index_in_dim(cumulative, head_idx, 0, keepdims=False)
        log_gaps = cum_head[:, None] - cum_head[None, :]
        decays = jnp.where(causal, jnp.exp(jnp.where(causal, log_gaps, 0.0)), 0.0)
        mixing = (scores * decays).astype(jnp.bfloat16)
        x_head = lax.dynamic_slice_in_dim(token_values, head_idx * head_dim, head_dim, 1)
        dy_head = lax.dynamic_slice_in_dim(grad_out, head_idx * head_dim, head_dim, 1)
        dx_head = lax.dot_general(
            mixing, dy_head, (((0,), (0,)), ((), ())), preferred_element_type=jnp.float32
        )
        dot_pairs = lax.dot_general(
            dy_head, x_head, (((1,), (1,)), ((), ())), preferred_element_type=jnp.float32
        )
        dx_local = lax.dynamic_update_slice_in_dim(dx_local, dx_head, head_idx * head_dim, 1)
        return (running + decays * dot_pairs, dx_local)

    start_pair = (
        jnp.zeros((length, length), jnp.float32),
        jnp.zeros((length, heads_here * head_dim), jnp.float32),
    )
    running, dx_local = lax.fori_loop(0, heads_here, head_step, start_pair)
    weighted = running.astype(jnp.bfloat16)
    db_part = lax.dot_general(
        weighted, c_inputs, (((0,), (0,)), ((), ())), preferred_element_type=jnp.float32
    )
    dc_part = jnp.dot(weighted, b_inputs, preferred_element_type=jnp.float32)
    to_end_cols = jnp.repeat(into_end.T, head_dim, axis=1)
    from_start_cols = jnp.repeat(from_start.T, head_dim, axis=1)
    grad_values = dx_local + to_end_cols * jnp.dot(b_float, adjoint_out, precision=PRECISE)
    db_part = db_part + jnp.dot(
        token_values.astype(jnp.float32) * to_end_cols, adjoint_out.T, precision=PRECISE
    )
    dc_part = dc_part + jnp.dot(
        grad_out.astype(jnp.float32) * from_start_cols, state_in.T, precision=PRECISE
    )
    grad_b, grad_c = (
        lax.psum(db_part.astype(jnp.bfloat16), "head").astype(jnp.float32),
        lax.psum(dc_part.astype(jnp.bfloat16), "head").astype(jnp.float32),
    )
    return (
        grad_values.astype(jnp.bfloat16),
        grad_b.astype(jnp.bfloat16),
        grad_c.astype(jnp.bfloat16),
    )


def solution(mesh):
    in_specs = (
        P("seq", "head"),
        P("seq", None),
        P("seq", None),
        P("head", "seq"),
        P("seq", "head"),
    )
    out_specs = (P("seq", "head"), P("seq", None), P("seq", None))
    return jax.shard_map(shards, mesh=mesh, in_specs=in_specs, out_specs=out_specs, check_vma=False)
```

profile of v0, /device:TPU:6, one launch (start us, length us, event | category | flops | bytes accessed | tf_op | source)
XLA Modules:
  0.0 438.4 jit_solution(4823493083981168481)
XLA Ops:
  7.2 1.9 reduce-window.6
  11.0 1.2 copy.24
  15.6 1.3 dynamic-slice
  17.8 115.8 %all-reduce = f32[512]{0:T(512)S(1)} all-reduce(f32[512]{0:T(512)S(1)} %dynamic-update-slice), channel_id=2, replica_groups=mesh['seq'=64,'head'=8] {'seq'}, use_global_device_ids=true, to_apply=%add | all-reduce | flops 512 | bytes 4096
  134.4 1.1 fusion.29
  135.5 27.8 %while.45 = (s32[]{:T(128)}, f32[384,384]{1,0:T(8,128)S(1)}, f32[384,512]{0,1:T(8,128)S(1)}, f32[8,384]{1,0:T(8,128)}, bf16[384,512]{1,0:T(8,128)(2,1)}, /*index...) while((s32[]{:T(128)}, f32[384,384]{1,0:T(8,128)S(1)}, ...), condition=%wide.region_3.4_spmd.clone.clone, body=%wide.region_2.3_spmd.clone.clone.sunk | while | flops 39665672 | bytes 4536012 | solution.py:92
  136.3 1.4 fusion.51
  137.8 1.2 convolution_dynamic-update-slice_fusion.2
  139.8 1.4 fusion.51
  141.2 1.2 convolution_dynamic-update-slice_fusion.2
  143.3 1.4 fusion.51
  144.7 1.2 convolution_dynamic-update-slice_fusion.2
  146.8 1.4 fusion.51
  148.2 1.2 convolution_dynamic-update-slice_fusion.2
  150.2 1.4 fusion.51
  151.7 1.2 convolution_dynamic-update-slice_fusion.2
  153.7 1.4 fusion.51
  155.1 1.2 convolution_dynamic-update-slice_fusion.2
  157.2 1.4 fusion.51
  158.6 1.2 convolution_dynamic-update-slice_fusion.2
  160.7 1.4 fusion.51
  162.1 1.2 convolution_dynamic-update-slice_fusion.2
  163.4 11.5 %while.44 = (s32[]{:T(128)}, f32[128,512]{1,0:T(8,128)S(1)}, s32[]{:T(128)}, f32[64,8]{1,0:T(8,128)}, f32[64,128,512]{2,1,0:T(8,128)}, /*index=5*/s32[]{:T(128)}, s32[]{:T(128)}, s32[]{:T(128)}) while((s32[]{:T(128)}, f32[128,512]{1,0:T(8,128)S(1)}, s32[]{:T(128)}, f32[64,8]{1,0:T(8,128)}, f32[64,128,512]{2,1,0:T(8,128)}, ...), condition=%wide.region_8.9_spmd, body=%wide.region_7.8_spmd.sunk | while | flops 131077 | bytes 794855 | solution.py:22
  166.2 1.1 bitcast_add_fusion.5
  168.1 1.1 bitcast_add_fusion.5
  174.9 53.5 %all-gather.4.cloned.1.call-done = f32[64,128,512]{2,1,0:T(8,128)} async-done(((f32[1,128,512]{2,1,0:T(8,128)}), f32[64,128,512]{2,1,0:T(8,128)}) %all-gather.4.cloned.1.call-update) | async-done | bytes 16777232 | tf_op jit(solution)/shard_map/all_gather | solution.py:13
  228.4 109.5 %while.43 = (s32[]{:T(128)}, f32[128,512]{1,0:T(8,128)S(1)}, s32[]{:T(128)}, f32[64,128,512]{2,1,0:T(8,128)}, f32[64,8]{1,0:T(8,128)}, /*index=5*/s32[]{:T(128)}, s32[]{:T(128)}, s32[]{:T(128)}, s32[]{:T(128)}) while((s32[]{:T(128)}, f32[128,512]{1,0:T(8,128)S(1)}, s32[]{:T(128)}, f32[64,128,512]{2,1,0:T(8,128)}, f32[64,8]{1,0:T(8,128)}, ...), condition=%wide.region_5.6_spmd, body=%wide.region_4.5_spmd.sunk | while | flops 131078 | bytes 794875 | solution.py:22
  338.0 1.4 fusion.31
  339.4 1.4 fusion.30
  344.4 84.4 %all-reduce.4.cloned.1.call-done = (bf16[384,128]{1,0:T(8,128)(2,1)}, bf16[384,128]{1,0:T(8,128)(2,1)}) async-done(((bf16[384,128]{1,0:T(8,128)(2,1)}, bf16[384,128]{1,0:T(8,128)(2,1)}), (bf16[384,128]{1,0:T(8,128)(2,1)}, bf16[384,128]{1,0:T(8,128)(2,1)})) %all-reduce.4.cloned.1.call-update) | async-done | bytes 196624 | tf_op jit(solution)/shard_map/psum | solution.py:108
  428.8 1.5 copy.56
  430.4 1.5 copy.57
  (321 shorter events, 133.6 us)
Async XLA Ops:
  7.2 6.6 %copy-start.3 = (bf16[384,128]{1,0:T(8,128)(2,1)S(1)}, bf16[384,128]{1,0:T(8,128)(2,1)}, u32[]{:S(2)}) copy-start(bf16[384,128]{1,0:T(8,128)(2,1)} %param.13) | copy-start | bytes 294916
  7.2 156.2 %all-gather.6.cloned.1.call-start = ((), (), s32[]{:S(2)}) async-start(), calls=%async_computation.1 | async-start | bytes 17039360 | tf_op jit(solution)/shard_map/all_gather | solution.py:13
  9.4 0.6 copy-start.7
  10.0 3.7 copy-start.6
  13.7 214.7 %all-gather.4.cloned.1.call-start = ((), (), s32[]{:S(2)}) async-start(), calls=%async_computation | async-start | bytes 17039360 | tf_op jit(solution)/shard_map/all_gather | solution.py:13
  14.6 119.7 %copy-start = (bf16[384,128]{1,0:T(8,128)(2,1)S(1)}, bf16[384,128]{1,0:T(8,128)(2,1)}, u32[]{:S(2)}) copy-start(bf16[384,128]{1,0:T(8,128)(2,1)} %param.12) | copy-start | bytes 294916
  15.5 413.3 %all-reduce.4.cloned.1.call-start = ((), (), s32[]{:S(2)}) async-start(), calls=%async_computation.2 | async-start | bytes 393216 | tf_op jit(solution)/shard_map/psum | solution.py:108
  135.5 2.2 copy-start.5
  139.0 2.2 copy-start.5
  142.5 2.2 copy-start.5
  146.0 2.2 copy-start.5
  149.4 2.2 copy-start.5
  152.9 2.2 copy-start.5
  156.4 2.2 copy-start.5
  159.8 2.2 copy-start.5
  338.0 2.9 copy-start.4
  338.0 3.8 copy-start.1
  340.8 1.9 copy-start.2
Sparse Core Ops, SparseCore 0:
  13.8 108.1 all-gather.5
  125.9 102.4 all-gather.3
  342.8 85.9 all-reduce.3
where the time goes:
time: 443 us; the launch traced here: 438 us
  waiting for transfers between devices  138 us (31%)
  blocking collectives  116 us (26%)
  local copies, waits for them, and re-layouts  69.9 us (16%)
  other arithmetic  69.4 us (16%)
  matrix products  28.6 us (6%)
  between operations  14.6 us (3%)
    unnamed x1, blocking collectives  116 us
    psum x1, waiting for transfers between devices, shards(): lax.psum(db_part.astype(jnp.bfloat16), 'head').astype(jnp.float32)  84.4 us
    add x57, other arithmetic, backward_combine(): later[1] + spread(later[0], head_dim) * earlier[1]  59.9 us
    all_gather x2, waiting for transfers between devices, entering(): gathered = jax.tree.map(lambda a: lax.all_gather(a, axis), part)  53.5 us
    squeeze x63, local copies, waits for them, and re-layouts, one(): lax.dynamic_index_in_dim(a, source, 0, False)  43.9 us
    dot_general x8, matrix products, head_step(): lax.dot_general(dy_head, x_head, (((1,), (1,)), ((), ())), preferred_elem...  11.2 us
    dot_general x8, matrix products, head_step(): lax.dot_general(mixing, dy_head, (((0,), (0,)), ((), ())), preferred_elem...  9.84 us
  transfers between devices with their start and end apart: 3, of which 2 were waited for; matrix products, arithmetic and copies ran while one was open for 10% of the time, Pallas kernels for 0%

commit v1 on v0

--- a/solution.py
+++ b/solution.py
@@ -1,3 +1,5 @@
+import functools
+
 import jax
 import jax.numpy as jnp
 from jax import lax
@@ -6,27 +8,29 @@
 PRECISE = lax.Precision.HIGHEST
 
 
-def entering(part, axis, combine, identity, reverse):
-    count = lax.axis_size(axis)
-    place = lax.axis_index(axis)
-    ahead = count - 1 - place if reverse else place
-    gathered = jax.tree.map(lambda a: lax.all_gather(a, axis), part)
-    state = jax.tree.map(lambda a, e: jnp.zeros_like(a) + jnp.asarray(e, a.dtype), part, identity)
-
-    def one(lap, state):
-        source = count - 1 - lap if reverse else lap
-        return combine(
-            state, jax.tree.map(lambda a: lax.dynamic_index_in_dim(a, source, 0, False), gathered)
-        )
-
-    return lax.fori_loop(0, ahead, one, state)
+def shift(value, count, distance, reverse):
+    if reverse:
+        pairs = [(p, p - distance) for p in range(distance, count)]
+    else:
+        pairs = [(p, p + distance) for p in range(count - distance)]
+    return lax.ppermute(value, "seq", pairs)
 
 
-def spread(values, width):
-    return jnp.repeat(values, width)[None, :]
+def exclusive_scans(count, decay_cols, parts):
+    packed = [jnp.concatenate([decay_cols, s], axis=0) for s, _ in parts]
+    windows = [shift(pk, count, 1, rev) for pk, (_, rev) in zip(packed, parts)]
+    distance = 1
+    while distance < count:
+        received = [shift(w, count, distance, rev) for w, (_, rev) in zip(windows, parts)]
+        windows = [
+            jnp.concatenate([w[:1] * r[:1], w[1:] + w[:1] * r[1:]], axis=0)
+            for w, r in zip(windows, received)
+        ]
+        distance *= 2
+    return [w[1:] for w in windows]
 
 
-def shards(token_values, b_inputs, c_inputs, log_decay, grad_out):
+def shards(count, token_values, b_inputs, c_inputs, log_decay, grad_out):
     length = token_values.shape[0]
     heads_here = log_decay.shape[0]
     head_dim = token_values.shape[1] // heads_here
@@ -48,19 +52,9 @@
     adjoint_local = jnp.einsum(
         "hsn,shp->nhp", decayed_c, dy_heads, preferred_element_type=jnp.float32
     ).reshape(state_size, heads_here * head_dim)
-
-    def forward_combine(earlier, later):
-        return (earlier[0] * later[0], spread(later[0], head_dim) * earlier[1] + later[1])
-
-    def backward_combine(earlier, later):
-        return (earlier[0] * later[0], later[1] + spread(later[0], head_dim) * earlier[1])
-
-    identity = (jnp.ones((heads_here,), jnp.float32), jnp.zeros_like(state_local))
-    carried_decay, state_in = entering(
-        (block_decay, state_local), "seq", forward_combine, identity, False
-    )
-    later_decay, adjoint_out = entering(
-        (block_decay, adjoint_local), "seq", backward_combine, identity, True
+    decay_cols = jnp.repeat(block_decay, head_dim)[None, :]
+    state_in, adjoint_out = exclusive_scans(
+        count, decay_cols, [(state_local, False), (adjoint_local, True)]
     )
     scores = lax.dot_general(
         c_inputs, b_inputs, (((1,), (1,)), ((), ())), preferred_element_type=jnp.float32
@@ -124,4 +118,5 @@
         P("seq", "head"),
     )
     out_specs = (P("seq", "head"), P("seq", None), P("seq", None))
-    return jax.shard_map(shards, mesh=mesh, in_specs=in_specs, out_specs=out_specs, check_vma=False)
+    body = functools.partial(shards, mesh.shape["seq"])
+    return jax.shard_map(body, mesh=mesh, in_specs=in_specs, out_specs=out_specs, check_vma=False)

time: 443 us -> 235 us (0.53)
  the two profiles are of different devices: /device:TPU:6 before, /device:TPU:2 now
where the time goes in v1:
time: 235 us; the launch traced here: 233 us
  waiting for transfers between devices  119 us (51%)
  starting transfers between devices  57.6 us (25%)
  matrix products  27.7 us (12%)
  between operations  14.5 us (6%)
  other arithmetic  7.18 us (3%)
  local copies, waits for them, and re-layouts  7.07 us (3%)
    psum x1, waiting for transfers between devices, shards(): lax.psum(db_part.astype(jnp.bfloat16), 'head').astype(jnp.float32)  84.9 us
    ppermute x14, starting transfers between devices, shift(): return lax.ppermute(value, 'seq', pairs)  57.5 us
    ppermute x14, waiting for transfers between devices, shift(): return lax.ppermute(value, 'seq', pairs)  34 us
    dot_general x8, matrix products, head_step(): lax.dot_general(dy_head, x_head, (((1,), (1,)), ((), ())), preferred_elem...  11.2 us
    dot_general x8, matrix products, head_step(): lax.dot_general(mixing, dy_head, (((0,), (0,)), ((), ())), preferred_elem...  9.8 us
    unnamed x11, local copies, waits for them, and re-layouts  6.02 us
  transfers between devices with their start and end apart: 15, of which 10 were waited for; matrix products, arithmetic and copies ran while one was open for 13% of the time, Pallas kernels for 0%

profile of v1, /device:TPU:2, one launch (start us, length us, event | category | flops | bytes accessed | tf_op | source)
XLA Modules:
  0.0 233.3 jit_solution(7088750057124576250)
XLA Ops:
  7.2 1.9 reduce-window.6
  14.2 1.9 collective-permute-start
  16.1 2.4 %collective-permute-start.7 = (f32[129,512]{1,0:T(8,128)S(1)}, f32[129,512]{1,0:T(8,128)}, u32[]{:S(2)}, u32[]{:S(2)}) collective-permute-start(f32[129,512]{1,0:T(8,128)S(1)} %get-tuple-element.224), channel_id=1, source_target_pairs={{0,8},{8,16},{16,24},{24,32},{32,40},{40,48},{48,56},{56,64},{64,7... | collective-permute-start | bytes 792584 | tf_op jit(solution)/shard_map/ppermute | solution.py:16
  18.9 21.5 %while.17 = (s32[]{:T(128)}, f32[384,384]{1,0:T(8,128)S(1)}, f32[384,512]{0,1:T(8,128)S(1)}, f32[8,384]{1,0:T(8,128)S(1)}, bf16[384,512]{1,0:T(8,128)(2,1)}, /*i...) while((s32[]{:T(128)}, f32[384,384]{1,0:T(8,128)S(1)}, ...), condition=%wide.region_3.4_spmd.clone.clone, body=%wide.region_2.3_spmd.clone.clone.sunk | while | flops 39665672 | bytes 2176688 | solution.py:86
  18.9 1.4 fusion.64
  21.6 1.4 fusion.64
  24.3 1.4 fusion.64
  27.0 1.4 fusion.64
  29.7 1.4 fusion.64
  32.3 1.4 fusion.64
  35.0 1.4 fusion.64
  37.7 1.4 fusion.64
  40.4 7.4 %collective-permute-start.1 = (f32[129,512]{1,0:T(8,128)}, f32[129,512]{1,0:T(8,128)S(1)}, u32[]{:S(2)}, u32[]{:S(2)}) collective-permute-start(f32[129,512]{1,0:T(8,128)} %collective-permute-done), channel_id=1, source_target_pairs={{8,0},{16,8},{24,16},{32,24},{40,32},{48,40},{56,48},{64,56},{72,6... | collective-permute-start | bytes 792584 | tf_op jit(solution)/shard_map/ppermute | solution.py:16
  48.5 1.9 collective-permute-start.8
  50.4 1.8 collective-permute-done.1
  53.9 1.9 collective-permute-start.2
  58.3 3.3 %collective-permute-start.9 = (f32[129,512]{1,0:T(8,128)S(1)}, f32[129,512]{1,0:T(8,128)S(1)}, u32[]{:S(2)}, u32[]{:S(2)}) collective-permute-start(f32[129,512]{1,0:T(8,128)S(1)} %pad_maximum_fusion.7), channel_id=1, source_target_pairs={{0,16},{8,24},{16,32},{24,40},{32,48},{40,56},{48,64},{56,72},{64,... | collective-permute-start | bytes 792584 | tf_op jit(solution)/shard_map/ppermute | solution.py:16
  63.8 11.6 %collective-permute-done.9 = f32[129,512]{1,0:T(8,128)S(1)} collective-permute-done((f32[129,512]{1,0:T(8,128)S(1)}, f32[129,512]{1,0:T(8,128)S(1)}, u32[]{:S(2)}, u32[]{:S(2)}) %collective-permute-start.9) | collective-permute-done | bytes 264224 | tf_op jit(solution)/shard_map/ppermute | solution.py:16
  75.5 2.3 collective-permute-start.10
  78.0 1.3 collective-permute-start.4
  79.3 5.3 %collective-permute-done.10 = f32[129,512]{1,0:T(8,128)S(1)} collective-permute-done((f32[129,512]{1,0:T(8,128)S(1)}, f32[129,512]{1,0:T(8,128)S(1)}, u32[]{:S(2)}, u32[]{:S(2)}) %collective-permute-start.10) | collective-permute-done | bytes 264224 | tf_op jit(solution)/shard_map/ppermute | solution.py:16
  84.7 7.9 %collective-permute-start.11 = (f32[129,512]{1,0:T(8,128)S(1)}, f32[129,512]{1,0:T(8,128)S(1)}, u32[]{:S(2)}, u32[]{:S(2)}) collective-permute-start(f32[129,512]{1,0:T(8,128)S(1)} %pad_maximum_fusion.9), channel_id=1, source_target_pairs={{0,64},{8,72},{16,80},{24,88},{32,96},{40,104},{48,112},{56,120},{... | collective-permute-start | bytes 792584 | tf_op jit(solution)/shard_map/ppermute | solution.py:16
  94.0 4.1 %collective-permute-done.11 = f32[129,512]{1,0:T(8,128)S(1)} collective-permute-done((f32[129,512]{1,0:T(8,128)S(1)}, f32[129,512]{1,0:T(8,128)S(1)}, u32[]{:S(2)}, u32[]{:S(2)}) %collective-permute-start.11) | collective-permute-done | bytes 264224 | tf_op jit(solution)/shard_map/ppermute | solution.py:16
  98.3 5.4 %collective-permute-start.12 = (f32[129,512]{1,0:T(8,128)S(1)}, f32[129,512]{1,0:T(8,128)S(1)}, u32[]{:S(2)}, u32[]{:S(2)}) collective-permute-start(f32[129,512]{1,0:T(8,128)S(1)} %pad_maximum_fusion.10), channel_id=1, source_target_pairs={{0,128},{8,136},{16,144},{24,152},{32,160},{40,168},{48,176},{56,1... | collective-permute-start | bytes 792584 | tf_op jit(solution)/shard_map/ppermute | solution.py:16
  103.7 5.6 %collective-permute-done.5 = f32[129,512]{1,0:T(8,128)S(1)} collective-permute-done((f32[129,512]{1,0:T(8,128)S(1)}, f32[129,512]{1,0:T(8,128)S(1)}, u32[]{:S(2)}, u32[]{:S(2)}) %collective-permute-start.5) | collective-permute-done | bytes 264224 | tf_op jit(solution)/shard_map/ppermute | solution.py:16
  110.8 17.8 %collective-permute-start.13 = (f32[129,512]{1,0:T(8,128)S(1)}, f32[129,512]{1,0:T(8,128)S(1)}, u32[]{:S(2)}, u32[]{:S(2)}) collective-permute-start(f32[129,512]{1,0:T(8,128)S(1)} %pad_maximum_fusion.11), channel_id=1, source_target_pairs={{0,256},{8,264},{16,272},{24,280},{32,288},{40,296},{48,304},{56,3... | collective-permute-start | bytes 792584 | tf_op jit(solution)/shard_map/ppermute | solution.py:16
  129.2 2.1 fusion.18
  131.3 3.5 %collective-permute-done.13 = f32[129,512]{1,0:T(8,128)S(1)} collective-permute-done((f32[129,512]{1,0:T(8,128)S(1)}, f32[129,512]{1,0:T(8,128)S(1)}, u32[]{:S(2)}, u32[]{:S(2)}) %collective-permute-start.13) | collective-permute-done | bytes 264224 | tf_op jit(solution)/shard_map/ppermute | solution.py:16
  134.7 2.1 fusion.19
  138.5 84.9 %all-reduce.3.cloned.1.call-done = (bf16[384,128]{1,0:T(8,128)(2,1)}, bf16[384,128]{1,0:T(8,128)(2,1)}) async-done(((bf16[384,128]{1,0:T(8,128)(2,1)}, bf16[384,128]{1,0:T(8,128)(2,1)}), (bf16[384,128]{1,0:T(8,128)(2,1)}, bf16[384,128]{1,0:T(8,128)(2,1)})) %all-reduce.3.cloned.1.call-update) | async-done | bytes 196624 | tf_op jit(solution)/shard_map/psum | solution.py:102
  223.4 1.5 copy.32
  224.9 1.5 copy.33
  (92 shorter events, 27.6 us)
Async XLA Ops:
  7.2 3.9 %copy-start = (bf16[384,128]{1,0:T(8,128)(2,1)S(1)}, bf16[384,128]{1,0:T(8,128)(2,1)}, u32[]{:S(2)}) copy-start(bf16[384,128]{1,0:T(8,128)(2,1)} %param.8) | copy-start | bytes 294916
  7.2 216.2 %all-reduce.3.cloned.1.call-start = ((), (), s32[]{:S(2)}) async-start(), calls=%async_computation | async-start | bytes 393216 | tf_op jit(solution)/shard_map/psum | solution.py:102
  11.1 1.0 copy-start.2
  11.7 0.9 copy-start.1
  14.2 26.1 %collective-permute-start = (f32[129,512]{1,0:T(8,128)}, f32[129,512]{1,0:T(8,128)}, u32[]{:S(2)}, u32[]{:S(2)}) collective-permute-start(f32[129,512]{1,0:T(8,128)} %get-tuple-element.225), channel_id=1, source_target_pairs={{8,0},{16,8},{24,16},{32,24},{40,32},{48,40},{56,48},{64,56},{72,6... | collective-permute-start | bytes 792584 | tf_op jit(solution)/shard_map/ppermute | solution.py:16
  16.1 32.3 %collective-permute-start.7 = (f32[129,512]{1,0:T(8,128)S(1)}, f32[129,512]{1,0:T(8,128)}, u32[]{:S(2)}, u32[]{:S(2)}) collective-permute-start(f32[129,512]{1,0:T(8,128)S(1)} %get-tuple-element.224), channel_id=1, source_target_pairs={{0,8},{8,16},{16,24},{24,32},{32,40},{40,48},{48,56},{56,64},{64,7... | collective-permute-start | bytes 792584 | tf_op jit(solution)/shard_map/ppermute | solution.py:16
  40.4 11.8 %collective-permute-start.1 = (f32[129,512]{1,0:T(8,128)}, f32[129,512]{1,0:T(8,128)S(1)}, u32[]{:S(2)}, u32[]{:S(2)}) collective-permute-start(f32[129,512]{1,0:T(8,128)} %collective-permute-done), channel_id=1, source_target_pairs={{8,0},{16,8},{24,16},{32,24},{40,32},{48,40},{56,48},{64,56},{72,6... | collective-permute-start | bytes 792584 | tf_op jit(solution)/shard_map/ppermute | solution.py:16
  48.5 8.1 %collective-permute-start.8 = (f32[129,512]{1,0:T(8,128)}, f32[129,512]{1,0:T(8,128)S(1)}, u32[]{:S(2)}, u32[]{:S(2)}) collective-permute-start(f32[129,512]{1,0:T(8,128)} %collective-permute-done.7), channel_id=1, source_target_pairs={{0,8},{8,16},{16,24},{24,32},{32,40},{40,48},{48,56},{56,64},{64,7... | collective-permute-start | bytes 792584 | tf_op jit(solution)/shard_map/ppermute | solution.py:16
  53.9 8.4 %collective-permute-start.2 = (f32[129,512]{1,0:T(8,128)S(1)}, f32[129,512]{1,0:T(8,128)S(1)}, u32[]{:S(2)}, u32[]{:S(2)}) collective-permute-start(f32[129,512]{1,0:T(8,128)S(1)} %pad_maximum_fusion.2), channel_id=1, source_target_pairs={{16,0},{24,8},{32,16},{40,24},{48,32},{56,40},{64,48},{72,56},{80,... | collective-permute-start | bytes 792584 | tf_op jit(solution)/shard_map/ppermute | solution.py:16
  58.3 17.1 %collective-permute-start.9 = (f32[129,512]{1,0:T(8,128)S(1)}, f32[129,512]{1,0:T(8,128)S(1)}, u32[]{:S(2)}, u32[]{:S(2)}) collective-permute-start(f32[129,512]{1,0:T(8,128)S(1)} %pad_maximum_fusion.7), channel_id=1, source_target_pairs={{0,16},{8,24},{16,32},{24,40},{32,48},{40,56},{48,64},{56,72},{64,... | collective-permute-start | bytes 792584 | tf_op jit(solution)/shard_map/ppermute | solution.py:16
  62.5 15.4 %collective-permute-start.3 = (f32[129,512]{1,0:T(8,128)S(1)}, f32[129,512]{1,0:T(8,128)S(1)}, u32[]{:S(2)}, u32[]{:S(2)}) collective-permute-start(f32[129,512]{1,0:T(8,128)S(1)} %pad_maximum_fusion.3), channel_id=1, source_target_pairs={{32,0},{40,8},{48,16},{56,24},{64,32},{72,40},{80,48},{88,56},{96,... | collective-permute-start | bytes 792584 | tf_op jit(solution)/shard_map/ppermute | solution.py:16
  75.5 9.1 %collective-permute-start.10 = (f32[129,512]{1,0:T(8,128)S(1)}, f32[129,512]{1,0:T(8,128)S(1)}, u32[]{:S(2)}, u32[]{:S(2)}) collective-permute-start(f32[129,512]{1,0:T(8,128)S(1)} %pad_maximum_fusion.8), channel_id=1, source_target_pairs={{0,32},{8,40},{16,48},{24,56},{32,64},{40,72},{48,80},{56,88},{64,... | collective-permute-start | bytes 792584 | tf_op jit(solution)/shard_map/ppermute | solution.py:16
  78.0 14.7 %collective-permute-start.4 = (f32[129,512]{1,0:T(8,128)S(1)}, f32[129,512]{1,0:T(8,128)S(1)}, u32[]{:S(2)}, u32[]{:S(2)}) collective-permute-start(f32[129,512]{1,0:T(8,128)S(1)} %pad_maximum_fusion.4), channel_id=1, source_target_pairs={{64,0},{72,8},{80,16},{88,24},{96,32},{104,40},{112,48},{120,56},{... | collective-permute-start | bytes 792584 | tf_op jit(solution)/shard_map/ppermute | solution.py:16
  84.7 13.5 %collective-permute-start.11 = (f32[129,512]{1,0:T(8,128)S(1)}, f32[129,512]{1,0:T(8,128)S(1)}, u32[]{:S(2)}, u32[]{:S(2)}) collective-permute-start(f32[129,512]{1,0:T(8,128)S(1)} %pad_maximum_fusion.9), channel_id=1, source_target_pairs={{0,64},{8,72},{16,80},{24,88},{32,96},{40,104},{48,112},{56,120},{... | collective-permute-start | bytes 792584 | tf_op jit(solution)/shard_map/ppermute | solution.py:16
  92.7 16.6 %collective-permute-start.5 = (f32[129,512]{1,0:T(8,128)S(1)}, f32[129,512]{1,0:T(8,128)S(1)}, u32[]{:S(2)}, u32[]{:S(2)}) collective-permute-start(f32[129,512]{1,0:T(8,128)S(1)} %pad_maximum_fusion.5), channel_id=1, source_target_pairs={{128,0},{136,8},{144,16},{152,24},{160,32},{168,40},{176,48},{184,... | collective-permute-start | bytes 792584 | tf_op jit(solution)/shard_map/ppermute | solution.py:16
  98.3 12.5 %collective-permute-start.12 = (f32[129,512]{1,0:T(8,128)S(1)}, f32[129,512]{1,0:T(8,128)S(1)}, u32[]{:S(2)}, u32[]{:S(2)}) collective-permute-start(f32[129,512]{1,0:T(8,128)S(1)} %pad_maximum_fusion.10), channel_id=1, source_target_pairs={{0,128},{8,136},{16,144},{24,152},{32,160},{40,168},{48,176},{56,1... | collective-permute-start | bytes 792584 | tf_op jit(solution)/shard_map/ppermute | solution.py:16
  109.4 19.8 %collective-permute-start.6 = (f32[129,512]{1,0:T(8,128)S(1)}, f32[129,512]{1,0:T(8,128)S(1)}, u32[]{:S(2)}, u32[]{:S(2)}) collective-permute-start(f32[129,512]{1,0:T(8,128)S(1)} %pad_maximum_fusion.6), channel_id=1, source_target_pairs={{256,0},{264,8},{272,16},{280,24},{288,32},{296,40},{304,48},{312,... | collective-permute-start | bytes 792584 | tf_op jit(solution)/shard_map/ppermute | solution.py:16
  110.8 23.9 %collective-permute-start.13 = (f32[129,512]{1,0:T(8,128)S(1)}, f32[129,512]{1,0:T(8,128)S(1)}, u32[]{:S(2)}, u32[]{:S(2)}) collective-permute-start(f32[129,512]{1,0:T(8,128)S(1)} %pad_maximum_fusion.11), channel_id=1, source_target_pairs={{0,256},{8,264},{16,272},{24,280},{32,288},{40,296},{48,304},{56,3... | collective-permute-start | bytes 792584 | tf_op jit(solution)/shard_map/ppermute | solution.py:16
Sparse Core Ops, SparseCore 0:
  136.9 86.3 all-reduce.2

commit v2 on v1

--- a/solution.py
+++ b/solution.py
@@ -3,9 +3,82 @@
 import jax
 import jax.numpy as jnp
 from jax import lax
+from jax.experimental import pallas as pl
+from jax.experimental.pallas import tpu as pltpu
 from jax.sharding import PartitionSpec as P
 
 PRECISE = lax.Precision.HIGHEST
+MESH = pl.DeviceIdType.MESH
+
+
+def head_sum_kernel(n, x_ref, o_ref, gather1, gather2, send1, recv1, send2, recv2):
+    me = lax.axis_index("head")
+    row = lax.axis_index("seq")
+    rows = gather1.shape[1]
+    barrier = pltpu.get_barrier_semaphore()
+    for k in range(1, n):
+        peer = lax.rem(me + k, n)
+        pl.semaphore_signal(barrier, inc=1, device_id=(row, peer), device_id_type=MESH)
+    pl.semaphore_wait(barrier, n - 1)
+
+    def chunk(i):
+        return x_ref.at[pl.ds(pl.multiple_of(i * rows, rows), rows)]
+
+    sends = []
+    for k in range(1, n):
+        peer = lax.rem(me + k, n)
+        c = pltpu.make_async_remote_copy(
+            src_ref=chunk(peer), dst_ref=gather1.at[me], send_sem=send1.at[k],
+            recv_sem=recv1.at[k], device_id=(row, peer), device_id_type=MESH)
+        c.start()
+        sends.append(c)
+    total = x_ref[pl.ds(pl.multiple_of(me * rows, rows), rows), :].astype(jnp.float32)
+    for k in range(1, n):
+        source = lax.rem(me + n - k, n)
+        pltpu.make_async_remote_copy(
+            src_ref=chunk(source), dst_ref=gather1.at[source], send_sem=send1.at[k],
+            recv_sem=recv1.at[k], device_id=(row, source), device_id_type=MESH).wait_recv()
+        total = total + gather1[source].astype(jnp.float32)
+    for c in sends:
+        c.wait_send()
+    gather2[me] = total.astype(gather2.dtype)
+    sends = []
+    for k in range(1, n):
+        peer = lax.rem(me + k, n)
+        c = pltpu.make_async_remote_copy(
+            src_ref=gather2.at[me], dst_ref=gather2.at[me], send_sem=send2.at[k],
+            recv_sem=recv2.at[k], device_id=(row, peer), device_id_type=MESH)
+        c.start()
+        sends.append(c)
+    for k in range(1, n):
+        source = lax.rem(me + n - k, n)
+        pltpu.make_async_remote_copy(
+            src_ref=gather2.at[source], dst_ref=gather2.at[source], send_sem=send2.at[k],
+            recv_sem=recv2.at[k], device_id=(row, source), device_id_type=MESH).wait_recv()
+    for c in sends:
+        c.wait_send()
+    o_ref[...] = gather2[...]
+
+
+def head_sum(n, parts):
+    rows = parts.shape[0] // n
+    width = parts.shape[1]
+    out = pl.pallas_call(
+        functools.partial(head_sum_kernel, n),
+        out_shape=jax.ShapeDtypeStruct((n, rows, width), parts.dtype),
+        in_specs=[pl.BlockSpec(memory_space=pltpu.VMEM)],
+        out_specs=pl.BlockSpec(memory_space=pltpu.VMEM),
+        scratch_shapes=[
+            pltpu.VMEM((n, rows, width), parts.dtype),
+            pltpu.VMEM((n, rows, width), parts.dtype),
+            pltpu.SemaphoreType.DMA((n,)),
+            pltpu.SemaphoreType.DMA((n,)),
+            pltpu.SemaphoreType.DMA((n,)),
+            pltpu.SemaphoreType.DMA((n,)),
+        ],
+        compiler_params=pltpu.CompilerParams(collective_id=0, has_side_effects=True),
+    )(parts)
+    return out.reshape(n * rows, width)
 
 
 def shift(value, count, distance, reverse):
@@ -30,7 +103,7 @@
     return [w[1:] for w in windows]
 
 
-def shards(count, token_values, b_inputs, c_inputs, log_decay, grad_out):
+def shards(count, groups, token_values, b_inputs, c_inputs, log_decay, grad_out):
     length = token_values.shape[0]
     heads_here = log_decay.shape[0]
     head_dim = token_values.shape[1] // heads_here
@@ -98,15 +171,10 @@
     dc_part = dc_part + jnp.dot(
         grad_out.astype(jnp.float32) * from_start_cols, state_in.T, precision=PRECISE
     )
-    grad_b, grad_c = (
-        lax.psum(db_part.astype(jnp.bfloat16), "head").astype(jnp.float32),
-        lax.psum(dc_part.astype(jnp.bfloat16), "head").astype(jnp.float32),
+    both = head_sum(
+        groups, jnp.concatenate([db_part, dc_part], axis=0).astype(jnp.bfloat16)
     )
-    return (
-        grad_values.astype(jnp.bfloat16),
-        grad_b.astype(jnp.bfloat16),
-        grad_c.astype(jnp.bfloat16),
-    )
+    return grad_values.astype(jnp.bfloat16), both[:length], both[length:]
 
 
 def solution(mesh):
@@ -118,5 +186,5 @@
         P("seq", "head"),
     )
     out_specs = (P("seq", "head"), P("seq", None), P("seq", None))
-    body = functools.partial(shards, mesh.shape["seq"])
+    body = functools.partial(shards, mesh.shape["seq"], mesh.shape["head"])
     return jax.shard_map(body, mesh=mesh, in_specs=in_specs, out_specs=out_specs, check_vma=False)

time: 235 us -> 154 us (0.66)
  the two profiles are of different devices: /device:TPU:2 before, /device:TPU:42 now
where the time goes in v2:
time: 154 us; the launch traced here: 153 us
  starting transfers between devices  53.8 us (35%)
  waiting for transfers between devices  34.6 us (22%)
  Pallas kernels  26.1 us (17%)
  matrix products  21.2 us (14%)
  other arithmetic  8.73 us (6%)
  local copies, waits for them, and re-layouts  7.26 us (5%)
    ppermute x14, starting transfers between devices, shift(): return lax.ppermute(value, 'seq', pairs)  53.8 us
    ppermute x14, waiting for transfers between devices, shift(): return lax.ppermute(value, 'seq', pairs)  34.6 us
    pallas_call x1, Pallas kernels, head_sum(): pl.pallas_call(functools.partial(head_sum_kernel, n), out_shape=jax.Shape...  26.1 us
    dot_general x8, matrix products, head_step(): lax.dot_general(dy_head, x_head, (((1,), (1,)), ((), ())), preferred_elem...  10.8 us
    unnamed x21, local copies, waits for them, and re-layouts  4.59 us
  transfers between devices with their start and end apart: 14, of which 6 were waited for; matrix products, arithmetic and copies ran while one was open for 16% of the time, Pallas kernels for 0%

profile of v2, /device:TPU:42, one launch (start us, length us, event | category | flops | bytes accessed | tf_op | source)
XLA Modules:
  0.0 153.2 jit_solution(11895996676051548306)
XLA Ops:
  0.6 2.0 %reduce-window.6 = f32[8,3,128]{2,0,1:T(8,128)S(1)} reduce-window(f32[8,3,128]{2,0,1:T(8,128)} %bitcast.71, f32[]{:T(128)} %constant.50.clone.1), window={size=1x1x128 pad=0_0x0_0x127_0}, to_apply=%region_0.0 | reduce-window | flops 390144 | bytes 24580 | tf_op jit(solution)/shard_map/reduce-window
  7.8 1.9 %collective-permute-start = (f32[129,512]{1,0:T(8,128)}, f32[129,512]{1,0:T(8,128)}, u32[]{:S(2)}, u32[]{:S(2)}) collective-permute-start(f32[129,512]{1,0:T(8,128)} %get-tuple-element.225), channel_id=1, source_target_pairs={{8,0},{16,8},{24,16},{32,24},{40,32},{48,40},{56,48},{64,56},{72,6... | collective-permute-start | bytes 792584 | tf_op jit(solution)/shard_map/ppermute | solution.py:89
  9.7 2.4 %collective-permute-start.7 = (f32[129,512]{1,0:T(8,128)}, f32[129,512]{1,0:T(8,128)}, u32[]{:S(2)}, u32[]{:S(2)}) collective-permute-start(f32[129,512]{1,0:T(8,128)} %get-tuple-element.224), channel_id=1, source_target_pairs={{0,8},{8,16},{16,24},{24,32},{32,40},{40,48},{48,56},{56,64},{64,7... | collective-permute-start | bytes 792584 | tf_op jit(solution)/shard_map/ppermute | solution.py:89
  12.5 13.9 %while.17 = (s32[]{:T(128)}, f32[384,384]{1,0:T(8,128)S(1)}, f32[384,512]{0,1:T(8,128)S(1)}, f32[8,384]{1,0:T(8,128)S(1)}, bf16[384,512]{1,0:T(8,128)(2,1)S(1)},...) while((s32[]{:T(128)}, f32[384,384]{1,0:T(8,128)S(1)}, ...), condition=%wide.region_3.4_spmd.clone.clone, body=%wide.region_2.3_spmd.clone.clone.sunk | while | flops 39665672 | bytes 2176688 | solution.py:159
  12.5 1.3 fusion.65
  14.2 1.3 fusion.65
  16.0 1.3 fusion.65
  17.7 1.3 fusion.65
  19.5 1.3 fusion.65
  21.2 1.3 fusion.65
  23.0 1.3 fusion.65
  24.7 1.3 fusion.65
  26.4 3.2 %collective-permute-start.1 = (f32[129,512]{1,0:T(8,128)}, f32[129,512]{1,0:T(8,128)S(1)}, u32[]{:S(2)}, u32[]{:S(2)}) collective-permute-start(f32[129,512]{1,0:T(8,128)} %collective-permute-done), channel_id=1, source_target_pairs={{8,0},{16,8},{24,16},{32,24},{40,32},{48,40},{56,48},{64,56},{72,6... | collective-permute-start | bytes 792584 | tf_op jit(solution)/shard_map/ppermute | solution.py:89
  32.5 1.9 %collective-permute-start.8 = (f32[129,512]{1,0:T(8,128)}, f32[129,512]{1,0:T(8,128)S(1)}, u32[]{:S(2)}, u32[]{:S(2)}) collective-permute-start(f32[129,512]{1,0:T(8,128)} %collective-permute-done.7), channel_id=1, source_target_pairs={{0,8},{8,16},{16,24},{24,32},{32,40},{40,48},{48,56},{56,64},{64,7... | collective-permute-start | bytes 792584 | tf_op jit(solution)/shard_map/ppermute | solution.py:89
  36.2 7.5 %collective-permute-start.2 = (f32[129,512]{1,0:T(8,128)S(1)}, f32[129,512]{1,0:T(8,128)S(1)}, u32[]{:S(2)}, u32[]{:S(2)}) collective-permute-start(f32[129,512]{1,0:T(8,128)S(1)} %pad_maximum_fusion.2), channel_id=1, source_target_pairs={{16,0},{24,8},{32,16},{40,24},{48,32},{56,40},{64,48},{72,56},{80,... | collective-permute-start | bytes 792584 | tf_op jit(solution)/shard_map/ppermute | solution.py:89
  45.6 1.9 %collective-permute-start.9 = (f32[129,512]{1,0:T(8,128)S(1)}, f32[129,512]{1,0:T(8,128)S(1)}, u32[]{:S(2)}, u32[]{:S(2)}) collective-permute-start(f32[129,512]{1,0:T(8,128)S(1)} %pad_maximum_fusion.7), channel_id=1, source_target_pairs={{0,16},{8,24},{16,32},{24,40},{32,48},{40,56},{48,64},{56,72},{64,... | collective-permute-start | bytes 792584 | tf_op jit(solution)/shard_map/ppermute | solution.py:89
  47.9 9.1 %collective-permute-start.3 = (f32[129,512]{1,0:T(8,128)S(1)}, f32[129,512]{1,0:T(8,128)S(1)}, u32[]{:S(2)}, u32[]{:S(2)}) collective-permute-start(f32[129,512]{1,0:T(8,128)S(1)} %pad_maximum_fusion.3), channel_id=1, source_target_pairs={{32,0},{40,8},{48,16},{56,24},{64,32},{72,40},{80,48},{88,56},{96,... | collective-permute-start | bytes 792584 | tf_op jit(solution)/shard_map/ppermute | solution.py:89
  57.0 7.2 %collective-permute-done.9 = f32[129,512]{1,0:T(8,128)S(1)} collective-permute-done((f32[129,512]{1,0:T(8,128)S(1)}, f32[129,512]{1,0:T(8,128)S(1)}, u32[]{:S(2)}, u32[]{:S(2)}) %collective-permute-start.9) | collective-permute-done | bytes 264224 | tf_op jit(solution)/shard_map/ppermute | solution.py:89
  64.3 1.9 %collective-permute-start.10 = (f32[129,512]{1,0:T(8,128)S(1)}, f32[129,512]{1,0:T(8,128)S(1)}, u32[]{:S(2)}, u32[]{:S(2)}) collective-permute-start(f32[129,512]{1,0:T(8,128)S(1)} %pad_maximum_fusion.8), channel_id=1, source_target_pairs={{0,32},{8,40},{16,48},{24,56},{32,64},{40,72},{48,80},{56,88},{64,... | collective-permute-start | bytes 792584 | tf_op jit(solution)/shard_map/ppermute | solution.py:89
  66.3 4.8 %collective-permute-start.4 = (f32[129,512]{1,0:T(8,128)S(1)}, f32[129,512]{1,0:T(8,128)S(1)}, u32[]{:S(2)}, u32[]{:S(2)}) collective-permute-start(f32[129,512]{1,0:T(8,128)S(1)} %pad_maximum_fusion.4), channel_id=1, source_target_pairs={{64,0},{72,8},{80,16},{88,24},{96,32},{104,40},{112,48},{120,56},{... | collective-permute-start | bytes 792584 | tf_op jit(solution)/shard_map/ppermute | solution.py:89
  71.1 4.8 %collective-permute-done.10 = f32[129,512]{1,0:T(8,128)S(1)} collective-permute-done((f32[129,512]{1,0:T(8,128)S(1)}, f32[129,512]{1,0:T(8,128)S(1)}, u32[]{:S(2)}, u32[]{:S(2)}) %collective-permute-start.10) | collective-permute-done | bytes 264224 | tf_op jit(solution)/shard_map/ppermute | solution.py:89
  76.1 2.6 %collective-permute-start.11 = (f32[129,512]{1,0:T(8,128)S(1)}, f32[129,512]{1,0:T(8,128)S(1)}, u32[]{:S(2)}, u32[]{:S(2)}) collective-permute-start(f32[129,512]{1,0:T(8,128)S(1)} %pad_maximum_fusion.9), channel_id=1, source_target_pairs={{0,64},{8,72},{16,80},{24,88},{32,96},{40,104},{48,112},{56,120},{... | collective-permute-start | bytes 792584 | tf_op jit(solution)/shard_map/ppermute | solution.py:89
  78.8 8.0 %collective-permute-start.5 = (f32[129,512]{1,0:T(8,128)S(1)}, f32[129,512]{1,0:T(8,128)S(1)}, u32[]{:S(2)}, u32[]{:S(2)}) collective-permute-start(f32[129,512]{1,0:T(8,128)S(1)} %pad_maximum_fusion.5), channel_id=1, source_target_pairs={{128,0},{136,8},{144,16},{152,24},{160,32},{168,40},{176,48},{184,... | collective-permute-start | bytes 792584 | tf_op jit(solution)/shard_map/ppermute | solution.py:89
  86.9 1.9 %collective-permute-start.12 = (f32[129,512]{1,0:T(8,128)S(1)}, f32[129,512]{1,0:T(8,128)S(1)}, u32[]{:S(2)}, u32[]{:S(2)}) collective-permute-start(f32[129,512]{1,0:T(8,128)S(1)} %pad_maximum_fusion.10), channel_id=1, source_target_pairs={{0,128},{8,136},{16,144},{24,152},{32,160},{40,168},{48,176},{56,1... | collective-permute-start | bytes 792584 | tf_op jit(solution)/shard_map/ppermute | solution.py:89
  88.8 7.3 %collective-permute-done.5 = f32[129,512]{1,0:T(8,128)S(1)} collective-permute-done((f32[129,512]{1,0:T(8,128)S(1)}, f32[129,512]{1,0:T(8,128)S(1)}, u32[]{:S(2)}, u32[]{:S(2)}) %collective-permute-start.5) | collective-permute-done | bytes 264224 | tf_op jit(solution)/shard_map/ppermute | solution.py:89
  96.2 5.4 %collective-permute-start.6 = (f32[129,512]{1,0:T(8,128)S(1)}, f32[129,512]{1,0:T(8,128)S(1)}, u32[]{:S(2)}, u32[]{:S(2)}) collective-permute-start(f32[129,512]{1,0:T(8,128)S(1)} %pad_maximum_fusion.6), channel_id=1, source_target_pairs={{256,0},{264,8},{272,16},{280,24},{288,32},{296,40},{304,48},{312,... | collective-permute-start | bytes 792584 | tf_op jit(solution)/shard_map/ppermute | solution.py:89
  103.6 9.6 %collective-permute-done.6 = f32[129,512]{1,0:T(8,128)S(1)} collective-permute-done((f32[129,512]{1,0:T(8,128)S(1)}, f32[129,512]{1,0:T(8,128)S(1)}, u32[]{:S(2)}, u32[]{:S(2)}) %collective-permute-start.6) | collective-permute-done | bytes 264224 | tf_op jit(solution)/shard_map/ppermute | solution.py:89
  115.6 1.4 fusion.18
  117.0 5.4 %collective-permute-done.13 = f32[129,512]{1,0:T(8,128)} collective-permute-done((f32[129,512]{1,0:T(8,128)}, f32[129,512]{1,0:T(8,128)}, u32[]{:S(2)}, u32[]{:S(2)}) %collective-permute-start.13) | collective-permute-done | bytes 264224 | tf_op jit(solution)/shard_map/ppermute | solution.py:89
  122.4 2.4 %fusion.19 = bf16[384,128]{1,0:T(8,128)(2,1)S(1)} fusion(f32[384,128]{1,0:T(8,128)S(1)} %copy-done.6, f32[384,512]{0,1:T(8,128)S(1)} %bitcast_multiply_fusion.1, f32[128,512]{1,0:T(8,128)S(1)} %fusion.28, f32[129,512]{1,0:T(8,128)} %collective-permute-done.13, f32[512]{0:T(512)S(1)} %bitcast.70), kind=kOutput, calls=%fused_computation.29 | convolution fusion | flops 302219264 | bytes 1607680 | tf_op jit(solution)/shard_map/dot_general | solution.py:171
  125.4 26.1 %shard_map.76 = bf16[8,96,128]{2,1,0:T(8,128)(2,1)} custom-call(bf16[768,128]{1,0:T(8,128)(2,1)} %pad_maximum_fusion.12.x_ref), custom_call_target="tpu_custom_call" | custom-call | tf_op jit(solution)/shard_map/pallas_call | solution.py:66
  151.5 1.6 %fusion.46 = (bf16[4,96,128]{2,1,0:T(8,128)(2,1)}, bf16[4,96,128]{2,1,0:T(8,128)(2,1)}) fusion(bf16[8,96,128]{2,1,0:T(8,128)(2,1)} %shard_map.76), kind=kLoop, calls=%fused_computation.94 | loop fusion | bytes 393216 | tf_op jit(solution)/shard_map/slice | solution.py:177
  (102 shorter events, 20.7 us)
Async XLA Ops:
  0.6 3.9 %copy-start = (bf16[384,128]{1,0:T(8,128)(2,1)S(1)}, bf16[384,128]{1,0:T(8,128)(2,1)}, u32[]{:S(2)}) copy-start(bf16[384,128]{1,0:T(8,128)(2,1)} %param.8) | copy-start | bytes 294916
  4.5 0.8 copy-start.1
  4.6 1.1 copy-start.8
  5.2 0.9 copy-start.5
  7.8 18.6 %collective-permute-start = (f32[129,512]{1,0:T(8,128)}, f32[129,512]{1,0:T(8,128)}, u32[]{:S(2)}, u32[]{:S(2)}) collective-permute-start(f32[129,512]{1,0:T(8,128)} %get-tuple-element.225), channel_id=1, source_target_pairs={{8,0},{16,8},{24,16},{32,24},{40,32},{48,40},{56,48},{64,56},{72,6... | collective-permute-start | bytes 792584 | tf_op jit(solution)/shard_map/ppermute | solution.py:89
  9.7 22.8 %collective-permute-start.7 = (f32[129,512]{1,0:T(8,128)}, f32[129,512]{1,0:T(8,128)}, u32[]{:S(2)}, u32[]{:S(2)}) collective-permute-start(f32[129,512]{1,0:T(8,128)} %get-tuple-element.224), channel_id=1, source_target_pairs={{0,8},{8,16},{16,24},{24,32},{32,40},{40,48},{48,56},{56,64},{64,7... | collective-permute-start | bytes 792584 | tf_op jit(solution)/shard_map/ppermute | solution.py:89
  26.4 8.0 %collective-permute-start.1 = (f32[129,512]{1,0:T(8,128)}, f32[129,512]{1,0:T(8,128)S(1)}, u32[]{:S(2)}, u32[]{:S(2)}) collective-permute-start(f32[129,512]{1,0:T(8,128)} %collective-permute-done), channel_id=1, source_target_pairs={{8,0},{16,8},{24,16},{32,24},{40,32},{48,40},{56,48},{64,56},{72,6... | collective-permute-start | bytes 792584 | tf_op jit(solution)/shard_map/ppermute | solution.py:89
  30.5 1.0 copy-start.2
  32.5 11.2 %collective-permute-start.8 = (f32[129,512]{1,0:T(8,128)}, f32[129,512]{1,0:T(8,128)S(1)}, u32[]{:S(2)}, u32[]{:S(2)}) collective-permute-start(f32[129,512]{1,0:T(8,128)} %collective-permute-done.7), channel_id=1, source_target_pairs={{0,8},{8,16},{16,24},{24,32},{32,40},{40,48},{48,56},{56,64},{64,7... | collective-permute-start | bytes 792584 | tf_op jit(solution)/shard_map/ppermute | solution.py:89
  36.2 11.6 %collective-permute-start.2 = (f32[129,512]{1,0:T(8,128)S(1)}, f32[129,512]{1,0:T(8,128)S(1)}, u32[]{:S(2)}, u32[]{:S(2)}) collective-permute-start(f32[129,512]{1,0:T(8,128)S(1)} %pad_maximum_fusion.2), channel_id=1, source_target_pairs={{16,0},{24,8},{32,16},{40,24},{48,32},{56,40},{64,48},{72,56},{80,... | collective-permute-start | bytes 792584 | tf_op jit(solution)/shard_map/ppermute | solution.py:89
  45.6 18.6 %collective-permute-start.9 = (f32[129,512]{1,0:T(8,128)S(1)}, f32[129,512]{1,0:T(8,128)S(1)}, u32[]{:S(2)}, u32[]{:S(2)}) collective-permute-start(f32[129,512]{1,0:T(8,128)S(1)} %pad_maximum_fusion.7), channel_id=1, source_target_pairs={{0,16},{8,24},{16,32},{24,40},{32,48},{40,56},{48,64},{56,72},{64,... | collective-permute-start | bytes 792584 | tf_op jit(solution)/shard_map/ppermute | solution.py:89
  47.9 18.3 %collective-permute-start.3 = (f32[129,512]{1,0:T(8,128)S(1)}, f32[129,512]{1,0:T(8,128)S(1)}, u32[]{:S(2)}, u32[]{:S(2)}) collective-permute-start(f32[129,512]{1,0:T(8,128)S(1)} %pad_maximum_fusion.3), channel_id=1, source_target_pairs={{32,0},{40,8},{48,16},{56,24},{64,32},{72,40},{80,48},{88,56},{96,... | collective-permute-start | bytes 792584 | tf_op jit(solution)/shard_map/ppermute | solution.py:89
  64.3 11.7 %collective-permute-start.10 = (f32[129,512]{1,0:T(8,128)S(1)}, f32[129,512]{1,0:T(8,128)S(1)}, u32[]{:S(2)}, u32[]{:S(2)}) collective-permute-start(f32[129,512]{1,0:T(8,128)S(1)} %pad_maximum_fusion.8), channel_id=1, source_target_pairs={{0,32},{8,40},{16,48},{24,56},{32,64},{40,72},{48,80},{56,88},{64,... | collective-permute-start | bytes 792584 | tf_op jit(solution)/shard_map/ppermute | solution.py:89
  66.3 12.3 %collective-permute-start.4 = (f32[129,512]{1,0:T(8,128)S(1)}, f32[129,512]{1,0:T(8,128)S(1)}, u32[]{:S(2)}, u32[]{:S(2)}) collective-permute-start(f32[129,512]{1,0:T(8,128)S(1)} %pad_maximum_fusion.4), channel_id=1, source_target_pairs={{64,0},{72,8},{80,16},{88,24},{96,32},{104,40},{112,48},{120,56},{... | collective-permute-start | bytes 792584 | tf_op jit(solution)/shard_map/ppermute | solution.py:89
  76.1 10.7 %collective-permute-start.11 = (f32[129,512]{1,0:T(8,128)S(1)}, f32[129,512]{1,0:T(8,128)S(1)}, u32[]{:S(2)}, u32[]{:S(2)}) collective-permute-start(f32[129,512]{1,0:T(8,128)S(1)} %pad_maximum_fusion.9), channel_id=1, source_target_pairs={{0,64},{8,72},{16,80},{24,88},{32,96},{40,104},{48,112},{56,120},{... | collective-permute-start | bytes 792584 | tf_op jit(solution)/shard_map/ppermute | solution.py:89
  78.8 17.3 %collective-permute-start.5 = (f32[129,512]{1,0:T(8,128)S(1)}, f32[129,512]{1,0:T(8,128)S(1)}, u32[]{:S(2)}, u32[]{:S(2)}) collective-permute-start(f32[129,512]{1,0:T(8,128)S(1)} %pad_maximum_fusion.5), channel_id=1, source_target_pairs={{128,0},{136,8},{144,16},{152,24},{160,32},{168,40},{176,48},{184,... | collective-permute-start | bytes 792584 | tf_op jit(solution)/shard_map/ppermute | solution.py:89
  86.9 14.7 %collective-permute-start.12 = (f32[129,512]{1,0:T(8,128)S(1)}, f32[129,512]{1,0:T(8,128)S(1)}, u32[]{:S(2)}, u32[]{:S(2)}) collective-permute-start(f32[129,512]{1,0:T(8,128)S(1)} %pad_maximum_fusion.10), channel_id=1, source_target_pairs={{0,128},{8,136},{16,144},{24,152},{32,160},{40,168},{48,176},{56,1... | collective-permute-start | bytes 792584 | tf_op jit(solution)/shard_map/ppermute | solution.py:89
  96.2 17.1 %collective-permute-start.6 = (f32[129,512]{1,0:T(8,128)S(1)}, f32[129,512]{1,0:T(8,128)S(1)}, u32[]{:S(2)}, u32[]{:S(2)}) collective-permute-start(f32[129,512]{1,0:T(8,128)S(1)} %pad_maximum_fusion.6), channel_id=1, source_target_pairs={{256,0},{264,8},{272,16},{280,24},{288,32},{296,40},{304,48},{312,... | collective-permute-start | bytes 792584 | tf_op jit(solution)/shard_map/ppermute | solution.py:89
  102.3 20.0 %collective-permute-start.13 = (f32[129,512]{1,0:T(8,128)}, f32[129,512]{1,0:T(8,128)}, u32[]{:S(2)}, u32[]{:S(2)}) collective-permute-start(f32[129,512]{1,0:T(8,128)} %pad_maximum_fusion.11), channel_id=1, source_target_pairs={{0,256},{8,264},{16,272},{24,280},{32,288},{40,296},{48,304},{56,3... | collective-permute-start | bytes 792584 | tf_op jit(solution)/shard_map/ppermute | solution.py:89
  113.2 0.7 copy-start.3
  114.6 1.0 copy-start.4
  114.6 1.0 copy-start.7
  115.6 6.8 %copy-start.6 = (f32[384,128]{1,0:T(8,128)S(1)}, f32[384,128]{1,0:T(8,128)}, u32[]{:S(2)}) copy-start(f32[384,128]{1,0:T(8,128)} %fusion.39) | copy-start | bytes 589828

commit v3 on v2

--- a/solution.py
+++ b/solution.py
@@ -81,26 +81,100 @@
     return out.reshape(n * rows, width)
 
 
-def shift(value, count, distance, reverse):
-    if reverse:
-        pairs = [(p, p - distance) for p in range(distance, count)]
-    else:
-        pairs = [(p, p + distance) for p in range(count - distance)]
-    return lax.ppermute(value, "seq", pairs)
-
-
-def exclusive_scans(count, decay_cols, parts):
-    packed = [jnp.concatenate([decay_cols, s], axis=0) for s, _ in parts]
-    windows = [shift(pk, count, 1, rev) for pk, (_, rev) in zip(packed, parts)]
-    distance = 1
-    while distance < count:
-        received = [shift(w, count, distance, rev) for w, (_, rev) in zip(windows, parts)]
-        windows = [
-            jnp.concatenate([w[:1] * r[:1], w[1:] + w[:1] * r[1:]], axis=0)
-            for w, r in zip(windows, received)
-        ]
-        distance *= 2
-    return [w[1:] for w in windows]
+def scan_steps(n):
+    steps, d = [1], 1
+    while d < n:
+        steps.append(d)
+        d *= 2
+    return steps
+
+
+def scan_kernel(n, x_ref, y_ref, xo_ref, yo_ref, recv, win, send_sem, recv_sem):
+    me = lax.axis_index("seq")
+    col = lax.axis_index("head")
+    s = xo_ref.shape[0]
+    steps = scan_steps(n)
+    spans = sorted(set(steps))
+    barrier = pltpu.get_barrier_semaphore()
+    for d in spans:
+        @pl.when(me + d < n)
+        def _():
+            pl.semaphore_signal(barrier, inc=1, device_id=(me + d, col), device_id_type=MESH)
+
+        @pl.when(me - d >= 0)
+        def _():
+            pl.semaphore_signal(barrier, inc=1, device_id=(me - d, col), device_id_type=MESH)
+    peers = 0
+    for d in spans:
+        peers = peers + ((n - 1 - me) // d + n - 1) // n + (me // d + n - 1) // n
+    pl.semaphore_wait(barrier, peers)
+
+    def copy(way, r, src, target):
+        return pltpu.make_async_remote_copy(
+            src_ref=src, dst_ref=recv.at[way, r], send_sem=send_sem.at[way, r],
+            recv_sem=recv_sem.at[way, r], device_id=(target, col), device_id_type=MESH)
+
+    for r, d in enumerate(steps):
+        for way, sign in ((0, 1), (1, -1)):
+            src = (x_ref if way == 0 else y_ref) if r == 0 else win.at[way, r]
+            target = me + sign * d
+
+            @pl.when(jnp.logical_and(target >= 0, target < n))
+            def _():
+                copy(way, r, src, target).start()
+        for way, sign in ((0, 1), (1, -1)):
+            source = me - sign * d
+            got = jnp.logical_and(source >= 0, source < n)
+
+            @pl.when(got)
+            def _():
+                copy(way, r, win.at[way, r], source).wait_recv()
+                if r == 0:
+                    win[way, 1] = recv[way, 0]
+                else:
+                    a = win[way, r, s:, :]
+                    win[way, r + 1, :s, :] = win[way, r, :s, :] + jnp.broadcast_to(
+                        a[:1], (s, a.shape[1])) * recv[way, r, :s, :]
+                    win[way, r + 1, s:, :] = a * recv[way, r, s:, :]
+
+            @pl.when(jnp.logical_not(got))
+            def _():
+                if r == 0:
+                    win[way, 1] = jnp.zeros(win.shape[2:], win.dtype)
+                else:
+                    win[way, r + 1] = win[way, r]
+    for r, d in enumerate(steps):
+        for way, sign in ((0, 1), (1, -1)):
+            target = me + sign * d
+            src = (x_ref if way == 0 else y_ref) if r == 0 else win.at[way, r]
+
+            @pl.when(jnp.logical_and(target >= 0, target < n))
+            def _():
+                copy(way, r, src, target).wait_send()
+    last = len(steps)
+    xo_ref[...] = win[0, last, :s, :]
+    yo_ref[...] = win[1, last, :s, :]
+
+
+def exclusive_scans(count, decay_cols, forward, backward):
+    s, w = forward.shape
+    rounds = len(scan_steps(count))
+    decay_rows = jnp.broadcast_to(decay_cols, (8, w))
+    x = jnp.concatenate([forward, decay_rows], axis=0)
+    y = jnp.concatenate([backward, decay_rows], axis=0)
+    return pl.pallas_call(
+        functools.partial(scan_kernel, count),
+        out_shape=(jax.ShapeDtypeStruct((s, w), jnp.float32),) * 2,
+        in_specs=[pl.BlockSpec(memory_space=pltpu.VMEM)] * 2,
+        out_specs=(pl.BlockSpec(memory_space=pltpu.VMEM),) * 2,
+        scratch_shapes=[
+            pltpu.VMEM((2, rounds, s + 8, w), jnp.float32),
+            pltpu.VMEM((2, rounds + 1, s + 8, w), jnp.float32),
+            pltpu.SemaphoreType.DMA((2, rounds)),
+            pltpu.SemaphoreType.DMA((2, rounds)),
+        ],
+        compiler_params=pltpu.CompilerParams(collective_id=1, has_side_effects=True),
+    )(x, y)
 
 
 def shards(count, groups, token_values, b_inputs, c_inputs, log_decay, grad_out):
@@ -126,9 +200,7 @@
         "hsn,shp->nhp", decayed_c, dy_heads, preferred_element_type=jnp.float32
     ).reshape(state_size, heads_here * head_dim)
     decay_cols = jnp.repeat(block_decay, head_dim)[None, :]
-    state_in, adjoint_out = exclusive_scans(
-        count, decay_cols, [(state_local, False), (adjoint_local, True)]
-    )
+    state_in, adjoint_out = exclusive_scans(count, decay_cols, state_local, adjoint_local)
     scores = lax.dot_general(
         c_inputs, b_inputs, (((1,), (1,)), ((), ())), preferred_element_type=jnp.float32
     )

time: 154 us -> 145 us (0.942)
  the two profiles are of different devices: /device:TPU:42 before, /device:TPU:62 now
where the time goes in v3:
time: 145 us; the launch traced here: 144 us
  Pallas kernels  107 us (74%)
  matrix products  21.5 us (15%)
  local copies, waits for them, and re-layouts  8.92 us (6%)
  other arithmetic  5.34 us (4%)
    pallas_call x1, Pallas kernels, exclusive_scans(): pl.pallas_call(functools.partial(scan_kernel, count), out_shape=(jax.Shap...  84.7 us
    pallas_call x1, Pallas kernels, head_sum(): pl.pallas_call(functools.partial(head_sum_kernel, n), out_shape=jax.Shape...  22.4 us
    dot_general x8, matrix products, head_step(): lax.dot_general(dy_head, x_head, (((1,), (1,)), ((), ())), preferred_elem...  10.8 us
    unnamed x15, local copies, waits for them, and re-layouts  4.59 us

profile of v3, /device:TPU:62, one launch (start us, length us, event | category | flops | bytes accessed | tf_op | source)
XLA Modules:
  0.0 144.0 jit_solution(9633781532780033869)
XLA Ops:
  0.6 1.9 %reduce-window.6 = f32[8,3,128]{2,0,1:T(8,128)S(1)} reduce-window(f32[8,3,128]{2,0,1:T(8,128)} %bitcast.51, f32[]{:T(128)} %constant.50.clone.1), window={size=1x1x128 pad=0_0x0_0x127_0}, to_apply=%region_0.0 | reduce-window | flops 390144 | bytes 24580 | tf_op jit(solution)/shard_map/reduce-window
  2.8 0.7 exponential_bitcast_fusion
  3.5 1.2 fusion.30
  4.8 13.9 %while.17 = (s32[]{:T(128)}, f32[384,384]{1,0:T(8,128)S(1)}, f32[384,512]{0,1:T(8,128)S(1)}, f32[8,384]{1,0:T(8,128)S(1)}, bf16[384,512]{1,0:T(8,128)(2,1)S(1)},...) while((s32[]{:T(128)}, f32[384,384]{1,0:T(8,128)S(1)}, ...), condition=%wide.region_3.4_spmd.clone.clone, body=%wide.region_2.3_spmd.clone.clone.sunk | while | flops 39665672 | bytes 2176688 | solution.py:231
  4.8 1.3 fusion.52
  6.6 1.3 fusion.52
  8.3 1.3 fusion.52
  10.0 1.3 fusion.52
  11.8 1.3 fusion.52
  13.1 0.3 convolution_dynamic-update-slice_fusion.2
  13.5 1.3 fusion.52
  14.9 0.3 convolution_dynamic-update-slice_fusion.2
  15.3 1.3 fusion.52
  16.6 0.3 convolution_dynamic-update-slice_fusion.2
  17.0 1.3 fusion.52
  18.4 0.3 convolution_dynamic-update-slice_fusion.2
  19.4 0.5 copy-done.2
  19.9 0.6 fusion.21
  20.7 1.2 copy.15
  21.9 1.3 fusion.20
  23.2 1.8 %copy.16 = f32[128,512]{1,0:T(8,128)} copy(f32[128,512]{0,1:T(8,128)} %bitcast.46) | data formatting | bytes 524288 | tf_op jit(solution)/shard_map/reshape | solution.py:198
  25.0 1.8 %pad_maximum_fusion = (f32[136,512]{1,0:T(8,128)}, f32[136,512]{1,0:T(8,128)}) fusion(f32[8,512]{1,0:T(8,128)S(1)} %broadcast_in_dim.46, f32[128,512]{1,0:T(8,128)S(1)} %copy.18, f32[128,512]{1,0:T(8,128)} %copy.16), kind=kLoop, calls=%fused_computation.37 | loop fusion | flops 139264 | bytes 1097728 | tf_op jit(solution)/shard_map/concatenate | solution.py:164
  26.8 84.7 %shard_map.76 = (f32[128,512]{1,0:T(8,128)}, f32[128,512]{1,0:T(8,128)}) custom-call(f32[136,512]{1,0:T(8,128)} %get-tuple-element.223.x_ref, f32[136,512]{1,0:T(8,128)} %get-tuple-element.222.y_ref), custom_call_target="tpu_custom_call" | custom-call | tf_op jit(solution)/shard_map/pallas_call | solution.py:165
  111.5 1.6 %fusion.17 = bf16[384,512]{0,1:T(8,128)(2,1)S(1)} fusion(f32[384,512]{0,1:T(8,128)S(1)} %get-tuple-element.148, f32[384,512]{0,1:T(8,128)S(1)} %bitcast.42, f32[128,512]{1,0:T(8,128)} %get-tuple-element.149, bf16[384,128]{1,0:T(8,128)(2,1)S(1)} %copy-done), kind=kOutput, calls=%fused_computation.24 | convolution fusion | flops 302579712 | bytes 2326528 | tf_op jit(solution)/shard_map/dot_general | solution.py:239
  113.1 0.9 copy.21
  114.1 0.9 copy-done.4
  115.0 1.4 fusion.32
  116.7 0.9 copy-done.1
  117.6 1.4 fusion.31
  119.3 0.7 pad_maximum_fusion.2.x_ref
  120.0 22.4 %shard_map.77 = bf16[8,96,128]{2,1,0:T(8,128)(2,1)} custom-call(bf16[768,128]{1,0:T(8,128)(2,1)} %pad_maximum_fusion.2.x_ref), custom_call_target="tpu_custom_call" | custom-call | tf_op jit(solution)/shard_map/pallas_call | solution.py:66
  142.4 1.6 %fusion.28 = (bf16[4,96,128]{2,1,0:T(8,128)(2,1)}, bf16[4,96,128]{2,1,0:T(8,128)(2,1)}) fusion(bf16[8,96,128]{2,1,0:T(8,128)(2,1)} %shard_map.77), kind=kLoop, calls=%fused_computation.47 | loop fusion | bytes 393216 | tf_op jit(solution)/shard_map/slice | solution.py:249
  (40 shorter events, 3.3 us)
Async XLA Ops:
  3.5 1.3 copy-start.3
  19.0 0.9 copy-start.2
  20.5 1.4 copy-start
  113.1 1.0 copy-start.5
  114.1 0.9 copy-start.4
  116.7 1.0 copy-start.1

commit v4 on v3

--- a/solution.py
+++ b/solution.py
@@ -89,92 +89,185 @@
     return steps
 
 
-def scan_kernel(n, x_ref, y_ref, xo_ref, yo_ref, recv, win, send_sem, recv_sem):
+def scan_kernel(rows_n, width, pack_ref, o_ref, recv1, win, out3, recv3, send1, rsem1,
+                send2, rsem2, send3, rsem3, local):
     me = lax.axis_index("seq")
     col = lax.axis_index("head")
-    s = xo_ref.shape[0]
-    steps = scan_steps(n)
+    c = me % width
+    y = me // width
+    piece = (recv1.shape[1] - 8) // 2
+    steps = scan_steps(rows_n)
     spans = sorted(set(steps))
+
     barrier = pltpu.get_barrier_semaphore()
+    for off in range(1, width):
+        peer = y * width + (c + off) % width
+        pl.semaphore_signal(barrier, inc=1, device_id=(peer, col), device_id_type=MESH)
     for d in spans:
-        @pl.when(me + d < n)
+        @pl.when(y + d < rows_n)
         def _():
-            pl.semaphore_signal(barrier, inc=1, device_id=(me + d, col), device_id_type=MESH)
-
-        @pl.when(me - d >= 0)
+            pl.semaphore_signal(barrier, inc=1, device_id=(me + d * width, col), device_id_type=MESH)
+
+        @pl.when(y - d >= 0)
         def _():
-            pl.semaphore_signal(barrier, inc=1, device_id=(me - d, col), device_id_type=MESH)
-    peers = 0
+            pl.semaphore_signal(barrier, inc=1, device_id=(me - d * width, col), device_id_type=MESH)
+    peers = width - 1
     for d in spans:
-        peers = peers + ((n - 1 - me) // d + n - 1) // n + (me // d + n - 1) // n
+        peers = peers + ((rows_n - 1 - y) // d + rows_n - 1) // rows_n + (y // d + rows_n - 1) // rows_n
     pl.semaphore_wait(barrier, peers)
 
-    def copy(way, r, src, target):
+    own = pltpu.make_async_copy(pack_ref.at[c], recv1.at[c], local.at[0])
+    own.start()
+    sends = []
+    for off in range(1, width):
+        k = (c + off) % width
+        cp = pltpu.make_async_remote_copy(
+            src_ref=pack_ref.at[k], dst_ref=recv1.at[c], send_sem=send1.at[off],
+            recv_sem=rsem1.at[off], device_id=(y * width + k, col), device_id_type=MESH)
+        cp.start()
+        sends.append(cp)
+    for off in range(1, width):
+        k = (c + width - off) % width
+        pltpu.make_async_remote_copy(
+            src_ref=pack_ref.at[k], dst_ref=recv1.at[k], send_sem=send1.at[off],
+            recv_sem=rsem1.at[off], device_id=(y * width + k, col), device_id_type=MESH).wait_recv()
+    own.wait()
+    for cp in sends:
+        cp.wait_send()
+
+    def decay(i):
+        return recv1[i, 2 * piece:2 * piece + 1, :]
+
+    fwd_e, fwd_g = [None] * width, [None] * width
+    e = jnp.zeros((piece, recv1.shape[2]), jnp.float32)
+    g = jnp.ones((1, recv1.shape[2]), jnp.float32)
+    for i in range(width):
+        fwd_e[i], fwd_g[i] = e, g
+        a = decay(i)
+        e = a * e + recv1[i, :piece, :]
+        g = g * a
+    bwd_e, bwd_g = [None] * width, [None] * width
+    f = jnp.zeros((piece, recv1.shape[2]), jnp.float32)
+    h = jnp.ones((1, recv1.shape[2]), jnp.float32)
+    for i in reversed(range(width)):
+        bwd_e[i], bwd_g[i] = f, h
+        a = decay(i)
+        f = a * f + recv1[i, piece:2 * piece, :]
+        h = h * a
+    win[0, 0, :piece, :] = e
+    win[0, 0, piece:, :] = jnp.broadcast_to(g, (win.shape[2] - piece, g.shape[1]))
+    win[1, 0, :piece, :] = f
+    win[1, 0, piece:, :] = jnp.broadcast_to(h, (win.shape[2] - piece, h.shape[1]))
+
+    def copy2(way, r, target):
+        src = win.at[way, 0] if r == 0 else win.at[way, r]
         return pltpu.make_async_remote_copy(
-            src_ref=src, dst_ref=recv.at[way, r], send_sem=send_sem.at[way, r],
-            recv_sem=recv_sem.at[way, r], device_id=(target, col), device_id_type=MESH)
-
+            src_ref=src, dst_ref=win.at[way, len(steps) + 1 + r],
+            send_sem=send2.at[way, r], recv_sem=rsem2.at[way, r],
+            device_id=(target, col), device_id_type=MESH)
+
+    base = len(steps) + 1
     for r, d in enumerate(steps):
         for way, sign in ((0, 1), (1, -1)):
-            src = (x_ref if way == 0 else y_ref) if r == 0 else win.at[way, r]
-            target = me + sign * d
-
-            @pl.when(jnp.logical_and(target >= 0, target < n))
+            target_row = y + sign * d
+
+            @pl.when(jnp.logical_and(target_row >= 0, target_row < rows_n))
             def _():
-                copy(way, r, src, target).start()
+                copy2(way, r, me + sign * d * width).start()
         for way, sign in ((0, 1), (1, -1)):
-            source = me - sign * d
-            got = jnp.logical_and(source >= 0, source < n)
+            source_row = y - sign * d
+            got = jnp.logical_and(source_row >= 0, source_row < rows_n)
+            cur = 0 if r == 0 else r
+            nxt = r + 1
 
             @pl.when(got)
             def _():
-                copy(way, r, win.at[way, r], source).wait_recv()
+                copy2(way, r, me - sign * d * width).wait_recv()
+                arrived = win[way, base + r]
                 if r == 0:
-                    win[way, 1] = recv[way, 0]
+                    win[way, nxt] = arrived
                 else:
-                    a = win[way, r, s:, :]
-                    win[way, r + 1, :s, :] = win[way, r, :s, :] + jnp.broadcast_to(
-                        a[:1], (s, a.shape[1])) * recv[way, r, :s, :]
-                    win[way, r + 1, s:, :] = a * recv[way, r, s:, :]
+                    a = win[way, cur, piece:, :]
+                    win[way, nxt, :piece, :] = win[way, cur, :piece, :] + jnp.broadcast_to(
+                        a[:1], (piece, a.shape[1])) * arrived[:piece]
+                    win[way, nxt, piece:, :] = a * arrived[piece:]
 
             @pl.when(jnp.logical_not(got))
             def _():
                 if r == 0:
-                    win[way, 1] = jnp.zeros(win.shape[2:], win.dtype)
+                    win[way, nxt] = jnp.zeros(win.shape[2:], win.dtype)
                 else:
-                    win[way, r + 1] = win[way, r]
+                    win[way, nxt] = win[way, cur]
     for r, d in enumerate(steps):
         for way, sign in ((0, 1), (1, -1)):
-            target = me + sign * d
-            src = (x_ref if way == 0 else y_ref) if r == 0 else win.at[way, r]
-
-            @pl.when(jnp.logical_and(target >= 0, target < n))
+            target_row = y + sign * d
+
+            @pl.when(jnp.logical_and(target_row >= 0, target_row < rows_n))
             def _():
-                copy(way, r, src, target).wait_send()
+                copy2(way, r, me + sign * d * width).wait_send()
     last = len(steps)
-    xo_ref[...] = win[0, last, :s, :]
-    yo_ref[...] = win[1, last, :s, :]
+    entering = win[0, last, :piece, :]
+    leaving = win[1, last, :piece, :]
+
+    for i in range(width):
+        out3[i, :piece, :] = fwd_e[i] + fwd_g[i] * entering
+        out3[i, piece:, :] = bwd_e[i] + bwd_g[i] * leaving
+    own = pltpu.make_async_copy(out3.at[c], recv3.at[c], local.at[1])
+    own.start()
+    sends = []
+    for off in range(1, width):
+        k = (c + off) % width
+        cp = pltpu.make_async_remote_copy(
+            src_ref=out3.at[k], dst_ref=recv3.at[c], send_sem=send3.at[off],
+            recv_sem=rsem3.at[off], device_id=(y * width + k, col), device_id_type=MESH)
+        cp.start()
+        sends.append(cp)
+    for off in range(1, width):
+        k = (c + width - off) % width
+        pltpu.make_async_remote_copy(
+            src_ref=out3.at[k], dst_ref=recv3.at[k], send_sem=send3.at[off],
+            recv_sem=rsem3.at[off], device_id=(y * width + k, col), device_id_type=MESH).wait_recv()
+    own.wait()
+    for cp in sends:
+        cp.wait_send()
+    o_ref[...] = recv3[...]
 
 
 def exclusive_scans(count, decay_cols, forward, backward):
     s, w = forward.shape
-    rounds = len(scan_steps(count))
-    decay_rows = jnp.broadcast_to(decay_cols, (8, w))
-    x = jnp.concatenate([forward, decay_rows], axis=0)
-    y = jnp.concatenate([backward, decay_rows], axis=0)
-    return pl.pallas_call(
-        functools.partial(scan_kernel, count),
-        out_shape=(jax.ShapeDtypeStruct((s, w), jnp.float32),) * 2,
-        in_specs=[pl.BlockSpec(memory_space=pltpu.VMEM)] * 2,
-        out_specs=(pl.BlockSpec(memory_space=pltpu.VMEM),) * 2,
+    width = 8 if count % 8 == 0 else 1
+    rows_n = count // width
+    piece = s // width
+    rounds = len(scan_steps(rows_n))
+    pack = jnp.concatenate(
+        [
+            forward.reshape(width, piece, w),
+            backward.reshape(width, piece, w),
+            jnp.broadcast_to(decay_cols[None], (width, 8, w)),
+        ],
+        axis=1,
+    )
+    out = pl.pallas_call(
+        functools.partial(scan_kernel, rows_n, width),
+        out_shape=jax.ShapeDtypeStruct((width, 2 * piece, w), jnp.float32),
+        in_specs=[pl.BlockSpec(memory_space=pltpu.VMEM)],
+        out_specs=pl.BlockSpec(memory_space=pltpu.VMEM),
         scratch_shapes=[
-            pltpu.VMEM((2, rounds, s + 8, w), jnp.float32),
-            pltpu.VMEM((2, rounds + 1, s + 8, w), jnp.float32),
+            pltpu.VMEM((width, 2 * piece + 8, w), jnp.float32),
+            pltpu.VMEM((2, 2 * rounds + 1, piece + 8, w), jnp.float32),
+            pltpu.VMEM((width, 2 * piece, w), jnp.float32),
+            pltpu.VMEM((width, 2 * piece, w), jnp.float32),
+            pltpu.SemaphoreType.DMA((width,)),
+            pltpu.SemaphoreType.DMA((width,)),
             pltpu.SemaphoreType.DMA((2, rounds)),
             pltpu.SemaphoreType.DMA((2, rounds)),
+            pltpu.SemaphoreType.DMA((width,)),
+            pltpu.SemaphoreType.DMA((width,)),
+            pltpu.SemaphoreType.DMA((2,)),
         ],
         compiler_params=pltpu.CompilerParams(collective_id=1, has_side_effects=True),
-    )(x, y)
+    )(pack)
+    return out[:, :piece].reshape(s, w), out[:, piece:].reshape(s, w)
 
 
 def shards(count, groups, token_values, b_inputs, c_inputs, log_decay, grad_out):

time: 145 us -> 106 us (0.73)
  the two profiles are of different devices: /device:TPU:62 before, /device:TPU:2 now
where the time goes in v4:
time: 106 us
  Pallas kernels  66.3 us (63%)
  matrix products  20.6 us (19%)
  local copies, waits for them, and re-layouts  12 us (11%)
  other arithmetic  5.47 us (5%)
    pallas_call x1, Pallas kernels, exclusive_scans(): pl.pallas_call(functools.partial(scan_kernel, rows_n, width), out_shape=j...  38.7 us
    pallas_call x1, Pallas kernels, head_sum(): pl.pallas_call(functools.partial(head_sum_kernel, n), out_shape=jax.Shape...  27.6 us
    dot_general x8, matrix products, head_step(): lax.dot_general(dy_head, x_head, (((1,), (1,)), ((), ())), preferred_elem...  10.8 us
    unnamed x17, local copies, waits for them, and re-layouts  4.74 us
    dot_general x8, matrix products, head_step(): lax.dot_general(mixing, dy_head, (((0,), (0,)), ((), ())), preferred_elem...  2.68 us

profile of v4, /device:TPU:2, one launch (start us, length us, event | category | flops | bytes accessed | tf_op | source)
XLA Modules:
  0.0 105.5 jit_solution(2456366265641676802)
XLA Ops:
  0.6 1.9 %reduce-window.6 = f32[8,3,128]{2,0,1:T(8,128)S(1)} reduce-window(f32[8,3,128]{2,0,1:T(8,128)} %bitcast.52, f32[]{:T(128)} %constant.50.clone.1), window={size=1x1x128 pad=0_0x0_0x127_0}, to_apply=%region_0.0 | reduce-window | flops 390144 | bytes 24580 | tf_op jit(solution)/shard_map/reduce-window
  2.8 0.7 exponential_bitcast_fusion
  3.5 1.2 %fusion.29 = f32[384,384]{1,0:T(8,128)S(1)} fusion(bf16[384,128]{1,0:T(8,128)(2,1)} %param.9, bf16[384,128]{1,0:T(8,128)(2,1)} %param.8), kind=kOutput, calls=%fused_computation.49 | convolution fusion | flops 37748736 | bytes 786432 | tf_op jit(solution)/shard_map/dot_general | solution.py:297
  4.8 13.9 %while.17 = (s32[]{:T(128)}, f32[384,384]{1,0:T(8,128)S(1)}, f32[384,512]{0,1:T(8,128)S(1)}, f32[8,384]{1,0:T(8,128)S(1)}, bf16[384,512]{1,0:T(8,128)(2,1)S(1)},...) while((s32[]{:T(128)}, f32[384,384]{1,0:T(8,128)S(1)}, ...), condition=%wide.region_3.4_spmd.clone.clone, body=%wide.region_2.3_spmd.clone.clone.sunk | while | flops 39665672 | bytes 2176688 | solution.py:324
  4.8 1.3 %fusion.51 = f32[384,384]{1,0:T(8,128)S(1)} fusion(f32[384,384]{1,0:T(8,128)S(1)} %get-tuple-element.277, f32[384]{0:T(512)S(1)} %dynamic-slice_reduce_fusion.2, pred[]{:T(512)S(6)} %compare.3, bf16[384,512]{1,0:T(8,128)(2,1)} %get-tuple-element.292, s32[]{:T(128)S(6)} %select_n.61, bf16[384,512]{1,0:T(8,128)(2,1)S(1)} %get-tuple-element.291), kind=kOutput, calls=%fused_computation.2.clone.1 | convolution fusion | flops 19906560 | bytes 1381888 | tf_op jit(solution)/shard_map/while/body/eval_jaxpr/dot_general | solution.py:314
  6.6 1.3 %fusion.51 = f32[384,384]{1,0:T(8,128)S(1)} fusion(f32[384,384]{1,0:T(8,128)S(1)} %get-tuple-element.277, f32[384]{0:T(512)S(1)} %dynamic-slice_reduce_fusion.2, pred[]{:T(512)S(6)} %compare.3, bf16[384,512]{1,0:T(8,128)(2,1)} %get-tuple-element.292, s32[]{:T(128)S(6)} %select_n.61, bf16[384,512]{1,0:T(8,128)(2,1)S(1)} %get-tuple-element.291), kind=kOutput, calls=%fused_computation.2.clone.1 | convolution fusion | flops 19906560 | bytes 1381888 | tf_op jit(solution)/shard_map/while/body/eval_jaxpr/dot_general | solution.py:314
  8.3 1.3 %fusion.51 = f32[384,384]{1,0:T(8,128)S(1)} fusion(f32[384,384]{1,0:T(8,128)S(1)} %get-tuple-element.277, f32[384]{0:T(512)S(1)} %dynamic-slice_reduce_fusion.2, pred[]{:T(512)S(6)} %compare.3, bf16[384,512]{1,0:T(8,128)(2,1)} %get-tuple-element.292, s32[]{:T(128)S(6)} %select_n.61, bf16[384,512]{1,0:T(8,128)(2,1)S(1)} %get-tuple-element.291), kind=kOutput, calls=%fused_computation.2.clone.1 | convolution fusion | flops 19906560 | bytes 1381888 | tf_op jit(solution)/shard_map/while/body/eval_jaxpr/dot_general | solution.py:314
  10.0 1.3 %fusion.51 = f32[384,384]{1,0:T(8,128)S(1)} fusion(f32[384,384]{1,0:T(8,128)S(1)} %get-tuple-element.277, f32[384]{0:T(512)S(1)} %dynamic-slice_reduce_fusion.2, pred[]{:T(512)S(6)} %compare.3, bf16[384,512]{1,0:T(8,128)(2,1)} %get-tuple-element.292, s32[]{:T(128)S(6)} %select_n.61, bf16[384,512]{1,0:T(8,128)(2,1)S(1)} %get-tuple-element.291), kind=kOutput, calls=%fused_computation.2.clone.1 | convolution fusion | flops 19906560 | bytes 1381888 | tf_op jit(solution)/shard_map/while/body/eval_jaxpr/dot_general | solution.py:314
  11.8 1.3 %fusion.51 = f32[384,384]{1,0:T(8,128)S(1)} fusion(f32[384,384]{1,0:T(8,128)S(1)} %get-tuple-element.277, f32[384]{0:T(512)S(1)} %dynamic-slice_reduce_fusion.2, pred[]{:T(512)S(6)} %compare.3, bf16[384,512]{1,0:T(8,128)(2,1)} %get-tuple-element.292, s32[]{:T(128)S(6)} %select_n.61, bf16[384,512]{1,0:T(8,128)(2,1)S(1)} %get-tuple-element.291), kind=kOutput, calls=%fused_computation.2.clone.1 | convolution fusion | flops 19906560 | bytes 1381888 | tf_op jit(solution)/shard_map/while/body/eval_jaxpr/dot_general | solution.py:314
  13.1 0.3 convolution_dynamic-update-slice_fusion.2
  13.5 1.3 %fusion.51 = f32[384,384]{1,0:T(8,128)S(1)} fusion(f32[384,384]{1,0:T(8,128)S(1)} %get-tuple-element.277, f32[384]{0:T(512)S(1)} %dynamic-slice_reduce_fusion.2, pred[]{:T(512)S(6)} %compare.3, bf16[384,512]{1,0:T(8,128)(2,1)} %get-tuple-element.292, s32[]{:T(128)S(6)} %select_n.61, bf16[384,512]{1,0:T(8,128)(2,1)S(1)} %get-tuple-element.291), kind=kOutput, calls=%fused_computation.2.clone.1 | convolution fusion | flops 19906560 | bytes 1381888 | tf_op jit(solution)/shard_map/while/body/eval_jaxpr/dot_general | solution.py:314
  15.3 1.3 %fusion.51 = f32[384,384]{1,0:T(8,128)S(1)} fusion(f32[384,384]{1,0:T(8,128)S(1)} %get-tuple-element.277, f32[384]{0:T(512)S(1)} %dynamic-slice_reduce_fusion.2, pred[]{:T(512)S(6)} %compare.3, bf16[384,512]{1,0:T(8,128)(2,1)} %get-tuple-element.292, s32[]{:T(128)S(6)} %select_n.61, bf16[384,512]{1,0:T(8,128)(2,1)S(1)} %get-tuple-element.291), kind=kOutput, calls=%fused_computation.2.clone.1 | convolution fusion | flops 19906560 | bytes 1381888 | tf_op jit(solution)/shard_map/while/body/eval_jaxpr/dot_general | solution.py:314
  17.0 1.3 %fusion.51 = f32[384,384]{1,0:T(8,128)S(1)} fusion(f32[384,384]{1,0:T(8,128)S(1)} %get-tuple-element.277, f32[384]{0:T(512)S(1)} %dynamic-slice_reduce_fusion.2, pred[]{:T(512)S(6)} %compare.3, bf16[384,512]{1,0:T(8,128)(2,1)} %get-tuple-element.292, s32[]{:T(128)S(6)} %select_n.61, bf16[384,512]{1,0:T(8,128)(2,1)S(1)} %get-tuple-element.291), kind=kOutput, calls=%fused_computation.2.clone.1 | convolution fusion | flops 19906560 | bytes 1381888 | tf_op jit(solution)/shard_map/while/body/eval_jaxpr/dot_general | solution.py:314
  19.2 0.6 broadcast_in_dim.46
  20.1 0.6 convolution_bitcast_fusion.1
  21.1 1.2 %copy.15 = bf16[384,512]{0,1:T(8,128)(2,1)S(1)} copy(bf16[384,512]{1,0:T(8,128)(2,1)} %get-tuple-element.299) | data formatting | bytes 786432 | tf_op args[0]
  22.4 0.7 copy-done.1
  23.1 1.3 %convolution_bitcast_fusion.2 = f32[128,8,64]{0,2,1:T(8,128)} fusion(bf16[384,8,64]{0,2,1:T(8,128)(2,1)S(1)} %bitcast.46, f32[384,128]{1,0:T(8,128)S(1)} %convert_element_type.32, f32[8,384]{1,0:T(8,128)S(1)} %get-tuple-element.221), kind=kOutput, calls=%fused_computation.27 | convolution fusion | flops 51118080 | bytes 864256 | tf_op jit(solution)/shard_map/htn,thp->nhp/dot_general | solution.py:289
  24.4 1.2 %copy.16 = f32[128,8,64]{2,1,0:T(8,128)S(1)} copy(f32[128,8,64]{0,2,1:T(8,128)} %convolution_bitcast_fusion.2) | data formatting | bytes 524288 | tf_op jit(solution)/shard_map/htn,thp->nhp/transpose | solution.py:289
  25.6 0.9 reshape_reshape.6
  26.5 1.9 %pad_maximum_fusion.pack_ref = f32[8,40,512]{2,1,0:T(8,128)} fusion(f32[8,8,512]{2,1,0:T(8,128)} %broadcast_in_dim.46, f32[8,16,512]{2,1,0:T(8,128)S(1)} %reshape_reshape.7, f32[8,16,512]{2,1,0:T(8,128)} %reshape_reshape.6), kind=kLoop, calls=%fused_computation.37 | loop fusion | flops 327680 | bytes 1310720 | tf_op jit(solution)/shard_map/concatenate | solution.py:242
  28.4 38.7 %shard_map.76 = f32[8,32,512]{2,1,0:T(8,128)} custom-call(f32[8,40,512]{2,1,0:T(8,128)} %pad_maximum_fusion.pack_ref), custom_call_target="tpu_custom_call" | custom-call | tf_op jit(solution)/shard_map/pallas_call | solution.py:250
  67.2 1.8 %fusion.26 = (f32[8,16,512]{2,1,0:T(8,128)}, f32[8,16,512]{2,1,0:T(8,128)S(1)}) fusion(f32[8,32,512]{2,1,0:T(8,128)} %shard_map.76), kind=kLoop, calls=%fused_computation.46 | loop fusion | bytes 1048576 | tf_op jit(solution)/shard_map/slice | solution.py:270
  68.9 0.6 fusion.17
  69.6 0.9 copy.21
  70.6 0.9 copy-done.3
  71.5 1.4 %fusion.31 = f32[384,128]{1,0:T(8,128)S(1)} fusion(f32[384,512]{0,1:T(8,128)S(1)} %bitcast_multiply_fusion.1, f32[128,512]{1,0:T(8,128)S(1)} %bitcast.47), kind=kOutput, calls=%fused_computation.51 | convolution fusion | flops 301989888 | bytes 1245184 | tf_op jit(solution)/shard_map/dot_general | solution.py:336
  73.2 0.7 copy-done.2
  74.0 1.4 %fusion.30 = f32[384,128]{1,0:T(8,128)S(1)} fusion(f32[384,512]{0,1:T(8,128)S(1)} %bitcast_multiply_fusion, f32[128,512]{1,0:T(8,128)S(1)} %bitcast.44), kind=kOutput, calls=%fused_computation.50 | convolution fusion | flops 301989888 | bytes 1245184 | tf_op jit(solution)/shard_map/dot_general | solution.py:333
  75.6 0.7 pad_maximum_fusion.1.x_ref
  76.3 27.6 %shard_map.77 = bf16[8,96,128]{2,1,0:T(8,128)(2,1)} custom-call(bf16[768,128]{1,0:T(8,128)(2,1)} %pad_maximum_fusion.1.x_ref), custom_call_target="tpu_custom_call" | custom-call | tf_op jit(solution)/shard_map/pallas_call | solution.py:66
  103.9 1.6 %fusion.27 = (bf16[4,96,128]{2,1,0:T(8,128)(2,1)}, bf16[4,96,128]{2,1,0:T(8,128)(2,1)}) fusion(bf16[8,96,128]{2,1,0:T(8,128)(2,1)} %shard_map.77), kind=kLoop, calls=%fused_computation.47 | loop fusion | bytes 393216 | tf_op jit(solution)/shard_map/slice | solution.py:342
  (45 shorter events, 4.5 us)
Async XLA Ops:
  3.5 1.3 %copy-start.5 = (bf16[384,512]{1,0:T(8,128)(2,1)S(1)}, bf16[384,512]{1,0:T(8,128)(2,1)}, u32[]{:S(2)}) copy-start(bf16[384,512]{1,0:T(8,128)(2,1)} %param.11) | copy-start | bytes 1179652
  19.0 1.1 %copy-start.4 = (bf16[384,128]{1,0:T(8,128)(2,1)S(1)}, bf16[384,128]{1,0:T(8,128)(2,1)}, u32[]{:S(2)}) copy-start(bf16[384,128]{1,0:T(8,128)(2,1)} %param.9) | copy-start | bytes 294916
  21.0 1.4 %copy-start = (bf16[384,128]{1,0:T(8,128)(2,1)S(1)}, bf16[384,128]{1,0:T(8,128)(2,1)}, u32[]{:S(2)}) copy-start(bf16[384,128]{1,0:T(8,128)(2,1)} %param.8) | copy-start | bytes 294916
  22.4 0.8 copy-start.1
  69.6 1.0 copy-start.6
  70.5 0.9 copy-start.3
  72.9 1.0 copy-start.2

commit v5 on v4

--- a/solution.py
+++ b/solution.py
@@ -61,6 +61,8 @@
 
 
 def head_sum(n, parts):
+    if n == 1:
+        return parts
     rows = parts.shape[0] // n
     width = parts.shape[1]
     out = pl.pallas_call(
@@ -89,8 +91,8 @@
     return steps
 
 
-def scan_kernel(rows_n, width, pack_ref, o_ref, recv1, win, out3, recv3, send1, rsem1,
-                send2, rsem2, send3, rsem3, local):
+def scan_kernel(rows_n, width, pack_ref, x_ref, dy_ref, sc_ref, cr_ref, cc_ref, o_ref, dx_ref,
+                run_ref, recv1, win, out3, recv3, send1, rsem1, send2, rsem2, send3, rsem3, local):
     me = lax.axis_index("seq")
     col = lax.axis_index("head")
     c = me % width
@@ -99,6 +101,27 @@
     steps = scan_steps(rows_n)
     spans = sorted(set(steps))
 
+    length = sc_ref.shape[0]
+    later = lax.broadcasted_iota(jnp.int32, (length, length), 1) >= lax.broadcasted_iota(
+        jnp.int32, (length, length), 0)
+    run_ref[...] = jnp.zeros(run_ref.shape, run_ref.dtype)
+
+    def head(h):
+        gaps = cr_ref[h:h + 1, :] - cc_ref[:, h:h + 1]
+        dec = jnp.where(later, jnp.exp(jnp.where(later, gaps, 0.0)), 0.0)
+        mix = (sc_ref[...] * dec).astype(jnp.bfloat16)
+        dx_ref[h] = jnp.dot(mix, dy_ref[h], preferred_element_type=jnp.float32)
+        pairs = lax.dot_general(
+            x_ref[h], dy_ref[h], (((1,), (1,)), ((), ())), preferred_element_type=jnp.float32)
+        run_ref[...] += dec * pairs
+
+    heads_left = list(range(x_ref.shape[0]))
+
+    def heads(k):
+        for _ in range(k):
+            if heads_left:
+                head(heads_left.pop(0))
+
     barrier = pltpu.get_barrier_semaphore()
     for off in range(1, width):
         peer = y * width + (c + off) % width
@@ -114,6 +137,7 @@
     peers = width - 1
     for d in spans:
         peers = peers + ((rows_n - 1 - y) // d + rows_n - 1) // rows_n + (y // d + rows_n - 1) // rows_n
+    heads(1)
     pl.semaphore_wait(barrier, peers)
 
     own = pltpu.make_async_copy(pack_ref.at[c], recv1.at[c], local.at[0])
@@ -126,6 +150,7 @@
             recv_sem=rsem1.at[off], device_id=(y * width + k, col), device_id_type=MESH)
         cp.start()
         sends.append(cp)
+    heads(3)
     for off in range(1, width):
         k = (c + width - off) % width
         pltpu.make_async_remote_copy(
@@ -174,6 +199,7 @@
             @pl.when(jnp.logical_and(target_row >= 0, target_row < rows_n))
             def _():
                 copy2(way, r, me + sign * d * width).start()
+        heads(1 if r < len(steps) - 1 else len(heads_left))
         for way, sign in ((0, 1), (1, -1)):
             source_row = y - sign * d
             got = jnp.logical_and(source_row >= 0, source_row < rows_n)
@@ -233,7 +259,7 @@
     o_ref[...] = recv3[...]
 
 
-def exclusive_scans(count, decay_cols, forward, backward):
+def exclusive_scans(count, decay_cols, forward, backward, x_heads, dy_heads, scores_t, cumulative):
     s, w = forward.shape
     width = 8 if count % 8 == 0 else 1
     rows_n = count // width
@@ -247,11 +273,16 @@
         ],
         axis=1,
     )
-    out = pl.pallas_call(
+    length = scores_t.shape[0]
+    out, dx, run = pl.pallas_call(
         functools.partial(scan_kernel, rows_n, width),
-        out_shape=jax.ShapeDtypeStruct((width, 2 * piece, w), jnp.float32),
-        in_specs=[pl.BlockSpec(memory_space=pltpu.VMEM)],
-        out_specs=pl.BlockSpec(memory_space=pltpu.VMEM),
+        out_shape=(
+            jax.ShapeDtypeStruct((width, 2 * piece, w), jnp.float32),
+            jax.ShapeDtypeStruct(x_heads.shape, jnp.float32),
+            jax.ShapeDtypeStruct((length, length), jnp.float32),
+        ),
+        in_specs=[pl.BlockSpec(memory_space=pltpu.VMEM)] * 6,
+        out_specs=(pl.BlockSpec(memory_space=pltpu.VMEM),) * 3,
         scratch_shapes=[
             pltpu.VMEM((width, 2 * piece + 8, w), jnp.float32),
             pltpu.VMEM((2, 2 * rounds + 1, piece + 8, w), jnp.float32),
@@ -266,8 +297,8 @@
             pltpu.SemaphoreType.DMA((2,)),
         ],
         compiler_params=pltpu.CompilerParams(collective_id=1, has_side_effects=True),
-    )(pack)
-    return out[:, :piece].reshape(s, w), out[:, piece:].reshape(s, w)
+    )(pack, x_heads, dy_heads, scores_t, cumulative, cumulative.T)
+    return out[:, :piece].reshape(s, w), out[:, piece:].reshape(s, w), dx, run
 
 
 def shards(count, groups, token_values, b_inputs, c_inputs, log_decay, grad_out):
@@ -293,40 +324,20 @@
         "hsn,shp->nhp", decayed_c, dy_heads, preferred_element_type=jnp.float32
     ).reshape(state_size, heads_here * head_dim)
     decay_cols = jnp.repeat(block_decay, head_dim)[None, :]
-    state_in, adjoint_out = exclusive_scans(count, decay_cols, state_local, adjoint_local)
-    scores = lax.dot_general(
-        c_inputs, b_inputs, (((1,), (1,)), ((), ())), preferred_element_type=jnp.float32
-    )
-    entry_indices = lax.iota(jnp.int32, length)
-    causal = entry_indices[:, None] >= entry_indices[None, :]
-
-    def head_step(head_idx, carried):
-        running, dx_local = carried
-        cum_head = lax.dynamic_index_in_dim(cumulative, head_idx, 0, keepdims=False)
-        log_gaps = cum_head[:, None] - cum_head[None, :]
-        decays = jnp.where(causal, jnp.exp(jnp.where(causal, log_gaps, 0.0)), 0.0)
-        mixing = (scores * decays).astype(jnp.bfloat16)
-        x_head = lax.dynamic_slice_in_dim(token_values, head_idx * head_dim, head_dim, 1)
-        dy_head = lax.dynamic_slice_in_dim(grad_out, head_idx * head_dim, head_dim, 1)
-        dx_head = lax.dot_general(
-            mixing, dy_head, (((0,), (0,)), ((), ())), preferred_element_type=jnp.float32
-        )
-        dot_pairs = lax.dot_general(
-            dy_head, x_head, (((1,), (1,)), ((), ())), preferred_element_type=jnp.float32
-        )
-        dx_local = lax.dynamic_update_slice_in_dim(dx_local, dx_head, head_idx * head_dim, 1)
-        return (running + decays * dot_pairs, dx_local)
-
-    start_pair = (
-        jnp.zeros((length, length), jnp.float32),
-        jnp.zeros((length, heads_here * head_dim), jnp.float32),
-    )
-    running, dx_local = lax.fori_loop(0, heads_here, head_step, start_pair)
-    weighted = running.astype(jnp.bfloat16)
-    db_part = lax.dot_general(
-        weighted, c_inputs, (((0,), (0,)), ((), ())), preferred_element_type=jnp.float32
-    )
-    dc_part = jnp.dot(weighted, b_inputs, preferred_element_type=jnp.float32)
+    scores_t = lax.dot_general(
+        b_inputs, c_inputs, (((1,), (1,)), ((), ())), preferred_element_type=jnp.float32
+    )
+    x_split = jnp.transpose(x_heads, (1, 0, 2))
+    dy_split = jnp.transpose(dy_heads, (1, 0, 2))
+    state_in, adjoint_out, dx_split, running_t = exclusive_scans(
+        count, decay_cols, state_local, adjoint_local, x_split, dy_split, scores_t, cumulative
+    )
+    dx_local = jnp.transpose(dx_split, (1, 0, 2)).reshape(length, heads_here * head_dim)
+    weighted_t = running_t.astype(jnp.bfloat16)
+    db_part = jnp.dot(weighted_t, c_inputs, preferred_element_type=jnp.float32)
+    dc_part = lax.dot_general(
+        weighted_t, b_inputs, (((0,), (0,)), ((), ())), preferred_element_type=jnp.float32
+    )
     to_end_cols = jnp.repeat(into_end.T, head_dim, axis=1)
     from_start_cols = jnp.repeat(from_start.T, head_dim, axis=1)
     grad_values = dx_local + to_end_cols * jnp.dot(b_float, adjoint_out, precision=PRECISE)

time: 106 us -> 89.9 us (0.85)
  the two profiles are of different devices: /device:TPU:2 before, /device:TPU:8 now
where the time goes in v5:
time: 89.9 us; the launch traced here: 89.6 us
  Pallas kernels  67.5 us (75%)
  local copies, waits for them, and re-layouts  10.9 us (12%)
  matrix products  6.29 us (7%)
  other arithmetic  3.92 us (4%)
  between operations  0.91 us (1%)
    pallas_call x1, Pallas kernels, exclusive_scans(): pl.pallas_call(functools.partial(scan_kernel, rows_n, width), out_shape=(...  41.2 us
    pallas_call x1, Pallas kernels, head_sum(): pl.pallas_call(functools.partial(head_sum_kernel, n), out_shape=jax.Shape...  26.3 us
    unnamed x17, local copies, waits for them, and re-layouts  2.45 us
    another operation x3, other arithmetic  2.08 us

profile of v5, /device:TPU:8, one launch (start us, length us, event | category | flops | bytes accessed | tf_op | source)
XLA Modules:
  0.0 89.6 jit_solution(7451053560041851218)
XLA Ops:
  0.6 2.0 %reduce-window.6 = f32[8,3,128]{2,0,1:T(8,128)S(1)} reduce-window(f32[8,3,128]{2,0,1:T(8,128)} %bitcast.71, f32[]{:T(128)} %constant.3.clone.1), window={size=1x1x128 pad=0_0x0_0x127_0}, to_apply=%region_0.0 | reduce-window | flops 390144 | bytes 24580 | tf_op jit(solution)/shard_map/reduce-window
  2.6 0.2 slice_reduce_fusion
  2.9 0.1 copy.19
  3.1 0.1 copy.20
  3.2 1.2 %copy.21 = bf16[384,512]{0,1:T(8,128)(2,1)S(1)} copy(bf16[384,512]{1,0:T(8,128)(2,1)} %param.5) | data formatting | bytes 786432 | tf_op args[0]
  4.5 0.6 convolution_bitcast_fusion.2
  5.1 0.2 copy.22
  5.3 0.1 reshape_reshape.6
  5.6 0.2 copy.24
  5.8 0.6 convolution_bitcast_fusion.1
  6.5 0.2 copy.25
  6.7 0.1 reshape_reshape.7
  6.9 0.1 broadcast_in_dim.21
  7.0 0.9 %pad_maximum_fusion.pack_ref = f32[8,40,512]{2,1,0:T(8,128)} fusion(f32[8,8,512]{2,1,0:T(8,128)S(1)} %broadcast_in_dim.22, f32[8,16,512]{2,1,0:T(8,128)S(1)} %reshape_reshape.7, f32[8,16,512]{2,1,0:T(8,128)S(1)} %reshape_reshape.6), kind=kLoop, calls=%fused_computation.18 | loop fusion | flops 327680 | bytes 1310720 | tf_op jit(solution)/shard_map/concatenate | solution.py:268
  7.9 0.7 copy.28.cr_ref
  8.6 1.2 %copy.26 = bf16[384,8,64]{2,0,1:T(8,128)(2,1)} copy(bf16[384,8,64]{0,2,1:T(8,128)(2,1)S(1)} %bitcast.52) | data formatting | bytes 786432 | tf_op jit(solution)/shard_map/reshape | solution.py:318
  9.8 1.2 %copy.27 = bf16[384,8,64]{2,0,1:T(8,128)(2,1)} copy(bf16[384,8,64]{0,2,1:T(8,128)(2,1)S(1)} %bitcast.54) | data formatting | bytes 786432 | tf_op jit(solution)/shard_map/reshape | solution.py:319
  11.0 1.1 %fusion.14.sc_ref = f32[384,384]{1,0:T(8,128)} fusion(bf16[384,128]{1,0:T(8,128)(2,1)S(1)} %copy-done.3, bf16[384,128]{1,0:T(8,128)(2,1)S(1)} %copy-done.5), kind=kOutput, calls=%fused_computation.30 | convolution fusion | flops 37748736 | bytes 786432 | tf_op jit(solution)/shard_map/dot_general | solution.py:327
  12.1 41.2 %shard_map.76 = (f32[8,32,512]{2,1,0:T(8,128)}, f32[8,384,64]{2,1,0:T(8,128)}, f32[384,384]{1,0:T(8,128)}) custom-call(f32[8,40,512]{2,1,0:T(8,128)} %pad_maximum_fusion.pack_ref, bf16[8,384,64]{2,1,0:T(8,128)(2,1)} %bitcast.59, bf16[8,384,64]{2,1,0:T(8,128)(2,1)} %bitcast.60, f32[384,384]{1,0:T(8,128)} %fusion.14.sc_ref, f32[8,384]{1,0:T(8,128)} %copy.28.cr_ref, ...), custom_call_target="tpu_custom_call" | custom-call | tf_op jit(solution)/shard_map/pallas_call | solution.py:277
  53.3 1.8 %fusion.12 = (f32[8,16,512]{2,1,0:T(8,128)}, f32[8,16,512]{2,1,0:T(8,128)S(1)}) fusion(f32[8,32,512]{2,1,0:T(8,128)} %get-tuple-element.7), kind=kLoop, calls=%fused_computation.28 | loop fusion | bytes 1048576 | tf_op jit(solution)/shard_map/slice | solution.py:301
  55.2 0.1 bitcast_multiply_fusion
  55.3 1.4 %fusion.15 = f32[384,128]{1,0:T(8,128)S(1)} fusion(f32[384,512]{0,1:T(8,128)S(1)} %bitcast_multiply_fusion, f32[128,512]{1,0:T(8,128)S(1)} %bitcast.63), kind=kOutput, calls=%fused_computation.31 | convolution fusion | flops 301989888 | bytes 1245184 | tf_op jit(solution)/shard_map/dot_general | solution.py:344
  56.7 0.2 fusion.3
  57.0 0.1 bitcast_multiply_fusion.1
  57.1 1.4 %fusion.16 = f32[384,128]{1,0:T(8,128)S(1)} fusion(f32[384,512]{0,1:T(8,128)S(1)} %bitcast_multiply_fusion.1, f32[128,512]{1,0:T(8,128)S(1)} %bitcast.68), kind=kOutput, calls=%fused_computation.32 | convolution fusion | flops 301989888 | bytes 1245184 | tf_op jit(solution)/shard_map/dot_general | solution.py:347
  58.5 0.3 fusion.4
  58.8 0.7 pad_maximum_fusion.1.x_ref
  59.5 26.3 %shard_map.77 = bf16[8,96,128]{2,1,0:T(8,128)(2,1)} custom-call(bf16[768,128]{1,0:T(8,128)(2,1)} %pad_maximum_fusion.1.x_ref), custom_call_target="tpu_custom_call" | custom-call | tf_op jit(solution)/shard_map/pallas_call | solution.py:68
  85.8 1.6 %fusion.13 = (bf16[4,96,128]{2,1,0:T(8,128)(2,1)}, bf16[4,96,128]{2,1,0:T(8,128)(2,1)}) fusion(bf16[8,96,128]{2,1,0:T(8,128)(2,1)} %shard_map.77), kind=kLoop, calls=%fused_computation.29 | loop fusion | bytes 393216 | tf_op jit(solution)/shard_map/slice | solution.py:353
  87.5 0.4 copy.29
  88.0 0.6 fusion.2
  88.6 0.9 %copy.34 = bf16[384,512]{1,0:T(8,128)(2,1)} copy(bf16[384,512]{0,1:T(8,128)(2,1)S(1)} %fusion.2) | data formatting | bytes 786432
  (27 shorter events, 0.6 us)
Async XLA Ops:
  0.6 3.8 %copy-start.3 = (bf16[384,128]{1,0:T(8,128)(2,1)S(1)}, bf16[384,128]{1,0:T(8,128)(2,1)}, u32[]{:S(2)}) copy-start(bf16[384,128]{1,0:T(8,128)(2,1)} %param.6) | copy-start | bytes 294916
  3.0 4.9 %copy-start = (f32[8,3,128]{0,2,1:T(8,128)}, f32[8,3,128]{0,2,1:T(8,128)S(1)}, u32[]{:S(2)}) copy-start(f32[8,3,128]{0,2,1:T(8,128)S(1)} %copy.19) | copy-start | bytes 36868
  4.4 1.1 %copy-start.6 = (bf16[384,512]{1,0:T(8,128)(2,1)S(1)}, bf16[384,512]{1,0:T(8,128)(2,1)}, u32[]{:S(2)}) copy-start(bf16[384,512]{1,0:T(8,128)(2,1)} %param.9) | copy-start | bytes 1179652
  4.5 1.3 %copy-start.5 = (bf16[384,128]{1,0:T(8,128)(2,1)S(1)}, bf16[384,128]{1,0:T(8,128)(2,1)}, u32[]{:S(2)}) copy-start(bf16[384,128]{1,0:T(8,128)(2,1)} %param.7) | copy-start | bytes 294916
  55.1 1.6 %copy-start.1 = (f32[384,384]{1,0:T(8,128)S(1)}, f32[384,384]{1,0:T(8,128)}, u32[]{:S(2)}) copy-start(f32[384,384]{1,0:T(8,128)} %get-tuple-element.8) | copy-start | bytes 1769476
  55.2 1.9 %copy-start.4 = (f32[8,16,512]{2,1,0:T(8,128)S(1)}, f32[8,16,512]{2,1,0:T(8,128)}, u32[]{:S(2)}) copy-start(f32[8,16,512]{2,1,0:T(8,128)} %get-tuple-element.15) | copy-start | bytes 786436
  57.1 30.4 %copy-start.2 = (f32[8,384,64]{2,1,0:T(8,128)S(1)}, f32[8,384,64]{2,1,0:T(8,128)}, u32[]{:S(2)}) copy-start(f32[8,384,64]{2,1,0:T(8,128)} %get-tuple-element.6) | copy-start | bytes 2359300

commit v6 on v5

--- a/solution.py
+++ b/solution.py
@@ -110,12 +110,15 @@
         gaps = cr_ref[h:h + 1, :] - cc_ref[:, h:h + 1]
         dec = jnp.where(later, jnp.exp(jnp.where(later, gaps, 0.0)), 0.0)
         mix = (sc_ref[...] * dec).astype(jnp.bfloat16)
-        dx_ref[h] = jnp.dot(mix, dy_ref[h], preferred_element_type=jnp.float32)
+        lanes = slice(h * hd, (h + 1) * hd)
+        dy_h = dy_ref[:, lanes]
+        dx_ref[:, lanes] = jnp.dot(mix, dy_h, preferred_element_type=jnp.float32)
         pairs = lax.dot_general(
-            x_ref[h], dy_ref[h], (((1,), (1,)), ((), ())), preferred_element_type=jnp.float32)
+            x_ref[:, lanes], dy_h, (((1,), (1,)), ((), ())), preferred_element_type=jnp.float32)
         run_ref[...] += dec * pairs
 
-    heads_left = list(range(x_ref.shape[0]))
+    heads_left = list(range(cr_ref.shape[0]))
+    hd = x_ref.shape[1] // cr_ref.shape[0]
 
     def heads(k):
         for _ in range(k):
@@ -327,12 +330,9 @@
     scores_t = lax.dot_general(
         b_inputs, c_inputs, (((1,), (1,)), ((), ())), preferred_element_type=jnp.float32
     )
-    x_split = jnp.transpose(x_heads, (1, 0, 2))
-    dy_split = jnp.transpose(dy_heads, (1, 0, 2))
-    state_in, adjoint_out, dx_split, running_t = exclusive_scans(
-        count, decay_cols, state_local, adjoint_local, x_split, dy_split, scores_t, cumulative
-    )
-    dx_local = jnp.transpose(dx_split, (1, 0, 2)).reshape(length, heads_here * head_dim)
+    state_in, adjoint_out, dx_local, running_t = exclusive_scans(
+        count, decay_cols, state_local, adjoint_local, token_values, grad_out, scores_t, cumulative
+    )
     weighted_t = running_t.astype(jnp.bfloat16)
     db_part = jnp.dot(weighted_t, c_inputs, preferred_element_type=jnp.float32)
     dc_part = lax.dot_general(

time: 89.9 us -> 86.8 us (0.966)
  local copies, waits for them, and re-layouts: 10.9 us -> 6.79 us
    reshape x2 -> x1, local copies, waits for them, and re-layouts: 2.35 us -> 0.26 us  [shards(): to_end_cols = jnp.repeat(into_end.T, head_dim, axis=1)]
    slice x1, local copies, waits for them, and re-layouts: 1.63 us -> 0.69 us  [shards(): return (grad_values.astype(jnp.bfloat16), both[:length], both[length:])]
    unnamed x17 -> x18, local copies, waits for them, and re-layouts: 2.45 us -> 2.43 us
where the time goes in v6:
time: 86.8 us; the launch traced here: 86.3 us
  Pallas kernels  67 us (77%)
  matrix products  6.89 us (8%)
  local copies, waits for them, and re-layouts  6.79 us (8%)
  other arithmetic  4.72 us (5%)
  between operations  0.89 us (1%)
    pallas_call x1, Pallas kernels, exclusive_scans(): pl.pallas_call(functools.partial(scan_kernel, rows_n, width), out_shape=(...  40.8 us
    pallas_call x1, Pallas kernels, head_sum(): pl.pallas_call(functools.partial(head_sum_kernel, n), out_shape=jax.Shape...  26.2 us
    unnamed x18, local copies, waits for them, and re-layouts  2.43 us
    another operation x3, other arithmetic  2.08 us

profile of v6, /device:TPU:8, one launch (start us, length us, event | category | flops | bytes accessed | tf_op | source)
XLA Modules:
  0.0 86.3 jit_solution(16230584824870440922)
XLA Ops:
  0.6 2.0 %reduce-window.6 = f32[8,3,128]{2,0,1:T(8,128)S(1)} reduce-window(f32[8,3,128]{2,0,1:T(8,128)} %bitcast.60, f32[]{:T(128)} %constant.3.clone.1), window={size=1x1x128 pad=0_0x0_0x127_0}, to_apply=%region_0.0 | reduce-window | flops 390144 | bytes 24580 | tf_op jit(solution)/shard_map/reduce-window
  2.6 0.2 slice_reduce_fusion
  2.9 0.1 copy.17
  3.2 0.7 copy.24.cr_ref
  3.9 0.9 %convert_element_type.27 = f32[384,128]{1,0:T(8,128)S(1)} convert(bf16[384,128]{1,0:T(8,128)(2,1)} %param.7) | non-fusion elementwise | flops 49152 | bytes 294912 | tf_op jit(solution)/shard_map/convert_element_type | solution.py:318
  5.0 0.1 copy.25
  5.1 0.1 copy.18
  5.2 0.1 copy.21
  5.3 0.5 copy-done.4
  5.9 0.2 copy.19
  6.1 0.6 convolution_bitcast_fusion.2
  6.7 0.2 copy.20
  7.0 0.1 reshape_reshape.6
  7.1 0.6 copy-done.3
  7.7 0.2 copy.22
  7.9 0.6 convolution_bitcast_fusion.1
  8.5 0.2 copy.23
  8.8 0.1 reshape_reshape.7
  8.9 0.9 %pad_maximum_fusion.pack_ref = f32[8,40,512]{2,1,0:T(8,128)} fusion(f32[8,8,512]{2,1,0:T(8,128)S(1)} %broadcast_in_dim.22, f32[8,16,512]{2,1,0:T(8,128)S(1)} %reshape_reshape.7, f32[8,16,512]{2,1,0:T(8,128)S(1)} %reshape_reshape.6), kind=kLoop, calls=%fused_computation.20 | loop fusion | flops 327680 | bytes 1310720 | tf_op jit(solution)/shard_map/concatenate | solution.py:271
  9.8 1.1 %fusion.17.sc_ref = f32[384,384]{1,0:T(8,128)} fusion(bf16[384,128]{1,0:T(8,128)(2,1)S(1)} %copy-done.2, bf16[384,128]{1,0:T(8,128)(2,1)S(1)} %copy-done.5), kind=kOutput, calls=%fused_computation.32 | convolution fusion | flops 37748736 | bytes 786432 | tf_op jit(solution)/shard_map/dot_general | solution.py:330
  10.9 40.8 %shard_map.76 = (f32[8,32,512]{2,1,0:T(8,128)}, f32[384,512]{1,0:T(8,128)}, f32[384,384]{1,0:T(8,128)}) custom-call(f32[8,40,512]{2,1,0:T(8,128)} %pad_maximum_fusion.pack_ref, bf16[384,512]{1,0:T(8,128)(2,1)} %x_ref.1, bf16[384,512]{1,0:T(8,128)(2,1)} %dy_ref.1, f32[384,384]{1,0:T(8,128)} %fusion.17.sc_ref, f32[8,384]{1,0:T(8,128)} %copy.24.cr_ref, ...), custom_call_target="tpu_custom_call" | custom-call | tf_op jit(solution)/shard_map/pallas_call | solution.py:280
  51.7 1.1 %fusion.15 = (f32[8,16,512]{2,1,0:T(8,128)S(1)}, f32[8,16,512]{2,1,0:T(8,128)S(1)}) fusion(f32[8,32,512]{2,1,0:T(8,128)} %get-tuple-element.7), kind=kLoop, calls=%fused_computation.30 | loop fusion | bytes 1048576 | tf_op jit(solution)/shard_map/slice | solution.py:304
  52.9 1.4 %fusion.18 = f32[384,128]{1,0:T(8,128)S(1)} fusion(f32[384,512]{0,1:T(8,128)S(1)} %bitcast_multiply_fusion, f32[128,512]{1,0:T(8,128)S(1)} %bitcast.57), kind=kOutput, calls=%fused_computation.33 | convolution fusion | flops 301989888 | bytes 1245184 | tf_op jit(solution)/shard_map/dot_general | solution.py:347
  54.3 0.3 fusion.4
  54.6 1.4 %fusion.5 = f32[384,128]{1,0:T(8,128)S(1)} fusion(f32[128,512]{1,0:T(8,128)S(1)} %bitcast.51, f32[384,512]{0,1:T(8,128)S(1)} %bitcast.45, bf16[384,512]{0,1:T(8,128)(2,1)S(1)} %copy.19), kind=kOutput, calls=%fused_computation.13 | convolution fusion | flops 302383104 | bytes 1638400 | tf_op jit(solution)/shard_map/dot_general | solution.py:344
  56.1 0.2 fusion.3
  56.3 0.7 pad_maximum_fusion.1.x_ref
  57.0 26.2 %shard_map.77 = bf16[8,96,128]{2,1,0:T(8,128)(2,1)} custom-call(bf16[768,128]{1,0:T(8,128)(2,1)} %pad_maximum_fusion.1.x_ref), custom_call_target="tpu_custom_call" | custom-call | tf_op jit(solution)/shard_map/pallas_call | solution.py:68
  83.3 0.3 copy.27
  83.5 0.9 copy-done.7
  84.4 1.2 %fusion.2 = bf16[384,512]{1,0:T(8,128)(2,1)} fusion(f32[384,512]{1,0:T(8,128)S(1)} %copy-done.7, f32[384,512]{1,0:T(8,128)S(1)} %copy.27, f32[128,512]{1,0:T(8,128)S(1)} %bitcast.52, bf16[384,128]{1,0:T(8,128)(2,1)S(1)} %copy-done.2), kind=kOutput, calls=%fused_computation.5 | convolution fusion | flops 302579712 | bytes 2326528 | tf_op jit(solution)/shard_map/dot_general | solution.py:343
  85.6 0.7 fusion.16
  (25 shorter events, 0.6 us)
Async XLA Ops:
  0.6 4.2 %copy-start.2 = (bf16[384,128]{1,0:T(8,128)(2,1)S(1)}, bf16[384,128]{1,0:T(8,128)(2,1)}, u32[]{:S(2)}) copy-start(bf16[384,128]{1,0:T(8,128)(2,1)} %param.6) | copy-start | bytes 294916
  3.0 2.0 %copy-start = (f32[8,3,128]{0,2,1:T(8,128)}, f32[8,3,128]{0,2,1:T(8,128)S(1)}, u32[]{:S(2)}) copy-start(f32[8,3,128]{0,2,1:T(8,128)S(1)} %copy.17) | copy-start | bytes 36868
  4.9 1.0 %copy-start.4 = (bf16[384,512]{1,0:T(8,128)(2,1)S(1)}, bf16[384,512]{1,0:T(8,128)(2,1)}, u32[]{:S(2)}) copy-start(bf16[384,512]{1,0:T(8,128)(2,1)} %x_ref.1) | copy-start | bytes 1179652
  6.7 1.0 %copy-start.3 = (bf16[384,512]{1,0:T(8,128)(2,1)S(1)}, bf16[384,512]{1,0:T(8,128)(2,1)}, u32[]{:S(2)}) copy-start(bf16[384,512]{1,0:T(8,128)(2,1)} %dy_ref.1) | copy-start | bytes 1179652
  8.9 0.9 %copy-start.5 = (bf16[384,128]{1,0:T(8,128)(2,1)S(1)}, bf16[384,128]{1,0:T(8,128)(2,1)}, u32[]{:S(2)}) copy-start(bf16[384,128]{1,0:T(8,128)(2,1)} %param.7) | copy-start | bytes 294916
  52.9 1.4 %copy-start.1 = (f32[384,384]{1,0:T(8,128)S(1)}, f32[384,384]{1,0:T(8,128)}, u32[]{:S(2)}) copy-start(f32[384,384]{1,0:T(8,128)} %get-tuple-element.8) | copy-start | bytes 1769476
  83.3 1.1 %copy-start.7 = (f32[384,512]{1,0:T(8,128)S(1)}, f32[384,512]{1,0:T(8,128)}, u32[]{:S(2)}) copy-start(f32[384,512]{1,0:T(8,128)} %get-tuple-element.6) | copy-start | bytes 2359300
  84.4 1.2 %copy-start.6 = (bf16[8,96,128]{2,1,0:T(8,128)(2,1)S(1)}, bf16[8,96,128]{2,1,0:T(8,128)(2,1)}, u32[]{:S(2)}) copy-start(bf16[8,96,128]{2,1,0:T(8,128)(2,1)} %shard_map.77) | copy-start | bytes 589828

commit v7 on v6

--- a/solution.py
+++ b/solution.py
@@ -11,78 +11,6 @@
 MESH = pl.DeviceIdType.MESH
 
 
-def head_sum_kernel(n, x_ref, o_ref, gather1, gather2, send1, recv1, send2, recv2):
-    me = lax.axis_index("head")
-    row = lax.axis_index("seq")
-    rows = gather1.shape[1]
-    barrier = pltpu.get_barrier_semaphore()
-    for k in range(1, n):
-        peer = lax.rem(me + k, n)
-        pl.semaphore_signal(barrier, inc=1, device_id=(row, peer), device_id_type=MESH)
-    pl.semaphore_wait(barrier, n - 1)
-
-    def chunk(i):
-        return x_ref.at[pl.ds(pl.multiple_of(i * rows, rows), rows)]
-
-    sends = []
-    for k in range(1, n):
-        peer = lax.rem(me + k, n)
-        c = pltpu.make_async_remote_copy(
-            src_ref=chunk(peer), dst_ref=gather1.at[me], send_sem=send1.at[k],
-            recv_sem=recv1.at[k], device_id=(row, peer), device_id_type=MESH)
-        c.start()
-        sends.append(c)
-    total = x_ref[pl.ds(pl.multiple_of(me * rows, rows), rows), :].astype(jnp.float32)
-    for k in range(1, n):
-        source = lax.rem(me + n - k, n)
-        pltpu.make_async_remote_copy(
-            src_ref=chunk(source), dst_ref=gather1.at[source], send_sem=send1.at[k],
-            recv_sem=recv1.at[k], device_id=(row, source), device_id_type=MESH).wait_recv()
-        total = total + gather1[source].astype(jnp.float32)
-    for c in sends:
-        c.wait_send()
-    gather2[me] = total.astype(gather2.dtype)
-    sends = []
-    for k in range(1, n):
-        peer = lax.rem(me + k, n)
-        c = pltpu.make_async_remote_copy(
-            src_ref=gather2.at[me], dst_ref=gather2.at[me], send_sem=send2.at[k],
-            recv_sem=recv2.at[k], device_id=(row, peer), device_id_type=MESH)
-        c.start()
-        sends.append(c)
-    for k in range(1, n):
-        source = lax.rem(me + n - k, n)
-        pltpu.make_async_remote_copy(
-            src_ref=gather2.at[source], dst_ref=gather2.at[source], send_sem=send2.at[k],
-            recv_sem=recv2.at[k], device_id=(row, source), device_id_type=MESH).wait_recv()
-    for c in sends:
-        c.wait_send()
-    o_ref[...] = gather2[...]
-
-
-def head_sum(n, parts):
-    if n == 1:
-        return parts
-    rows = parts.shape[0] // n
-    width = parts.shape[1]
-    out = pl.pallas_call(
-        functools.partial(head_sum_kernel, n),
-        out_shape=jax.ShapeDtypeStruct((n, rows, width), parts.dtype),
-        in_specs=[pl.BlockSpec(memory_space=pltpu.VMEM)],
-        out_specs=pl.BlockSpec(memory_space=pltpu.VMEM),
-        scratch_shapes=[
-            pltpu.VMEM((n, rows, width), parts.dtype),
-            pltpu.VMEM((n, rows, width), parts.dtype),
-            pltpu.SemaphoreType.DMA((n,)),
-            pltpu.SemaphoreType.DMA((n,)),
-            pltpu.SemaphoreType.DMA((n,)),
-            pltpu.SemaphoreType.DMA((n,)),
-        ],
-        compiler_params=pltpu.CompilerParams(collective_id=0, has_side_effects=True),
-    )(parts)
-    return out.reshape(n * rows, width)
-
-
 def scan_steps(n):
     steps, d = [1], 1
     while d < n:
@@ -91,8 +19,22 @@
     return steps
 
 
-def scan_kernel(rows_n, width, pack_ref, x_ref, dy_ref, sc_ref, cr_ref, cc_ref, o_ref, dx_ref,
-                run_ref, recv1, win, out3, recv3, send1, rsem1, send2, rsem2, send3, rsem3, local):
+def nt_dot(p, q):
+    return lax.dot_general(p, q, (((1,), (1,)), ((), ())), preferred_element_type=jnp.float32)
+
+
+def nt_dot_f32(p, q):
+    ph = p.astype(jnp.bfloat16)
+    pl_ = (p - ph.astype(jnp.float32)).astype(jnp.bfloat16)
+    qh = q.astype(jnp.bfloat16)
+    ql = (q - qh.astype(jnp.float32)).astype(jnp.bfloat16)
+    return nt_dot(ph, qh) + (nt_dot(ph, ql) + nt_dot(pl_, qh))
+
+
+def scan_kernel(rows_n, width, groups, pack_ref, x_ref, dy_ref, sc_ref, cr_ref, cc_ref, xs_ref,
+                ds_ref, b_ref, c_ref, o_ref, dx_ref, sum_ref, run_ref, recv1, win, out3, recv3,
+                full, parts, gather1, gather2, send1, rsem1, send2, rsem2, send3, rsem3, local,
+                hsend1, hrecv1, hsend2, hrecv2):
     me = lax.axis_index("seq")
     col = lax.axis_index("head")
     c = me % width
@@ -137,7 +79,11 @@
         @pl.when(y - d >= 0)
         def _():
             pl.semaphore_signal(barrier, inc=1, device_id=(me - d * width, col), device_id_type=MESH)
-    peers = width - 1
+    z = lax.axis_index("head")
+    for off in range(1, groups):
+        pl.semaphore_signal(
+            barrier, inc=1, device_id=(me, (z + off) % groups), device_id_type=MESH)
+    peers = width - 1 + groups - 1
     for d in spans:
         peers = peers + ((rows_n - 1 - y) // d + rows_n - 1) // rows_n + (y // d + rows_n - 1) // rows_n
     heads(1)
@@ -261,8 +207,62 @@
         cp.wait_send()
     o_ref[...] = recv3[...]
 
-
-def exclusive_scans(count, decay_cols, forward, backward, x_heads, dy_heads, scores_t, cumulative):
+    s = width * piece
+    for k in range(width):
+        full[0, k * piece:(k + 1) * piece, :] = recv3[k, :piece, :]
+        full[1, k * piece:(k + 1) * piece, :] = recv3[k, piece:, :]
+    weighted = run_ref[...].astype(jnp.bfloat16)
+    part_b = jnp.dot(weighted, c_ref[...], preferred_element_type=jnp.float32) + nt_dot_f32(
+        xs_ref[...], full[1])
+    part_c = lax.dot_general(
+        weighted, b_ref[...], (((0,), (0,)), ((), ())), preferred_element_type=jnp.float32
+    ) + nt_dot_f32(ds_ref[...], full[0])
+    n_rows = part_b.shape[0]
+    parts[:n_rows, :] = part_b.astype(parts.dtype)
+    parts[n_rows:, :] = part_c.astype(parts.dtype)
+    rows = gather1.shape[1]
+
+    def chunk(i):
+        return parts.at[pl.ds(pl.multiple_of(i * rows, rows), rows)]
+
+    sends = []
+    for k in range(1, groups):
+        peer = (z + k) % groups
+        cp = pltpu.make_async_remote_copy(
+            src_ref=chunk(peer), dst_ref=gather1.at[z], send_sem=hsend1.at[k],
+            recv_sem=hrecv1.at[k], device_id=(me, peer), device_id_type=MESH)
+        cp.start()
+        sends.append(cp)
+    total = parts[pl.ds(pl.multiple_of(z * rows, rows), rows), :].astype(jnp.float32)
+    for k in range(1, groups):
+        source = (z + groups - k) % groups
+        pltpu.make_async_remote_copy(
+            src_ref=chunk(source), dst_ref=gather1.at[source], send_sem=hsend1.at[k],
+            recv_sem=hrecv1.at[k], device_id=(me, source), device_id_type=MESH).wait_recv()
+        total = total + gather1[source].astype(jnp.float32)
+    for cp in sends:
+        cp.wait_send()
+    gather2[z] = total.astype(gather2.dtype)
+    sends = []
+    for k in range(1, groups):
+        peer = (z + k) % groups
+        cp = pltpu.make_async_remote_copy(
+            src_ref=gather2.at[z], dst_ref=gather2.at[z], send_sem=hsend2.at[k],
+            recv_sem=hrecv2.at[k], device_id=(me, peer), device_id_type=MESH)
+        cp.start()
+        sends.append(cp)
+    for k in range(1, groups):
+        source = (z + groups - k) % groups
+        pltpu.make_async_remote_copy(
+            src_ref=gather2.at[source], dst_ref=gather2.at[source], send_sem=hsend2.at[k],
+            recv_sem=hrecv2.at[k], device_id=(me, source), device_id_type=MESH).wait_recv()
+    for cp in sends:
+        cp.wait_send()
+    sum_ref[...] = gather2[...]
+
+
+def exclusive_scans(count, groups, decay_cols, forward, backward, x, dy, scores_t, cumulative,
+                    x_scaled, dy_scaled, b_inputs, c_inputs):
     s, w = forward.shape
     width = 8 if count % 8 == 0 else 1
     rows_n = count // width
@@ -277,20 +277,26 @@
         axis=1,
     )
     length = scores_t.shape[0]
-    out, dx, run = pl.pallas_call(
-        functools.partial(scan_kernel, rows_n, width),
+    chunk_rows = 2 * length // groups
+    out, dx, sums = pl.pallas_call(
+        functools.partial(scan_kernel, rows_n, width, groups),
         out_shape=(
             jax.ShapeDtypeStruct((width, 2 * piece, w), jnp.float32),
-            jax.ShapeDtypeStruct(x_heads.shape, jnp.float32),
-            jax.ShapeDtypeStruct((length, length), jnp.float32),
+            jax.ShapeDtypeStruct(x.shape, jnp.float32),
+            jax.ShapeDtypeStruct((groups, chunk_rows, s), jnp.bfloat16),
         ),
-        in_specs=[pl.BlockSpec(memory_space=pltpu.VMEM)] * 6,
+        in_specs=[pl.BlockSpec(memory_space=pltpu.VMEM)] * 10,
         out_specs=(pl.BlockSpec(memory_space=pltpu.VMEM),) * 3,
         scratch_shapes=[
+            pltpu.VMEM((length, length), jnp.float32),
             pltpu.VMEM((width, 2 * piece + 8, w), jnp.float32),
             pltpu.VMEM((2, 2 * rounds + 1, piece + 8, w), jnp.float32),
             pltpu.VMEM((width, 2 * piece, w), jnp.float32),
             pltpu.VMEM((width, 2 * piece, w), jnp.float32),
+            pltpu.VMEM((2, s, w), jnp.float32),
+            pltpu.VMEM((2 * length, s), jnp.bfloat16),
+            pltpu.VMEM((groups, chunk_rows, s), jnp.bfloat16),
+            pltpu.VMEM((groups, chunk_rows, s), jnp.bfloat16),
             pltpu.SemaphoreType.DMA((width,)),
             pltpu.SemaphoreType.DMA((width,)),
             pltpu.SemaphoreType.DMA((2, rounds)),
@@ -298,10 +304,15 @@
             pltpu.SemaphoreType.DMA((width,)),
             pltpu.SemaphoreType.DMA((width,)),
             pltpu.SemaphoreType.DMA((2,)),
+            pltpu.SemaphoreType.DMA((groups,)),
+            pltpu.SemaphoreType.DMA((groups,)),
+            pltpu.SemaphoreType.DMA((groups,)),
+            pltpu.SemaphoreType.DMA((groups,)),
         ],
         compiler_params=pltpu.CompilerParams(collective_id=1, has_side_effects=True),
-    )(pack, x_heads, dy_heads, scores_t, cumulative, cumulative.T)
-    return out[:, :piece].reshape(s, w), out[:, piece:].reshape(s, w), dx, run
+    )(pack, x, dy, scores_t, cumulative, cumulative.T, x_scaled, dy_scaled, b_inputs, c_inputs)
+    sums = sums.reshape(2 * length, s)
+    return out[:, :piece].reshape(s, w), out[:, piece:].reshape(s, w), dx, sums[:length], sums[length:]
 
 
 def shards(count, groups, token_values, b_inputs, c_inputs, log_decay, grad_out):
@@ -330,27 +341,15 @@
     scores_t = lax.dot_general(
         b_inputs, c_inputs, (((1,), (1,)), ((), ())), preferred_element_type=jnp.float32
     )
-    state_in, adjoint_out, dx_local, running_t = exclusive_scans(
-        count, decay_cols, state_local, adjoint_local, token_values, grad_out, scores_t, cumulative
-    )
-    weighted_t = running_t.astype(jnp.bfloat16)
-    db_part = jnp.dot(weighted_t, c_inputs, preferred_element_type=jnp.float32)
-    dc_part = lax.dot_general(
-        weighted_t, b_inputs, (((0,), (0,)), ((), ())), preferred_element_type=jnp.float32
-    )
     to_end_cols = jnp.repeat(into_end.T, head_dim, axis=1)
     from_start_cols = jnp.repeat(from_start.T, head_dim, axis=1)
+    state_in, adjoint_out, dx_local, grad_b, grad_c = exclusive_scans(
+        count, groups, decay_cols, state_local, adjoint_local, token_values, grad_out, scores_t,
+        cumulative, token_values.astype(jnp.float32) * to_end_cols,
+        grad_out.astype(jnp.float32) * from_start_cols, b_inputs, c_inputs,
+    )
     grad_values = dx_local + to_end_cols * jnp.dot(b_float, adjoint_out, precision=PRECISE)
-    db_part = db_part + jnp.dot(
-        token_values.astype(jnp.float32) * to_end_cols, adjoint_out.T, precision=PRECISE
-    )
-    dc_part = dc_part + jnp.dot(
-        grad_out.astype(jnp.float32) * from_start_cols, state_in.T, precision=PRECISE
-    )
-    both = head_sum(
-        groups, jnp.concatenate([db_part, dc_part], axis=0).astype(jnp.bfloat16)
-    )
-    return grad_values.astype(jnp.bfloat16), both[:length], both[length:]
+    return grad_values.astype(jnp.bfloat16), grad_b, grad_c
 
 
 def solution(mesh):

time: 86.8 us -> 82.3 us (0.948)
  the two profiles are of different devices: /device:TPU:8 before, /device:TPU:1 now
where the time goes in v7:
time: 82.3 us; the launch traced here: 81.9 us
  Pallas kernels  64.9 us (79%)
  local copies, waits for them, and re-layouts  7.17 us (9%)
  other arithmetic  5.43 us (7%)
  matrix products  3.55 us (4%)
  between operations  0.86 us (1%)
    pallas_call x1, Pallas kernels, exclusive_scans(): pl.pallas_call(functools.partial(scan_kernel, rows_n, width, groups), out...  64.9 us
    another operation x3, other arithmetic  2.08 us
    slice x1, local copies, waits for them, and re-layouts, exclusive_scans(): sums[length:]  1.71 us

profile of v7, /device:TPU:1, one launch (start us, length us, event | category | flops | bytes accessed | tf_op | source)
XLA Modules:
  0.0 81.9 jit_solution(3610323587310158265)
XLA Ops:
  0.6 2.0 %reduce-window.6 = f32[8,3,128]{2,0,1:T(8,128)S(1)} reduce-window(f32[8,3,128]{2,0,1:T(8,128)} %bitcast.51, f32[]{:T(128)} %constant.3.clone.1), window={size=1x1x128 pad=0_0x0_0x127_0}, to_apply=%region_0.0 | reduce-window | flops 390144 | bytes 24580 | tf_op jit(solution)/shard_map/reduce-window
  2.6 0.2 slice_reduce_fusion
  2.8 0.1 broadcast_add_fusion
  2.9 0.1 copy.17
  3.1 0.1 broadcast_in_dim.20
  3.1 0.1 broadcast_in_dim.21
  3.2 0.7 copy.28.cr_ref
  3.9 0.9 %convert_element_type.23 = f32[384,128]{1,0:T(8,128)S(1)} convert(bf16[384,128]{1,0:T(8,128)(2,1)} %c_ref.1) | non-fusion elementwise | flops 49152 | bytes 294912 | tf_op jit(solution)/shard_map/convert_element_type | solution.py:329
  4.9 0.1 subtract_exponential_fusion
  4.9 0.1 copy.26
  5.0 0.1 copy.24
  5.1 0.1 copy.18
  5.2 0.1 copy.21
  5.3 0.5 copy-done.1
  5.9 0.2 copy.19
  6.1 0.6 convolution_bitcast_fusion.2
  6.7 0.2 copy.20
  7.0 0.1 reshape_reshape.6
  7.1 0.6 copy-done
  7.7 0.2 copy.22
  7.9 0.6 convolution_bitcast_fusion.1
  8.5 0.2 copy.23
  8.8 0.1 reshape_reshape.7
  8.9 0.9 %pad_maximum_fusion.pack_ref = f32[8,40,512]{2,1,0:T(8,128)} fusion(f32[8,8,512]{2,1,0:T(8,128)S(1)} %broadcast_in_dim.22, f32[8,16,512]{2,1,0:T(8,128)S(1)} %reshape_reshape.7, f32[8,16,512]{2,1,0:T(8,128)S(1)} %reshape_reshape.6), kind=kLoop, calls=%fused_computation.14 | loop fusion | flops 327680 | bytes 1310720 | tf_op jit(solution)/shard_map/concatenate | solution.py:271
  9.8 1.1 %fusion.9.sc_ref = f32[384,384]{1,0:T(8,128)} fusion(bf16[384,128]{1,0:T(8,128)(2,1)S(1)} %copy-done.3, bf16[384,128]{1,0:T(8,128)(2,1)S(1)} %copy-done.5), kind=kOutput, calls=%fused_computation.22 | convolution fusion | flops 37748736 | bytes 786432 | tf_op jit(solution)/shard_map/dot_general | solution.py:341
  11.0 0.3 copy.25
  11.3 0.3 copy.27
  11.6 1.5 %convert_multiply_fusion = (f32[384,512]{1,0:T(8,128)}, f32[384,512]{1,0:T(8,128)}) fusion(f32[384,512]{1,0:T(8,128)S(1)} %copy.27, bf16[384,512]{1,0:T(8,128)(2,1)S(1)} %copy-done, f32[384,512]{1,0:T(8,128)S(1)} %copy.25, bf16[384,512]{1,0:T(8,128)(2,1)S(1)} %copy-done.1), kind=kLoop, calls=%fused_computation.8 | loop fusion | flops 786432 | bytes 3932160 | tf_op jit(solution)/shard_map/mul | solution.py:349
  13.0 64.9 %shard_map.76 = (f32[8,32,512]{2,1,0:T(8,128)}, f32[384,512]{1,0:T(8,128)}, bf16[8,96,128]{2,1,0:T(8,128)(2,1)}) custom-call(f32[8,40,512]{2,1,0:T(8,128)} %pad_maximum_fusion.pack_ref, bf16[384,512]{1,0:T(8,128)(2,1)} %x_ref.1, bf16[384,512]{1,0:T(8,128)(2,1)} %dy_ref.1, f32[384,384]{1,0:T(8,128)} %fusion.9.sc_ref, f32[8,384]{1,0:T(8,128)} %copy.28.cr_ref, ...), custom_call_target="tpu_custom_call" | custom-call | tf_op jit(solution)/shard_map/pallas_call | solution.py:281
  78.0 1.7 %fusion.8 = (bf16[4,96,128]{2,1,0:T(8,128)(2,1)}, bf16[4,96,128]{2,1,0:T(8,128)(2,1)}) fusion(bf16[8,96,128]{2,1,0:T(8,128)(2,1)} %get-tuple-element.8), kind=kLoop, calls=%fused_computation.21 | loop fusion | bytes 393216 | tf_op jit(solution)/shard_map/slice | solution.py:315
  79.7 1.0 %slice.30 = f32[8,16,512]{2,1,0:T(8,128)S(1)} slice(f32[8,32,512]{2,1,0:T(8,128)} %get-tuple-element.7), slice={[0:8], [16:32], [0:512]} | slice | bytes 524288 | tf_op jit(solution)/shard_map/slice | solution.py:315
  80.7 1.2 %fusion.2 = bf16[384,512]{1,0:T(8,128)(2,1)} fusion(f32[384,512]{1,0:T(8,128)S(1)} %copy-done.6, f32[384,512]{1,0:T(8,128)S(1)} %copy.25, f32[128,512]{1,0:T(8,128)S(1)} %bitcast.46, bf16[384,128]{1,0:T(8,128)(2,1)S(1)} %copy-done.4), kind=kOutput, calls=%fused_computation.5 | convolution fusion | flops 302579712 | bytes 2326528 | tf_op jit(solution)/shard_map/dot_general | solution.py:351
  (19 shorter events, 0.2 us)
Async XLA Ops:
  0.6 4.2 %copy-start.3 = (bf16[384,128]{1,0:T(8,128)(2,1)S(1)}, bf16[384,128]{1,0:T(8,128)(2,1)}, u32[]{:S(2)}) copy-start(bf16[384,128]{1,0:T(8,128)(2,1)} %b_ref.1) | copy-start | bytes 294916
  3.0 2.0 %copy-start.2 = (f32[8,3,128]{0,2,1:T(8,128)}, f32[8,3,128]{0,2,1:T(8,128)S(1)}, u32[]{:S(2)}) copy-start(f32[8,3,128]{0,2,1:T(8,128)S(1)} %copy.17) | copy-start | bytes 36868
  4.9 1.0 %copy-start.1 = (bf16[384,512]{1,0:T(8,128)(2,1)S(1)}, bf16[384,512]{1,0:T(8,128)(2,1)}, u32[]{:S(2)}) copy-start(bf16[384,512]{1,0:T(8,128)(2,1)} %x_ref.1) | copy-start | bytes 1179652
  6.7 1.0 %copy-start = (bf16[384,512]{1,0:T(8,128)(2,1)S(1)}, bf16[384,512]{1,0:T(8,128)(2,1)}, u32[]{:S(2)}) copy-start(bf16[384,512]{1,0:T(8,128)(2,1)} %dy_ref.1) | copy-start | bytes 1179652
  8.9 0.9 %copy-start.5 = (bf16[384,128]{1,0:T(8,128)(2,1)S(1)}, bf16[384,128]{1,0:T(8,128)(2,1)}, u32[]{:S(2)}) copy-start(bf16[384,128]{1,0:T(8,128)(2,1)} %c_ref.1) | copy-start | bytes 294916
  78.0 2.7 %copy-start.4 = (bf16[384,128]{1,0:T(8,128)(2,1)S(1)}, bf16[384,128]{1,0:T(8,128)(2,1)}, u32[]{:S(2)}) copy-start(bf16[384,128]{1,0:T(8,128)(2,1)} %b_ref.1) | copy-start | bytes 294916
  78.0 2.7 %copy-start.6 = (f32[384,512]{1,0:T(8,128)S(1)}, f32[384,512]{1,0:T(8,128)}, u32[]{:S(2)}) copy-start(f32[384,512]{1,0:T(8,128)} %get-tuple-element.6) | copy-start | bytes 2359300

commit v8 on v7

--- a/solution.py
+++ b/solution.py
@@ -31,9 +31,9 @@
     return nt_dot(ph, qh) + (nt_dot(ph, ql) + nt_dot(pl_, qh))
 
 
-def scan_kernel(rows_n, width, groups, pack_ref, x_ref, dy_ref, sc_ref, cr_ref, cc_ref, xs_ref,
-                ds_ref, b_ref, c_ref, o_ref, dx_ref, sum_ref, run_ref, recv1, win, out3, recv3,
-                full, parts, gather1, gather2, send1, rsem1, send2, rsem2, send3, rsem3, local,
+def scan_kernel(rows_n, width, groups, pack_ref, x_ref, dy_ref, sc_ref, cr_ref, cc_ref, ie_ref,
+                fs_ref, b_ref, c_ref, gv_ref, sum_ref, run_ref, dx_ref, xs_ref, ds_ref, recv1, win,
+                out3, recv3, full, parts, gather1, gather2, send1, rsem1, send2, rsem2, send3, rsem3, local,
                 hsend1, hrecv1, hsend2, hrecv2):
     me = lax.axis_index("seq")
     col = lax.axis_index("head")
@@ -54,9 +54,12 @@
         mix = (sc_ref[...] * dec).astype(jnp.bfloat16)
         lanes = slice(h * hd, (h + 1) * hd)
         dy_h = dy_ref[:, lanes]
+        x_h = x_ref[:, lanes]
+        xs_ref[:, lanes] = x_h.astype(jnp.float32) * ie_ref[:, h:h + 1]
+        ds_ref[:, lanes] = dy_h.astype(jnp.float32) * fs_ref[:, h:h + 1]
         dx_ref[:, lanes] = jnp.dot(mix, dy_h, preferred_element_type=jnp.float32)
         pairs = lax.dot_general(
-            x_ref[:, lanes], dy_h, (((1,), (1,)), ((), ())), preferred_element_type=jnp.float32)
+            x_h, dy_h, (((1,), (1,)), ((), ())), preferred_element_type=jnp.float32)
         run_ref[...] += dec * pairs
 
     heads_left = list(range(cr_ref.shape[0]))
@@ -205,7 +208,6 @@
     own.wait()
     for cp in sends:
         cp.wait_send()
-    o_ref[...] = recv3[...]
 
     s = width * piece
     for k in range(width):
@@ -218,6 +220,15 @@
         weighted, b_ref[...], (((0,), (0,)), ((), ())), preferred_element_type=jnp.float32
     ) + nt_dot_f32(ds_ref[...], full[0])
     n_rows = part_b.shape[0]
+    adj = full[1]
+    adj_hi = adj.astype(jnp.bfloat16)
+    adj_lo = (adj - adj_hi.astype(jnp.float32)).astype(jnp.bfloat16)
+    b_adj = jnp.dot(b_ref[...], adj_hi, preferred_element_type=jnp.float32) + jnp.dot(
+        b_ref[...], adj_lo, preferred_element_type=jnp.float32)
+    for h in range(cr_ref.shape[0]):
+        lanes = slice(h * hd, (h + 1) * hd)
+        gv_ref[:, lanes] = (dx_ref[:, lanes] + ie_ref[:, h:h + 1] * b_adj[:, lanes]).astype(
+            gv_ref.dtype)
     parts[:n_rows, :] = part_b.astype(parts.dtype)
     parts[n_rows:, :] = part_c.astype(parts.dtype)
     rows = gather1.shape[1]
@@ -262,7 +273,7 @@
 
 
 def exclusive_scans(count, groups, decay_cols, forward, backward, x, dy, scores_t, cumulative,
-                    x_scaled, dy_scaled, b_inputs, c_inputs):
+                    into_end, from_start, b_inputs, c_inputs):
     s, w = forward.shape
     width = 8 if count % 8 == 0 else 1
     rows_n = count // width
@@ -278,17 +289,19 @@
     )
     length = scores_t.shape[0]
     chunk_rows = 2 * length // groups
-    out, dx, sums = pl.pallas_call(
+    grad_values, sums = pl.pallas_call(
         functools.partial(scan_kernel, rows_n, width, groups),
         out_shape=(
-            jax.ShapeDtypeStruct((width, 2 * piece, w), jnp.float32),
-            jax.ShapeDtypeStruct(x.shape, jnp.float32),
+            jax.ShapeDtypeStruct(x.shape, jnp.bfloat16),
             jax.ShapeDtypeStruct((groups, chunk_rows, s), jnp.bfloat16),
         ),
         in_specs=[pl.BlockSpec(memory_space=pltpu.VMEM)] * 10,
-        out_specs=(pl.BlockSpec(memory_space=pltpu.VMEM),) * 3,
+        out_specs=(pl.BlockSpec(memory_space=pltpu.VMEM),) * 2,
         scratch_shapes=[
             pltpu.VMEM((length, length), jnp.float32),
+            pltpu.VMEM(x.shape, jnp.float32),
+            pltpu.VMEM(x.shape, jnp.float32),
+            pltpu.VMEM(x.shape, jnp.float32),
             pltpu.VMEM((width, 2 * piece + 8, w), jnp.float32),
             pltpu.VMEM((2, 2 * rounds + 1, piece + 8, w), jnp.float32),
             pltpu.VMEM((width, 2 * piece, w), jnp.float32),
@@ -310,9 +323,9 @@
             pltpu.SemaphoreType.DMA((groups,)),
         ],
         compiler_params=pltpu.CompilerParams(collective_id=1, has_side_effects=True),
-    )(pack, x, dy, scores_t, cumulative, cumulative.T, x_scaled, dy_scaled, b_inputs, c_inputs)
+    )(pack, x, dy, scores_t, cumulative, cumulative.T, into_end.T, from_start.T, b_inputs, c_inputs)
     sums = sums.reshape(2 * length, s)
-    return out[:, :piece].reshape(s, w), out[:, piece:].reshape(s, w), dx, sums[:length], sums[length:]
+    return grad_values, sums[:length], sums[length:]
 
 
 def shards(count, groups, token_values, b_inputs, c_inputs, log_decay, grad_out):
@@ -341,15 +354,11 @@
     scores_t = lax.dot_general(
         b_inputs, c_inputs, (((1,), (1,)), ((), ())), preferred_element_type=jnp.float32
     )
-    to_end_cols = jnp.repeat(into_end.T, head_dim, axis=1)
-    from_start_cols = jnp.repeat(from_start.T, head_dim, axis=1)
-    state_in, adjoint_out, dx_local, grad_b, grad_c = exclusive_scans(
+    grad_values, grad_b, grad_c = exclusive_scans(
         count, groups, decay_cols, state_local, adjoint_local, token_values, grad_out, scores_t,
-        cumulative, token_values.astype(jnp.float32) * to_end_cols,
-        grad_out.astype(jnp.float32) * from_start_cols, b_inputs, c_inputs,
+        cumulative, into_end, from_start, b_inputs, c_inputs,
     )
-    grad_values = dx_local + to_end_cols * jnp.dot(b_float, adjoint_out, precision=PRECISE)
-    return grad_values.astype(jnp.bfloat16), grad_b, grad_c
+    return grad_values, grad_b, grad_c
 
 
 def solution(mesh):

time: 82.3 us -> 77.3 us (0.939)
  other arithmetic: 5.43 us -> 3.09 us
  matrix products: 3.55 us -> 2.32 us
  local copies, waits for them, and re-layouts: 7.17 us -> 6.24 us
    mul x1 -> x0, other arithmetic: 1.46 us -> none  [shards(): grad_out.astype(jnp.float32) * from_start_cols]
    dot_general x1 -> x0, matrix products: 1.25 us -> none  [shards(): jnp.dot(b_float, adjoint_out, precision=PRECISE)]
    slice x3 -> x2, local copies, waits for them, and re-layouts: 2.83 us -> 1.83 us  [the longest x1 1.68 us: exclusive_scans(): return (grad_values, sums[:length], sums[length:])]
    unnamed x16 -> x19, local copies, waits for them, and re-layouts: 1.58 us -> 2.49 us
    convert_element_type x1, other arithmetic: 0.91 us -> 0.02 us  [shards(): c_float = c_inputs.astype(jnp.float32)]
where the time goes in v8:
time: 77.3 us; the launch traced here: 77 us
  Pallas kernels  64.5 us (83%)
  local copies, waits for them, and re-layouts  6.24 us (8%)
  other arithmetic  3.09 us (4%)
  matrix products  2.32 us (3%)
  between operations  0.86 us (1%)
    pallas_call x1, Pallas kernels, exclusive_scans(): pl.pallas_call(functools.partial(scan_kernel, rows_n, width, groups), out...  64.5 us
    unnamed x19, local copies, waits for them, and re-layouts  2.49 us
    another operation x3, other arithmetic  2.11 us
    slice x1, local copies, waits for them, and re-layouts, exclusive_scans(): return (grad_values, sums[:length], sums[length:])  1.68 us

profile of v8, /device:TPU:1, one launch (start us, length us, event | category | flops | bytes accessed | tf_op | source)
XLA Modules:
  0.0 77.0 jit_solution(11350819803123058635)
XLA Ops:
  0.6 0.0 copy-start.5
  0.6 0.0 copy-start.6
  0.7 2.0 %reduce-window.6 = f32[8,3,128]{2,0,1:T(8,128)S(1)} reduce-window(f32[8,3,128]{2,0,1:T(8,128)} %bitcast.35, f32[]{:T(128)} %constant.3.clone.1), window={size=1x1x128 pad=0_0x0_0x127_0}, to_apply=%region_0.0 | reduce-window | flops 390144 | bytes 24580 | tf_op jit(solution)/shard_map/reduce-window
  2.6 0.2 slice_reduce_fusion
  2.8 0.1 broadcast_add_fusion
  2.9 0.1 copy.16
  3.1 0.0 copy-start
  3.1 0.1 broadcast_in_dim.6
  3.2 0.1 broadcast_in_dim.7
  3.2 0.7 copy.23.cr_ref
  4.0 0.0 copy-start.4
  4.0 0.1 subtract_exponential_fusion
  4.1 0.0 copy-done
  4.1 0.0 copy-start.1
  4.1 0.1 copy.17
  4.2 0.1 copy.20
  4.3 0.7 copy-done.4
  5.0 0.2 copy.18
  5.2 0.6 convolution_bitcast_fusion.1
  5.9 0.0 copy-start.3
  5.9 0.2 copy.19
  6.1 0.1 reshape_reshape.6
  6.3 0.6 copy-done.3
  6.9 0.2 copy.21
  7.1 0.6 convolution_bitcast_fusion
  7.7 0.2 copy.22
  7.9 0.1 reshape_reshape.7
  8.1 0.9 %pad_maximum_fusion.pack_ref = f32[8,40,512]{2,1,0:T(8,128)} fusion(f32[8,8,512]{2,1,0:T(8,128)S(1)} %broadcast_in_dim.16, f32[8,16,512]{2,1,0:T(8,128)S(1)} %reshape_reshape.7, f32[8,16,512]{2,1,0:T(8,128)S(1)} %reshape_reshape.6), kind=kLoop, calls=%fused_computation.8 | loop fusion | flops 327680 | bytes 1310720 | tf_op jit(solution)/shard_map/concatenate | solution.py:282
  9.0 1.1 %fusion.6.sc_ref = f32[384,384]{1,0:T(8,128)} fusion(bf16[384,128]{1,0:T(8,128)(2,1)S(1)} %copy-done.6, bf16[384,128]{1,0:T(8,128)(2,1)S(1)} %copy-done.5), kind=kOutput, calls=%fused_computation.16 | convolution fusion | flops 37748736 | bytes 786432 | tf_op jit(solution)/shard_map/dot_general | solution.py:354
  10.1 64.5 %shard_map.76 = (bf16[384,512]{1,0:T(8,128)(2,1)}, bf16[8,96,128]{2,1,0:T(8,128)(2,1)}) custom-call(f32[8,40,512]{2,1,0:T(8,128)} %pad_maximum_fusion.pack_ref, bf16[384,512]{1,0:T(8,128)(2,1)} %x_ref.1, bf16[384,512]{1,0:T(8,128)(2,1)} %dy_ref.1, f32[384,384]{1,0:T(8,128)} %fusion.6.sc_ref, f32[8,384]{1,0:T(8,128)} %copy.23.cr_ref, f32[384,8]{1,0:T(8,128)} %bitcast.28, ...), custom_call_target="tpu_custom_call" | custom-call | tf_op jit(solution)/shard_map/pallas_call | solution.py:292
  74.6 1.7 %fusion.5 = (bf16[4,96,128]{2,1,0:T(8,128)(2,1)}, bf16[4,96,128]{2,1,0:T(8,128)(2,1)}) fusion(bf16[8,96,128]{2,1,0:T(8,128)(2,1)} %get-tuple-element.6), kind=kLoop, calls=%fused_computation.15 | loop fusion | bytes 393216 | tf_op jit(solution)/shard_map/slice | solution.py:328
  76.3 0.7 copy.25
  (13 shorter events, 0.1 us)
Async XLA Ops:
  0.6 3.4 %copy-start.5 = (bf16[384,128]{1,0:T(8,128)(2,1)S(1)}, bf16[384,128]{1,0:T(8,128)(2,1)}, u32[]{:S(2)}) copy-start(bf16[384,128]{1,0:T(8,128)(2,1)} %c_ref.1) | copy-start | bytes 294916
  0.6 3.3 %copy-start.6 = (bf16[384,128]{1,0:T(8,128)(2,1)S(1)}, bf16[384,128]{1,0:T(8,128)(2,1)}, u32[]{:S(2)}) copy-start(bf16[384,128]{1,0:T(8,128)(2,1)} %b_ref.1) | copy-start | bytes 294916
  3.1 1.1 %copy-start = (f32[8,3,128]{0,2,1:T(8,128)}, f32[8,3,128]{0,2,1:T(8,128)S(1)}, u32[]{:S(2)}) copy-start(f32[8,3,128]{0,2,1:T(8,128)S(1)} %copy.16) | copy-start | bytes 36868
  4.0 1.0 %copy-start.4 = (bf16[384,512]{1,0:T(8,128)(2,1)S(1)}, bf16[384,512]{1,0:T(8,128)(2,1)}, u32[]{:S(2)}) copy-start(bf16[384,512]{1,0:T(8,128)(2,1)} %x_ref.1) | copy-start | bytes 1179652
  4.1 1.7 %copy-start.1 = (f32[8,384]{0,1:T(8,128)}, f32[8,384]{0,1:T(8,128)S(1)}, u32[]{:S(2)}) copy-start(f32[8,384]{0,1:T(8,128)S(1)} %get-tuple-element.9) | copy-start | bytes 36868
  4.1 1.7 %copy-start.2 = (f32[8,384]{0,1:T(8,128)}, f32[8,384]{0,1:T(8,128)S(1)}, u32[]{:S(2)}) copy-start(f32[8,384]{0,1:T(8,128)S(1)} %get-tuple-element.10) | copy-start | bytes 36868
  5.9 1.0 %copy-start.3 = (bf16[384,512]{1,0:T(8,128)(2,1)S(1)}, bf16[384,512]{1,0:T(8,128)(2,1)}, u32[]{:S(2)}) copy-start(bf16[384,512]{1,0:T(8,128)(2,1)} %dy_ref.1) | copy-start | bytes 1179652
  74.6 1.7 %copy-start.7 = (bf16[384,512]{1,0:T(8,128)(2,1)S(1)}, bf16[384,512]{1,0:T(8,128)(2,1)}, u32[]{:S(2)}) copy-start(bf16[384,512]{1,0:T(8,128)(2,1)} %get-tuple-element.14) | copy-start | bytes 1179652

commit v9 on v8

--- a/solution.py
+++ b/solution.py
@@ -220,6 +220,21 @@
         weighted, b_ref[...], (((0,), (0,)), ((), ())), preferred_element_type=jnp.float32
     ) + nt_dot_f32(ds_ref[...], full[0])
     n_rows = part_b.shape[0]
+    parts[:n_rows, :] = part_b.astype(parts.dtype)
+    parts[n_rows:, :] = part_c.astype(parts.dtype)
+    rows = gather1.shape[1]
+
+    def chunk(i):
+        return parts.at[pl.ds(pl.multiple_of(i * rows, rows), rows)]
+
+    sends = []
+    for k in range(1, groups):
+        peer = (z + k) % groups
+        cp = pltpu.make_async_remote_copy(
+            src_ref=chunk(peer), dst_ref=gather1.at[z], send_sem=hsend1.at[k],
+            recv_sem=hrecv1.at[k], device_id=(me, peer), device_id_type=MESH)
+        cp.start()
+        sends.append(cp)
     adj = full[1]
     adj_hi = adj.astype(jnp.bfloat16)
     adj_lo = (adj - adj_hi.astype(jnp.float32)).astype(jnp.bfloat16)
@@ -229,21 +244,6 @@
         lanes = slice(h * hd, (h + 1) * hd)
         gv_ref[:, lanes] = (dx_ref[:, lanes] + ie_ref[:, h:h + 1] * b_adj[:, lanes]).astype(
             gv_ref.dtype)
-    parts[:n_rows, :] = part_b.astype(parts.dtype)
-    parts[n_rows:, :] = part_c.astype(parts.dtype)
-    rows = gather1.shape[1]
-
-    def chunk(i):
-        return parts.at[pl.ds(pl.multiple_of(i * rows, rows), rows)]
-
-    sends = []
-    for k in range(1, groups):
-        peer = (z + k) % groups
-        cp = pltpu.make_async_remote_copy(
-            src_ref=chunk(peer), dst_ref=gather1.at[z], send_sem=hsend1.at[k],
-            recv_sem=hrecv1.at[k], device_id=(me, peer), device_id_type=MESH)
-        cp.start()
-        sends.append(cp)
     total = parts[pl.ds(pl.multiple_of(z * rows, rows), rows), :].astype(jnp.float32)
     for k in range(1, groups):
         source = (z + groups - k) % groups
@@ -333,7 +333,9 @@
     heads_here = log_decay.shape[0]
     head_dim = token_values.shape[1] // heads_here
     state_size = b_inputs.shape[1]
-    cumulative = jnp.cumsum(log_decay, axis=1)
+    positions = lax.iota(jnp.int32, length)
+    upto = (positions[:, None] <= positions[None, :]).astype(jnp.float32)
+    cumulative = jnp.dot(log_decay, upto, precision=PRECISE)
     block_log = cumulative[:, -1]
     into_end = jnp.exp(block_log[:, None] - cumulative)
     from_start = jnp.exp(cumulative)

time: 77.3 us -> 75.8 us (0.981)
  other arithmetic: 3.09 us -> 1.72 us
    another operation x3 -> x0, other arithmetic: 2.11 us -> none
    another operation x2 -> x0, local copies, waits for them, and re-layouts: 0.83 us -> none
where the time goes in v9:
time: 75.8 us; the launch traced here: 75.5 us
  Pallas kernels  64.3 us (85%)
  local copies, waits for them, and re-layouts  6.22 us (8%)
  matrix products  2.52 us (3%)
  other arithmetic  1.72 us (2%)
  between operations  0.83 us (1%)
    pallas_call x1, Pallas kernels, exclusive_scans(): pl.pallas_call(functools.partial(scan_kernel, rows_n, width, groups), out...  64.3 us
    unnamed x19, local copies, waits for them, and re-layouts  2.51 us
    slice x1, local copies, waits for them, and re-layouts, exclusive_scans(): return (grad_values, sums[:length], sums[length:])  1.68 us

profile of v9, /device:TPU:1, one launch (start us, length us, event | category | flops | bytes accessed | tf_op | source)
XLA Modules:
  0.0 75.5 jit_solution(2679211917195043561)
XLA Ops:
  0.6 0.0 copy-start
  0.6 0.0 copy-start.5
  0.7 0.7 copy-done
  1.3 0.2 fusion.6
  1.6 0.0 copy-start.7
  1.6 0.0 copy-start.4
  1.6 0.2 slice_reduce_fusion
  1.8 0.1 broadcast_in_dim.6
  1.9 0.1 broadcast_in_dim.7
  1.9 0.1 subtract_exponential_fusion.1
  2.0 0.0 copy-start.3
  2.0 0.8 %copy.29.fs_ref = f32[384,8]{1,0:T(8,128)} copy(f32[384,8]{0,1:T(8,128)S(1)} %get-tuple-element.11) | data formatting | bytes 24576 | tf_op jit(solution)/shard_map/exp | solution.py:341
  2.9 0.1 copy.28.cc_ref
  3.0 0.0 copy-start.1
  3.0 0.7 subtract_exponential_fusion.ie_ref
  3.7 0.0 copy-done.5
  3.7 0.0 copy-done.4
  3.8 0.2 copy.22
  4.0 0.6 convolution_bitcast_fusion.1
  4.7 0.0 copy-start.2
  4.7 0.2 copy.23
  4.9 0.1 reshape_reshape.6
  5.1 0.6 copy-done.2
  5.6 0.2 copy.24
  5.9 0.6 convolution_bitcast_fusion
  6.5 0.2 copy.25
  6.7 0.1 reshape_reshape.7
  6.9 0.9 %pad_maximum_fusion.pack_ref = f32[8,40,512]{2,1,0:T(8,128)} fusion(f32[8,8,512]{2,1,0:T(8,128)S(1)} %broadcast_in_dim.8, f32[8,16,512]{2,1,0:T(8,128)S(1)} %reshape_reshape.7, f32[8,16,512]{2,1,0:T(8,128)S(1)} %reshape_reshape.6), kind=kLoop, calls=%fused_computation.8 | loop fusion | flops 327680 | bytes 1310720 | tf_op jit(solution)/shard_map/concatenate | solution.py:282
  7.8 1.1 %fusion.7.sc_ref = f32[384,384]{1,0:T(8,128)} fusion(bf16[384,128]{1,0:T(8,128)(2,1)S(1)} %copy-done.5, bf16[384,128]{1,0:T(8,128)(2,1)S(1)} %copy-done.4), kind=kOutput, calls=%fused_computation.17 | convolution fusion | flops 37748736 | bytes 786432 | tf_op jit(solution)/shard_map/dot_general | solution.py:356
  8.9 64.3 %shard_map.76 = (bf16[384,512]{1,0:T(8,128)(2,1)}, bf16[8,96,128]{2,1,0:T(8,128)(2,1)}) custom-call(f32[8,40,512]{2,1,0:T(8,128)} %pad_maximum_fusion.pack_ref, bf16[384,512]{1,0:T(8,128)(2,1)} %x_ref.1, bf16[384,512]{1,0:T(8,128)(2,1)} %dy_ref.1, f32[384,384]{1,0:T(8,128)} %fusion.7.sc_ref, f32[8,384]{1,0:T(8,128)} %bitcast.19, f32[384,8]{1,0:T(8,128)} %copy-done.1, ...), custom_call_target="tpu_custom_call" | custom-call | tf_op jit(solution)/shard_map/pallas_call | solution.py:292
  73.1 1.7 %fusion.5 = (bf16[4,96,128]{2,1,0:T(8,128)(2,1)}, bf16[4,96,128]{2,1,0:T(8,128)(2,1)}) fusion(bf16[8,96,128]{2,1,0:T(8,128)(2,1)} %get-tuple-element.6), kind=kLoop, calls=%fused_computation.15 | loop fusion | bytes 393216 | tf_op jit(solution)/shard_map/slice | solution.py:328
  74.8 0.7 copy.32
  (9 shorter events, 0.1 us)
Async XLA Ops:
  0.6 0.7 copy-start
  0.6 3.1 %copy-start.5 = (bf16[384,128]{1,0:T(8,128)(2,1)S(1)}, bf16[384,128]{1,0:T(8,128)(2,1)}, u32[]{:S(2)}) copy-start(bf16[384,128]{1,0:T(8,128)(2,1)} %b_ref.1) | copy-start | bytes 294916
  1.6 2.2 %copy-start.7 = (f32[384,8]{0,1:T(8,128)}, f32[384,8]{0,1:T(8,128)S(1)}, u32[]{:S(2)}) copy-start(f32[384,8]{0,1:T(8,128)S(1)} %get-tuple-element.12) | copy-start | bytes 36868
  1.6 2.2 %copy-start.4 = (bf16[384,128]{1,0:T(8,128)(2,1)S(1)}, bf16[384,128]{1,0:T(8,128)(2,1)}, u32[]{:S(2)}) copy-start(bf16[384,128]{1,0:T(8,128)(2,1)} %c_ref.1) | copy-start | bytes 294916
  2.0 1.8 %copy-start.3 = (bf16[384,512]{1,0:T(8,128)(2,1)S(1)}, bf16[384,512]{1,0:T(8,128)(2,1)}, u32[]{:S(2)}) copy-start(bf16[384,512]{1,0:T(8,128)(2,1)} %x_ref.1) | copy-start | bytes 1179652
  3.0 1.0 %copy-start.1 = (f32[384,8]{1,0:T(8,128)}, f32[384,8]{1,0:T(8,128)S(1)}, u32[]{:S(2)}) copy-start(f32[384,8]{1,0:T(8,128)S(1)} %copy.28.cc_ref) | copy-start | bytes 36868
  4.7 1.0 %copy-start.2 = (bf16[384,512]{1,0:T(8,128)(2,1)S(1)}, bf16[384,512]{1,0:T(8,128)(2,1)}, u32[]{:S(2)}) copy-start(bf16[384,512]{1,0:T(8,128)(2,1)} %dy_ref.1) | copy-start | bytes 1179652
  73.1 1.7 %copy-start.6 = (bf16[384,512]{1,0:T(8,128)(2,1)S(1)}, bf16[384,512]{1,0:T(8,128)(2,1)}, u32[]{:S(2)}) copy-start(bf16[384,512]{1,0:T(8,128)(2,1)} %get-tuple-element.16) | copy-start | bytes 1179652

commit v10 on v9

--- a/solution.py
+++ b/solution.py
@@ -31,15 +31,15 @@
     return nt_dot(ph, qh) + (nt_dot(ph, ql) + nt_dot(pl_, qh))
 
 
-def scan_kernel(rows_n, width, groups, pack_ref, x_ref, dy_ref, sc_ref, cr_ref, cc_ref, ie_ref,
-                fs_ref, b_ref, c_ref, gv_ref, sum_ref, run_ref, dx_ref, xs_ref, ds_ref, recv1, win,
-                out3, recv3, full, parts, gather1, gather2, send1, rsem1, send2, rsem2, send3, rsem3, local,
-                hsend1, hrecv1, hsend2, hrecv2):
+def scan_kernel(rows_n, width, groups, pack_ref, pdec_ref, x_ref, dy_ref, sc_ref, cr_ref, cc_ref, ie_ref,
+                fs_ref, b_ref, c_ref, gv_ref, sum_ref, run_ref, dx_ref, xs_ref, ds_ref, recv1, rdec,
+                win, out3, recv3, full, parts, gather1, gather2, send1, rsem1, send2, rsem2, send3, rsem3,
+                local, dsend, drecv, hsend1, hrecv1, hsend2, hrecv2):
     me = lax.axis_index("seq")
     col = lax.axis_index("head")
     c = me % width
     y = me // width
-    piece = (recv1.shape[1] - 8) // 2
+    piece = recv1.shape[1] // 2
     steps = scan_steps(rows_n)
     spans = sorted(set(steps))
 
@@ -94,6 +94,8 @@
 
     own = pltpu.make_async_copy(pack_ref.at[c], recv1.at[c], local.at[0])
     own.start()
+    own_dec = pltpu.make_async_copy(pdec_ref, rdec.at[c], local.at[2])
+    own_dec.start()
     sends = []
     for off in range(1, width):
         k = (c + off) % width
@@ -102,18 +104,27 @@
             recv_sem=rsem1.at[off], device_id=(y * width + k, col), device_id_type=MESH)
         cp.start()
         sends.append(cp)
+        cp = pltpu.make_async_remote_copy(
+            src_ref=pdec_ref, dst_ref=rdec.at[c], send_sem=dsend.at[off],
+            recv_sem=drecv.at[off], device_id=(y * width + k, col), device_id_type=MESH)
+        cp.start()
+        sends.append(cp)
     heads(3)
     for off in range(1, width):
         k = (c + width - off) % width
         pltpu.make_async_remote_copy(
             src_ref=pack_ref.at[k], dst_ref=recv1.at[k], send_sem=send1.at[off],
             recv_sem=rsem1.at[off], device_id=(y * width + k, col), device_id_type=MESH).wait_recv()
+        pltpu.make_async_remote_copy(
+            src_ref=pdec_ref, dst_ref=rdec.at[k], send_sem=dsend.at[off],
+            recv_sem=drecv.at[off], device_id=(y * width + k, col), device_id_type=MESH).wait_recv()
     own.wait()
+    own_dec.wait()
     for cp in sends:
         cp.wait_send()
 
     def decay(i):
-        return recv1[i, 2 * piece:2 * piece + 1, :]
+        return rdec[i, 0:1, :]
 
     fwd_e, fwd_g = [None] * width, [None] * width
     e = jnp.zeros((piece, recv1.shape[2]), jnp.float32)
@@ -121,7 +132,7 @@
     for i in range(width):
         fwd_e[i], fwd_g[i] = e, g
         a = decay(i)
-        e = a * e + recv1[i, :piece, :]
+        e = a * e + recv1[i, :piece, :].astype(jnp.float32)
         g = g * a
     bwd_e, bwd_g = [None] * width, [None] * width
     f = jnp.zeros((piece, recv1.shape[2]), jnp.float32)
@@ -129,7 +140,7 @@
     for i in reversed(range(width)):
         bwd_e[i], bwd_g[i] = f, h
         a = decay(i)
-        f = a * f + recv1[i, piece:2 * piece, :]
+        f = a * f + recv1[i, piece:2 * piece, :].astype(jnp.float32)
         h = h * a
     win[0, 0, :piece, :] = e
     win[0, 0, piece:, :] = jnp.broadcast_to(g, (win.shape[2] - piece, g.shape[1]))
@@ -188,8 +199,8 @@
     leaving = win[1, last, :piece, :]
 
     for i in range(width):
-        out3[i, :piece, :] = fwd_e[i] + fwd_g[i] * entering
-        out3[i, piece:, :] = bwd_e[i] + bwd_g[i] * leaving
+        out3[i, :piece, :] = (fwd_e[i] + fwd_g[i] * entering).astype(out3.dtype)
+        out3[i, piece:, :] = (bwd_e[i] + bwd_g[i] * leaving).astype(out3.dtype)
     own = pltpu.make_async_copy(out3.at[c], recv3.at[c], local.at[1])
     own.start()
     sends = []
@@ -211,8 +222,8 @@
 
     s = width * piece
     for k in range(width):
-        full[0, k * piece:(k + 1) * piece, :] = recv3[k, :piece, :]
-        full[1, k * piece:(k + 1) * piece, :] = recv3[k, piece:, :]
+        full[0, k * piece:(k + 1) * piece, :] = recv3[k, :piece, :].astype(jnp.float32)
+        full[1, k * piece:(k + 1) * piece, :] = recv3[k, piece:, :].astype(jnp.float32)
     weighted = run_ref[...].astype(jnp.bfloat16)
     part_b = jnp.dot(weighted, c_ref[...], preferred_element_type=jnp.float32) + nt_dot_f32(
         xs_ref[...], full[1])
@@ -280,13 +291,9 @@
     piece = s // width
     rounds = len(scan_steps(rows_n))
     pack = jnp.concatenate(
-        [
-            forward.reshape(width, piece, w),
-            backward.reshape(width, piece, w),
-            jnp.broadcast_to(decay_cols[None], (width, 8, w)),
-        ],
-        axis=1,
-    )
+        [forward.reshape(width, piece, w), backward.reshape(width, piece, w)], axis=1
+    ).astype(jnp.bfloat16)
+    decay_rows = jnp.broadcast_to(decay_cols, (8, w))
     length = scores_t.shape[0]
     chunk_rows = 2 * length // groups
     grad_values, sums = pl.pallas_call(
@@ -295,17 +302,18 @@
             jax.ShapeDtypeStruct(x.shape, jnp.bfloat16),
             jax.ShapeDtypeStruct((groups, chunk_rows, s), jnp.bfloat16),
         ),
-        in_specs=[pl.BlockSpec(memory_space=pltpu.VMEM)] * 10,
+        in_specs=[pl.BlockSpec(memory_space=pltpu.VMEM)] * 11,
         out_specs=(pl.BlockSpec(memory_space=pltpu.VMEM),) * 2,
         scratch_shapes=[
             pltpu.VMEM((length, length), jnp.float32),
             pltpu.VMEM(x.shape, jnp.float32),
             pltpu.VMEM(x.shape, jnp.float32),
             pltpu.VMEM(x.shape, jnp.float32),
-            pltpu.VMEM((width, 2 * piece + 8, w), jnp.float32),
+            pltpu.VMEM((width, 2 * piece, w), jnp.bfloat16),
+            pltpu.VMEM((width, 8, w), jnp.float32),
             pltpu.VMEM((2, 2 * rounds + 1, piece + 8, w), jnp.float32),
-            pltpu.VMEM((width, 2 * piece, w), jnp.float32),
-            pltpu.VMEM((width, 2 * piece, w), jnp.float32),
+            pltpu.VMEM((width, 2 * piece, w), jnp.bfloat16),
+            pltpu.VMEM((width, 2 * piece, w), jnp.bfloat16),
             pltpu.VMEM((2, s, w), jnp.float32),
             pltpu.VMEM((2 * length, s), jnp.bfloat16),
             pltpu.VMEM((groups, chunk_rows, s), jnp.bfloat16),
@@ -316,14 +324,16 @@
             pltpu.SemaphoreType.DMA((2, rounds)),
             pltpu.SemaphoreType.DMA((width,)),
             pltpu.SemaphoreType.DMA((width,)),
-            pltpu.SemaphoreType.DMA((2,)),
+            pltpu.SemaphoreType.DMA((3,)),
+            pltpu.SemaphoreType.DMA((width,)),
+            pltpu.SemaphoreType.DMA((width,)),
             pltpu.SemaphoreType.DMA((groups,)),
             pltpu.SemaphoreType.DMA((groups,)),
             pltpu.SemaphoreType.DMA((groups,)),
             pltpu.SemaphoreType.DMA((groups,)),
         ],
         compiler_params=pltpu.CompilerParams(collective_id=1, has_side_effects=True),
-    )(pack, x, dy, scores_t, cumulative, cumulative.T, into_end.T, from_start.T, b_inputs, c_inputs)
+    )(pack, decay_rows, x, dy, scores_t, cumulative, cumulative.T, into_end.T, from_start.T, b_inputs, c_inputs)
     sums = sums.reshape(2 * length, s)
     return grad_values, sums[:length], sums[length:]
 

time: 75.8 us -> 71.4 us (0.942)
  the two profiles are of different devices: /device:TPU:1 before, /device:TPU:64 now
where the time goes in v10:
time: 71.4 us; the launch traced here: 71.2 us
  Pallas kernels  59.4 us (83%)
  local copies, waits for them, and re-layouts  6.87 us (10%)
  matrix products  2.53 us (4%)
  other arithmetic  1.58 us (2%)
  between operations  0.79 us (1%)
    pallas_call x1, Pallas kernels, exclusive_scans(): pl.pallas_call(functools.partial(scan_kernel, rows_n, width, groups), out...  59.4 us
    unnamed x19, local copies, waits for them, and re-layouts  2.51 us
    slice x1, local copies, waits for them, and re-layouts, exclusive_scans(): return (grad_values, sums[:length], sums[length:])  1.68 us

profile of v10, /device:TPU:64, one launch (start us, length us, event | category | flops | bytes accessed | tf_op | source)
XLA Modules:
  0.0 71.2 jit_solution(4401699296578575114)
XLA Ops:
  0.6 0.0 copy-start
  0.6 0.0 copy-start.5
  0.7 0.7 copy-done
  1.3 0.2 fusion.8
  1.6 0.0 copy-start.7
  1.6 0.2 slice_reduce_fusion
  1.8 0.1 broadcast_in_dim.6
  1.9 0.1 broadcast_in_dim.7
  1.9 0.6 broadcast_in_dim.8.pdec_ref
  2.5 0.1 subtract_exponential_fusion.1
  2.6 0.8 %copy.29.fs_ref = f32[384,8]{1,0:T(8,128)} copy(f32[384,8]{0,1:T(8,128)S(1)} %get-tuple-element.11) | data formatting | bytes 24576 | tf_op jit(solution)/shard_map/exp | solution.py:351
  3.4 0.1 copy.28.cc_ref
  3.6 0.0 copy-start.1
  3.6 0.8 %subtract_exponential_fusion.ie_ref = f32[384,8]{1,0:T(8,128)} fusion(f32[384,8]{1,0:T(8,128)S(1)} %copy.28.cc_ref, f32[8]{0:T(128)S(1)} %slice_reduce_fusion), kind=kLoop, calls=%fused_computation.13 | loop fusion | flops 3072 | bytes 24608 | tf_op jit(solution)/shard_map/exp | solution.py:350
  4.3 0.0 copy-done.5
  4.3 0.0 copy-done.7
  4.4 0.0 copy-done.3
  4.4 0.2 copy.22
  4.7 0.6 fusion
  5.3 0.0 copy-start.2
  5.3 0.2 copy.23
  5.5 0.2 reshape_reshape.8
  5.7 0.6 copy-done.2
  6.3 0.2 copy.24
  6.5 0.6 fusion.1
  7.1 0.2 copy.25
  7.3 0.2 reshape_reshape.9
  7.5 0.7 %pad_maximum_fusion.pack_ref = bf16[8,32,512]{2,1,0:T(8,128)(2,1)} fusion(bf16[8,16,512]{2,1,0:T(8,128)(2,1)S(1)} %reshape_reshape.9, bf16[8,16,512]{2,1,0:T(8,128)(2,1)S(1)} %reshape_reshape.8), kind=kLoop, calls=%fused_computation.12 | loop fusion | flops 524288 | bytes 524288 | tf_op jit(solution)/shard_map/concatenate | solution.py:293
  8.3 1.1 %fusion.9.sc_ref = f32[384,384]{1,0:T(8,128)} fusion(bf16[384,128]{1,0:T(8,128)(2,1)S(1)} %copy-done.5, bf16[384,128]{1,0:T(8,128)(2,1)S(1)} %copy-done.4), kind=kOutput, calls=%fused_computation.19 | convolution fusion | flops 37748736 | bytes 786432 | tf_op jit(solution)/shard_map/dot_general | solution.py:366
  9.3 59.4 %shard_map.76 = (bf16[384,512]{1,0:T(8,128)(2,1)}, bf16[8,96,128]{2,1,0:T(8,128)(2,1)}) custom-call(bf16[8,32,512]{2,1,0:T(8,128)(2,1)} %pad_maximum_fusion.pack_ref, f32[8,512]{1,0:T(8,128)} %broadcast_in_dim.8.pdec_ref, bf16[384,512]{1,0:T(8,128)(2,1)} %x_ref.1, bf16[384,512]{1,0:T(8,128)(2,1)} %dy_ref.1, f32[384,384]{1,0:T(8,128)} %fusion.9.sc_ref, ...), custom_call_target="tpu_custom_call" | custom-call | tf_op jit(solution)/shard_map/pallas_call | solution.py:299
  68.7 1.7 %fusion.7 = (bf16[4,96,128]{2,1,0:T(8,128)(2,1)}, bf16[4,96,128]{2,1,0:T(8,128)(2,1)}) fusion(bf16[8,96,128]{2,1,0:T(8,128)(2,1)} %get-tuple-element.6), kind=kLoop, calls=%fused_computation.17 | loop fusion | bytes 393216 | tf_op jit(solution)/shard_map/slice | solution.py:338
  70.4 0.7 %copy.32 = bf16[384,512]{1,0:T(8,128)(2,1)} copy(bf16[384,512]{1,0:T(8,128)(2,1)S(1)} %copy-done.6) | data formatting | bytes 786432
  (9 shorter events, 0.0 us)
Async XLA Ops:
  0.6 0.7 %copy-start = (f32[8,384]{1,0:T(8,128)S(1)}, f32[8,384]{1,0:T(8,128)}, u32[]{:S(2)}) copy-start(f32[8,384]{1,0:T(8,128)} %param.8) | copy-start | bytes 36868
  0.6 3.7 %copy-start.5 = (bf16[384,128]{1,0:T(8,128)(2,1)S(1)}, bf16[384,128]{1,0:T(8,128)(2,1)}, u32[]{:S(2)}) copy-start(bf16[384,128]{1,0:T(8,128)(2,1)} %b_ref.1) | copy-start | bytes 294916
  1.6 2.8 %copy-start.7 = (f32[384,8]{0,1:T(8,128)}, f32[384,8]{0,1:T(8,128)S(1)}, u32[]{:S(2)}) copy-start(f32[384,8]{0,1:T(8,128)S(1)} %get-tuple-element.12) | copy-start | bytes 36868
  1.8 2.6 %copy-start.4 = (bf16[384,128]{1,0:T(8,128)(2,1)S(1)}, bf16[384,128]{1,0:T(8,128)(2,1)}, u32[]{:S(2)}) copy-start(bf16[384,128]{1,0:T(8,128)(2,1)} %c_ref.1) | copy-start | bytes 294916
  3.4 1.0 %copy-start.3 = (bf16[384,512]{1,0:T(8,128)(2,1)S(1)}, bf16[384,512]{1,0:T(8,128)(2,1)}, u32[]{:S(2)}) copy-start(bf16[384,512]{1,0:T(8,128)(2,1)} %x_ref.1) | copy-start | bytes 1179652
  3.6 1.1 %copy-start.1 = (f32[384,8]{1,0:T(8,128)}, f32[384,8]{1,0:T(8,128)S(1)}, u32[]{:S(2)}) copy-start(f32[384,8]{1,0:T(8,128)S(1)} %copy.28.cc_ref) | copy-start | bytes 36868
  5.3 1.0 %copy-start.2 = (bf16[384,512]{1,0:T(8,128)(2,1)S(1)}, bf16[384,512]{1,0:T(8,128)(2,1)}, u32[]{:S(2)}) copy-start(bf16[384,512]{1,0:T(8,128)(2,1)} %dy_ref.1) | copy-start | bytes 1179652
  68.7 1.7 %copy-start.6 = (bf16[384,512]{1,0:T(8,128)(2,1)S(1)}, bf16[384,512]{1,0:T(8,128)(2,1)}, u32[]{:S(2)}) copy-start(bf16[384,512]{1,0:T(8,128)(2,1)} %get-tuple-element.16) | copy-start | bytes 1179652

commit v11 on v10

--- a/solution.py
+++ b/solution.py
@@ -9,14 +9,6 @@
 
 PRECISE = lax.Precision.HIGHEST
 MESH = pl.DeviceIdType.MESH
-
-
-def scan_steps(n):
-    steps, d = [1], 1
-    while d < n:
-        steps.append(d)
-        d *= 2
-    return steps
 
 
 def nt_dot(p, q):
@@ -40,8 +32,7 @@
     c = me % width
     y = me // width
     piece = recv1.shape[1] // 2
-    steps = scan_steps(rows_n)
-    spans = sorted(set(steps))
+    spans = [1, 2, 3, 4]
 
     length = sc_ref.shape[0]
     later = lax.broadcasted_iota(jnp.int32, (length, length), 1) >= lax.broadcasted_iota(
@@ -147,56 +138,67 @@
     win[1, 0, :piece, :] = f
     win[1, 0, piece:, :] = jnp.broadcast_to(h, (win.shape[2] - piece, h.shape[1]))
 
-    def copy2(way, r, target):
-        src = win.at[way, 0] if r == 0 else win.at[way, r]
+    def combine(w_near, w_far):
+        a = w_near[piece:, :]
+        return w_near[:piece, :] + jnp.broadcast_to(a[:1], (piece, a.shape[1])) * w_far[:piece, :], a * w_far[piece:, :]
+
+    def copy2(way, slot, src_slot, target, sem):
         return pltpu.make_async_remote_copy(
-            src_ref=src, dst_ref=win.at[way, len(steps) + 1 + r],
-            send_sem=send2.at[way, r], recv_sem=rsem2.at[way, r],
-            device_id=(target, col), device_id_type=MESH)
-
-    base = len(steps) + 1
-    for r, d in enumerate(steps):
-        for way, sign in ((0, 1), (1, -1)):
-            target_row = y + sign * d
-
-            @pl.when(jnp.logical_and(target_row >= 0, target_row < rows_n))
+            src_ref=win.at[way, src_slot], dst_ref=win.at[way, slot], send_sem=send2.at[way, sem],
+            recv_sem=rsem2.at[way, sem], device_id=(target, col), device_id_type=MESH)
+
+    def exists(row):
+        return jnp.logical_and(row >= 0, row < rows_n)
+
+    near = [1, 2, 3]
+    for way, sign in ((0, 1), (1, -1)):
+        for k in near:
+            @pl.when(exists(y + sign * k))
             def _():
-                copy2(way, r, me + sign * d * width).start()
-        heads(1 if r < len(steps) - 1 else len(heads_left))
-        for way, sign in ((0, 1), (1, -1)):
-            source_row = y - sign * d
-            got = jnp.logical_and(source_row >= 0, source_row < rows_n)
-            cur = 0 if r == 0 else r
-            nxt = r + 1
-
-            @pl.when(got)
+                copy2(way, k, 0, me + sign * k * width, k - 1).start()
+    heads(2)
+    for way, sign in ((0, 1), (1, -1)):
+        win[way, 4] = jnp.zeros(win.shape[2:], win.dtype)
+        for k in near:
+            @pl.when(exists(y - sign * k))
             def _():
-                copy2(way, r, me - sign * d * width).wait_recv()
-                arrived = win[way, base + r]
-                if r == 0:
-                    win[way, nxt] = arrived
+                copy2(way, k, 0, me - sign * k * width, k - 1).wait_recv()
+                s_new, a_new = combine(win[way, 4], win[way, k])
+                if k == 1:
+                    win[way, 4] = win[way, 1]
                 else:
-                    a = win[way, cur, piece:, :]
-                    win[way, nxt, :piece, :] = win[way, cur, :piece, :] + jnp.broadcast_to(
-                        a[:1], (piece, a.shape[1])) * arrived[:piece]
-                    win[way, nxt, piece:, :] = a * arrived[piece:]
-
-            @pl.when(jnp.logical_not(got))
+                    win[way, 4, :piece, :] = s_new
+                    win[way, 4, piece:, :] = a_new
+        s_inc, a_inc = combine(win[way, 0], win[way, 4])
+        win[way, 5, :piece, :] = s_inc
+        win[way, 5, piece:, :] = a_inc
+
+        @pl.when(exists(y + sign * 4))
+        def _():
+            copy2(way, 6, 5, me + sign * 4 * width, 3).start()
+    heads(len(heads_left))
+    for way, sign in ((0, 1), (1, -1)):
+        @pl.when(exists(y - sign * 4))
+        def _():
+            copy2(way, 6, 5, me - sign * 4 * width, 3).wait_recv()
+            s_new, a_new = combine(win[way, 4], win[way, 6])
+            win[way, 7, :piece, :] = s_new
+            win[way, 7, piece:, :] = a_new
+
+        @pl.when(jnp.logical_not(exists(y - sign * 4)))
+        def _():
+            win[way, 7] = win[way, 4]
+    for way, sign in ((0, 1), (1, -1)):
+        for k in near:
+            @pl.when(exists(y + sign * k))
             def _():
-                if r == 0:
-                    win[way, nxt] = jnp.zeros(win.shape[2:], win.dtype)
-                else:
-                    win[way, nxt] = win[way, cur]
-    for r, d in enumerate(steps):
-        for way, sign in ((0, 1), (1, -1)):
-            target_row = y + sign * d
-
-            @pl.when(jnp.logical_and(target_row >= 0, target_row < rows_n))
-            def _():
-                copy2(way, r, me + sign * d * width).wait_send()
-    last = len(steps)
-    entering = win[0, last, :piece, :]
-    leaving = win[1, last, :piece, :]
+                copy2(way, k, 0, me + sign * k * width, k - 1).wait_send()
+
+        @pl.when(exists(y + sign * 4))
+        def _():
+            copy2(way, 6, 5, me + sign * 4 * width, 3).wait_send()
+    entering = win[0, 7, :piece, :]
+    leaving = win[1, 7, :piece, :]
 
     for i in range(width):
         out3[i, :piece, :] = (fwd_e[i] + fwd_g[i] * entering).astype(out3.dtype)
@@ -289,7 +291,7 @@
     width = 8 if count % 8 == 0 else 1
     rows_n = count // width
     piece = s // width
-    rounds = len(scan_steps(rows_n))
+    assert rows_n <= 8
     pack = jnp.concatenate(
         [forward.reshape(width, piece, w), backward.reshape(width, piece, w)], axis=1
     ).astype(jnp.bfloat16)
@@ -311,7 +313,7 @@
             pltpu.VMEM(x.shape, jnp.float32),
             pltpu.VMEM((width, 2 * piece, w), jnp.bfloat16),
             pltpu.VMEM((width, 8, w), jnp.float32),
-            pltpu.VMEM((2, 2 * rounds + 1, piece + 8, w), jnp.float32),
+            pltpu.VMEM((2, 8, piece + 8, w), jnp.float32),
             pltpu.VMEM((width, 2 * piece, w), jnp.bfloat16),
             pltpu.VMEM((width, 2 * piece, w), jnp.bfloat16),
             pltpu.VMEM((2, s, w), jnp.float32),
@@ -320,8 +322,8 @@
             pltpu.VMEM((groups, chunk_rows, s), jnp.bfloat16),
             pltpu.SemaphoreType.DMA((width,)),
             pltpu.SemaphoreType.DMA((width,)),
-            pltpu.SemaphoreType.DMA((2, rounds)),
-            pltpu.SemaphoreType.DMA((2, rounds)),
+            pltpu.SemaphoreType.DMA((2, 4)),
+            pltpu.SemaphoreType.DMA((2, 4)),
             pltpu.SemaphoreType.DMA((width,)),
             pltpu.SemaphoreType.DMA((width,)),
             pltpu.SemaphoreType.DMA((3,)),

time: 71.4 us -> 70.5 us (0.987)
  the two profiles are of different devices: /device:TPU:64 before, /device:TPU:16 now
where the time goes in v11:
time: 70.5 us; the launch traced here: 70.2 us
  Pallas kernels  58.5 us (83%)
  local copies, waits for them, and re-layouts  6.87 us (10%)
  matrix products  2.53 us (4%)
  other arithmetic  1.58 us (2%)
  between operations  0.79 us (1%)
    pallas_call x1, Pallas kernels, exclusive_scans(): pl.pallas_call(functools.partial(scan_kernel, rows_n, width, groups), out...  58.5 us
    unnamed x19, local copies, waits for them, and re-layouts  2.51 us
    slice x1, local copies, waits for them, and re-layouts, exclusive_scans(): return (grad_values, sums[:length], sums[length:])  1.68 us

profile of v11, /device:TPU:16, one launch (start us, length us, event | category | flops | bytes accessed | tf_op | source)
XLA Modules:
  0.0 70.2 jit_solution(11892012220838849703)
XLA Ops:
  0.6 0.0 copy-start
  0.6 0.0 copy-start.5
  0.7 0.7 copy-done
  1.3 0.2 fusion.8
  1.6 0.0 copy-start.7
  1.6 0.2 slice_reduce_fusion
  1.8 0.1 broadcast_in_dim.6
  1.9 0.1 broadcast_in_dim.7
  1.9 0.6 broadcast_in_dim.8.pdec_ref
  2.5 0.1 subtract_exponential_fusion.1
  2.6 0.8 %copy.29.fs_ref = f32[384,8]{1,0:T(8,128)} copy(f32[384,8]{0,1:T(8,128)S(1)} %get-tuple-element.11) | data formatting | bytes 24576 | tf_op jit(solution)/shard_map/exp | solution.py:353
  3.4 0.1 copy.28.cc_ref
  3.6 0.0 copy-start.1
  3.6 0.8 %subtract_exponential_fusion.ie_ref = f32[384,8]{1,0:T(8,128)} fusion(f32[384,8]{1,0:T(8,128)S(1)} %copy.28.cc_ref, f32[8]{0:T(128)S(1)} %slice_reduce_fusion), kind=kLoop, calls=%fused_computation.13 | loop fusion | flops 3072 | bytes 24608 | tf_op jit(solution)/shard_map/exp | solution.py:352
  4.3 0.0 copy-done.7
  4.4 0.0 copy-done.4
  4.4 0.0 copy-done.3
  4.4 0.2 copy.22
  4.7 0.6 fusion
  5.3 0.0 copy-start.2
  5.3 0.2 copy.23
  5.5 0.2 reshape_reshape.8
  5.7 0.6 copy-done.2
  6.3 0.2 copy.24
  6.5 0.6 fusion.1
  7.1 0.2 copy.25
  7.3 0.2 reshape_reshape.9
  7.5 0.7 %pad_maximum_fusion.pack_ref = bf16[8,32,512]{2,1,0:T(8,128)(2,1)} fusion(bf16[8,16,512]{2,1,0:T(8,128)(2,1)S(1)} %reshape_reshape.9, bf16[8,16,512]{2,1,0:T(8,128)(2,1)S(1)} %reshape_reshape.8), kind=kLoop, calls=%fused_computation.12 | loop fusion | flops 524288 | bytes 524288 | tf_op jit(solution)/shard_map/concatenate | solution.py:295
  8.3 1.1 %fusion.9.sc_ref = f32[384,384]{1,0:T(8,128)} fusion(bf16[384,128]{1,0:T(8,128)(2,1)S(1)} %copy-done.5, bf16[384,128]{1,0:T(8,128)(2,1)S(1)} %copy-done.4), kind=kOutput, calls=%fused_computation.19 | convolution fusion | flops 37748736 | bytes 786432 | tf_op jit(solution)/shard_map/dot_general | solution.py:368
  9.3 58.5 %shard_map.76 = (bf16[384,512]{1,0:T(8,128)(2,1)}, bf16[8,96,128]{2,1,0:T(8,128)(2,1)}) custom-call(bf16[8,32,512]{2,1,0:T(8,128)(2,1)} %pad_maximum_fusion.pack_ref, f32[8,512]{1,0:T(8,128)} %broadcast_in_dim.8.pdec_ref, bf16[384,512]{1,0:T(8,128)(2,1)} %x_ref.1, bf16[384,512]{1,0:T(8,128)(2,1)} %dy_ref.1, f32[384,384]{1,0:T(8,128)} %fusion.9.sc_ref, ...), custom_call_target="tpu_custom_call" | custom-call | tf_op jit(solution)/shard_map/pallas_call | solution.py:301
  67.8 1.7 %fusion.7 = (bf16[4,96,128]{2,1,0:T(8,128)(2,1)}, bf16[4,96,128]{2,1,0:T(8,128)(2,1)}) fusion(bf16[8,96,128]{2,1,0:T(8,128)(2,1)} %get-tuple-element.6), kind=kLoop, calls=%fused_computation.17 | loop fusion | bytes 393216 | tf_op jit(solution)/shard_map/slice | solution.py:340
  69.5 0.7 %copy.32 = bf16[384,512]{1,0:T(8,128)(2,1)} copy(bf16[384,512]{1,0:T(8,128)(2,1)S(1)} %copy-done.6) | data formatting | bytes 786432
  (9 shorter events, 0.0 us)
Async XLA Ops:
  0.6 0.7 %copy-start = (f32[8,384]{1,0:T(8,128)S(1)}, f32[8,384]{1,0:T(8,128)}, u32[]{:S(2)}) copy-start(f32[8,384]{1,0:T(8,128)} %param.8) | copy-start | bytes 36868
  0.6 3.7 %copy-start.5 = (bf16[384,128]{1,0:T(8,128)(2,1)S(1)}, bf16[384,128]{1,0:T(8,128)(2,1)}, u32[]{:S(2)}) copy-start(bf16[384,128]{1,0:T(8,128)(2,1)} %b_ref.1) | copy-start | bytes 294916
  1.6 2.8 %copy-start.7 = (f32[384,8]{0,1:T(8,128)}, f32[384,8]{0,1:T(8,128)S(1)}, u32[]{:S(2)}) copy-start(f32[384,8]{0,1:T(8,128)S(1)} %get-tuple-element.12) | copy-start | bytes 36868
  1.8 2.6 %copy-start.4 = (bf16[384,128]{1,0:T(8,128)(2,1)S(1)}, bf16[384,128]{1,0:T(8,128)(2,1)}, u32[]{:S(2)}) copy-start(bf16[384,128]{1,0:T(8,128)(2,1)} %c_ref.1) | copy-start | bytes 294916
  3.4 1.0 %copy-start.3 = (bf16[384,512]{1,0:T(8,128)(2,1)S(1)}, bf16[384,512]{1,0:T(8,128)(2,1)}, u32[]{:S(2)}) copy-start(bf16[384,512]{1,0:T(8,128)(2,1)} %x_ref.1) | copy-start | bytes 1179652
  3.6 1.1 %copy-start.1 = (f32[384,8]{1,0:T(8,128)}, f32[384,8]{1,0:T(8,128)S(1)}, u32[]{:S(2)}) copy-start(f32[384,8]{1,0:T(8,128)S(1)} %copy.28.cc_ref) | copy-start | bytes 36868
  5.3 1.0 %copy-start.2 = (bf16[384,512]{1,0:T(8,128)(2,1)S(1)}, bf16[384,512]{1,0:T(8,128)(2,1)}, u32[]{:S(2)}) copy-start(bf16[384,512]{1,0:T(8,128)(2,1)} %dy_ref.1) | copy-start | bytes 1179652
  67.8 1.7 %copy-start.6 = (bf16[384,512]{1,0:T(8,128)(2,1)S(1)}, bf16[384,512]{1,0:T(8,128)(2,1)}, u32[]{:S(2)}) copy-start(bf16[384,512]{1,0:T(8,128)(2,1)} %get-tuple-element.16) | copy-start | bytes 1179652

commit v12 on v11

--- a/solution.py
+++ b/solution.py
@@ -23,8 +23,8 @@
     return nt_dot(ph, qh) + (nt_dot(ph, ql) + nt_dot(pl_, qh))
 
 
-def scan_kernel(rows_n, width, groups, pack_ref, pdec_ref, x_ref, dy_ref, sc_ref, cr_ref, cc_ref, ie_ref,
-                fs_ref, b_ref, c_ref, gv_ref, sum_ref, run_ref, dx_ref, xs_ref, ds_ref, recv1, rdec,
+def scan_kernel(rows_n, width, groups, pack_ref, pdec_ref, x_ref, dy_ref, sc_ref, cr_ref, cc_ref,
+                b_ref, c_ref, gv_ref, sum_ref, run_ref, dx_ref, xs_ref, ds_ref, recv1, rdec,
                 win, out3, recv3, full, parts, gather1, gather2, send1, rsem1, send2, rsem2, send3, rsem3,
                 local, dsend, drecv, hsend1, hrecv1, hsend2, hrecv2):
     me = lax.axis_index("seq")
@@ -41,19 +41,21 @@
 
     def head(h):
         gaps = cr_ref[h:h + 1, :] - cc_ref[:, h:h + 1]
+
         dec = jnp.where(later, jnp.exp(jnp.where(later, gaps, 0.0)), 0.0)
         mix = (sc_ref[...] * dec).astype(jnp.bfloat16)
         lanes = slice(h * hd, (h + 1) * hd)
         dy_h = dy_ref[:, lanes]
         x_h = x_ref[:, lanes]
-        xs_ref[:, lanes] = x_h.astype(jnp.float32) * ie_ref[:, h:h + 1]
-        ds_ref[:, lanes] = dy_h.astype(jnp.float32) * fs_ref[:, h:h + 1]
+        xs_ref[:, lanes] = x_h.astype(jnp.float32) * cc_ref[:, nh + h:nh + h + 1]
+        ds_ref[:, lanes] = dy_h.astype(jnp.float32) * cc_ref[:, 2 * nh + h:2 * nh + h + 1]
         dx_ref[:, lanes] = jnp.dot(mix, dy_h, preferred_element_type=jnp.float32)
         pairs = lax.dot_general(
             x_h, dy_h, (((1,), (1,)), ((), ())), preferred_element_type=jnp.float32)
         run_ref[...] += dec * pairs
 
-    heads_left = list(range(cr_ref.shape[0]))
+    nh = cr_ref.shape[0]
+    heads_left = list(range(nh))
     hd = x_ref.shape[1] // cr_ref.shape[0]
 
     def heads(k):
@@ -80,7 +82,7 @@
     peers = width - 1 + groups - 1
     for d in spans:
         peers = peers + ((rows_n - 1 - y) // d + rows_n - 1) // rows_n + (y // d + rows_n - 1) // rows_n
-    heads(1)
+    heads(2)
     pl.semaphore_wait(barrier, peers)
 
     own = pltpu.make_async_copy(pack_ref.at[c], recv1.at[c], local.at[0])
@@ -255,7 +257,7 @@
         b_ref[...], adj_lo, preferred_element_type=jnp.float32)
     for h in range(cr_ref.shape[0]):
         lanes = slice(h * hd, (h + 1) * hd)
-        gv_ref[:, lanes] = (dx_ref[:, lanes] + ie_ref[:, h:h + 1] * b_adj[:, lanes]).astype(
+        gv_ref[:, lanes] = (dx_ref[:, lanes] + cc_ref[:, nh + h:nh + h + 1] * b_adj[:, lanes]).astype(
             gv_ref.dtype)
     total = parts[pl.ds(pl.multiple_of(z * rows, rows), rows), :].astype(jnp.float32)
     for k in range(1, groups):
@@ -298,13 +300,14 @@
     decay_rows = jnp.broadcast_to(decay_cols, (8, w))
     length = scores_t.shape[0]
     chunk_rows = 2 * length // groups
+    columns = jnp.concatenate([cumulative, into_end, from_start], axis=0).T
     grad_values, sums = pl.pallas_call(
         functools.partial(scan_kernel, rows_n, width, groups),
         out_shape=(
             jax.ShapeDtypeStruct(x.shape, jnp.bfloat16),
             jax.ShapeDtypeStruct((groups, chunk_rows, s), jnp.bfloat16),
         ),
-        in_specs=[pl.BlockSpec(memory_space=pltpu.VMEM)] * 11,
+        in_specs=[pl.BlockSpec(memory_space=pltpu.VMEM)] * 9,
         out_specs=(pl.BlockSpec(memory_space=pltpu.VMEM),) * 2,
         scratch_shapes=[
             pltpu.VMEM((length, length), jnp.float32),
@@ -335,7 +338,7 @@
             pltpu.SemaphoreType.DMA((groups,)),
         ],
         compiler_params=pltpu.CompilerParams(collective_id=1, has_side_effects=True),
-    )(pack, decay_rows, x, dy, scores_t, cumulative, cumulative.T, into_end.T, from_start.T, b_inputs, c_inputs)
+    )(pack, decay_rows, x, dy, scores_t, cumulative, columns, b_inputs, c_inputs)
     sums = sums.reshape(2 * length, s)
     return grad_values, sums[:length], sums[length:]
 

time: 70.5 us -> 69.4 us (0.984)
  other arithmetic: 1.58 us -> 0.83 us
    concatenate x0 -> x1, local copies, waits for them, and re-layouts: none -> 0.82 us  [exclusive_scans(): columns = jnp.concatenate([cumulative, into_end, from_start], axis=0).T]
    exp x1 -> x0, local copies, waits for them, and re-layouts: 0.81 us -> none  [shards(): from_start = jnp.exp(cumulative)]
    exp x2 -> x1, other arithmetic: 0.83 us -> 0.07 us  [shards(): into_end = jnp.exp(block_log[:, None] - cumulative)]
    unnamed x19 -> x17, local copies, waits for them, and re-layouts: 2.51 us -> 2.45 us
where the time goes in v12:
time: 69.4 us; the launch traced here: 69.2 us
  Pallas kernels  58.3 us (84%)
  local copies, waits for them, and re-layouts  6.73 us (10%)
  matrix products  2.51 us (4%)
  other arithmetic  0.83 us (1%)
  between operations  0.78 us (1%)
    pallas_call x1, Pallas kernels, exclusive_scans(): pl.pallas_call(functools.partial(scan_kernel, rows_n, width, groups), out...  58.3 us
    unnamed x17, local copies, waits for them, and re-layouts  2.45 us
    slice x1, local copies, waits for them, and re-layouts, exclusive_scans(): return (grad_values, sums[:length], sums[length:])  1.68 us

profile of v12, /device:TPU:16, one launch (start us, length us, event | category | flops | bytes accessed | tf_op | source)
XLA Modules:
  0.0 69.2 jit_solution(13530269918389616978)
XLA Ops:
  0.6 0.0 copy-start
  0.6 0.0 copy-start.3
  0.7 0.0 copy-start.4
  0.7 0.0 copy-start.2
  0.7 0.7 copy-done
  1.3 0.2 convolution_bitcast_fusion.cr_ref
  1.6 0.2 slice_reduce_fusion
  1.8 0.1 broadcast_in_dim.6
  1.8 0.1 broadcast_in_dim.7
  1.9 0.6 broadcast_in_dim.8.pdec_ref
  2.5 0.1 subtract_exponential_fusion
  2.6 0.8 %copy.33 = f32[24,384]{0,1:T(8,128)} copy(f32[24,384]{1,0:T(8,128)S(1)} %pad_maximum_fusion.1) | data formatting | bytes 73728 | tf_op jit(solution)/shard_map/concatenate | solution.py:303
  3.4 0.0 copy-done.4
  3.5 0.0 copy-done.3
  3.5 0.0 copy-done.2
  3.5 0.2 copy.29
  3.7 0.0 copy-done.6
  3.7 0.6 fusion
  4.4 0.0 copy-start.1
  4.4 0.2 copy.30
  4.6 0.2 reshape_reshape.8
  4.8 0.6 copy-done.1
  5.4 0.2 copy.31
  5.6 0.6 fusion.1
  6.2 0.2 copy.32
  6.4 0.2 reshape_reshape.9
  6.6 0.7 %pad_maximum_fusion.pack_ref = bf16[8,32,512]{2,1,0:T(8,128)(2,1)} fusion(bf16[8,16,512]{2,1,0:T(8,128)(2,1)S(1)} %reshape_reshape.9, bf16[8,16,512]{2,1,0:T(8,128)(2,1)S(1)} %reshape_reshape.8), kind=kLoop, calls=%fused_computation.12 | loop fusion | flops 524288 | bytes 524288 | tf_op jit(solution)/shard_map/concatenate | solution.py:297
  7.3 1.1 %fusion.7.sc_ref = f32[384,384]{1,0:T(8,128)} fusion(bf16[384,128]{1,0:T(8,128)(2,1)S(1)} %copy-done.4, bf16[384,128]{1,0:T(8,128)(2,1)S(1)} %copy-done.3), kind=kOutput, calls=%fused_computation.17 | convolution fusion | flops 37748736 | bytes 786432 | tf_op jit(solution)/shard_map/dot_general | solution.py:371
  8.4 58.3 %shard_map.76 = (bf16[384,512]{1,0:T(8,128)(2,1)}, bf16[8,96,128]{2,1,0:T(8,128)(2,1)}) custom-call(bf16[8,32,512]{2,1,0:T(8,128)(2,1)} %pad_maximum_fusion.pack_ref, f32[8,512]{1,0:T(8,128)} %broadcast_in_dim.8.pdec_ref, bf16[384,512]{1,0:T(8,128)(2,1)} %x_ref.1, bf16[384,512]{1,0:T(8,128)(2,1)} %dy_ref.1, f32[384,384]{1,0:T(8,128)} %fusion.7.sc_ref, ...), custom_call_target="tpu_custom_call" | custom-call | tf_op jit(solution)/shard_map/pallas_call | solution.py:304
  66.8 0.0 copy-start.5
  66.8 1.7 %fusion.6 = (bf16[4,96,128]{2,1,0:T(8,128)(2,1)}, bf16[4,96,128]{2,1,0:T(8,128)(2,1)}) fusion(bf16[8,96,128]{2,1,0:T(8,128)(2,1)} %get-tuple-element.6), kind=kLoop, calls=%fused_computation.16 | loop fusion | bytes 393216 | tf_op jit(solution)/shard_map/slice | solution.py:343
  68.4 0.7 %copy.35 = bf16[384,512]{1,0:T(8,128)(2,1)} copy(bf16[384,512]{1,0:T(8,128)(2,1)S(1)} %copy-done.5) | data formatting | bytes 786432
  (6 shorter events, 0.0 us)
Async XLA Ops:
  0.6 0.7 %copy-start = (f32[8,384]{1,0:T(8,128)S(1)}, f32[8,384]{1,0:T(8,128)}, u32[]{:S(2)}) copy-start(f32[8,384]{1,0:T(8,128)} %param.8) | copy-start | bytes 36868
  0.6 2.8 %copy-start.3 = (bf16[384,128]{1,0:T(8,128)(2,1)S(1)}, bf16[384,128]{1,0:T(8,128)(2,1)}, u32[]{:S(2)}) copy-start(bf16[384,128]{1,0:T(8,128)(2,1)} %c_ref.1) | copy-start | bytes 294916
  0.7 2.8 %copy-start.4 = (bf16[384,128]{1,0:T(8,128)(2,1)S(1)}, bf16[384,128]{1,0:T(8,128)(2,1)}, u32[]{:S(2)}) copy-start(bf16[384,128]{1,0:T(8,128)(2,1)} %b_ref.1) | copy-start | bytes 294916
  0.7 2.8 %copy-start.2 = (bf16[384,512]{1,0:T(8,128)(2,1)S(1)}, bf16[384,512]{1,0:T(8,128)(2,1)}, u32[]{:S(2)}) copy-start(bf16[384,512]{1,0:T(8,128)(2,1)} %x_ref.1) | copy-start | bytes 1179652
  1.6 2.2 %copy-start.6 = (f32[8,384]{1,0:T(8,128)}, f32[8,384]{1,0:T(8,128)S(1)}, u32[]{:S(2)}) copy-start(f32[8,384]{1,0:T(8,128)S(1)} %convolution_bitcast_fusion.cr_ref) | copy-start | bytes 36868
  4.4 1.0 %copy-start.1 = (bf16[384,512]{1,0:T(8,128)(2,1)S(1)}, bf16[384,512]{1,0:T(8,128)(2,1)}, u32[]{:S(2)}) copy-start(bf16[384,512]{1,0:T(8,128)(2,1)} %dy_ref.1) | copy-start | bytes 1179652
  66.8 1.7 %copy-start.5 = (bf16[384,512]{1,0:T(8,128)(2,1)S(1)}, bf16[384,512]{1,0:T(8,128)(2,1)}, u32[]{:S(2)}) copy-start(bf16[384,512]{1,0:T(8,128)(2,1)} %get-tuple-element.14) | copy-start | bytes 1179652

commit v13 on v12

--- a/solution.py
+++ b/solution.py
@@ -23,10 +23,10 @@
     return nt_dot(ph, qh) + (nt_dot(ph, ql) + nt_dot(pl_, qh))
 
 
-def scan_kernel(rows_n, width, groups, pack_ref, pdec_ref, x_ref, dy_ref, sc_ref, cr_ref, cc_ref,
+def scan_kernel(rows_n, width, groups, pack_ref, dcol_ref, x_ref, dy_ref, cr_ref, cc_ref,
                 b_ref, c_ref, gv_ref, sum_ref, run_ref, dx_ref, xs_ref, ds_ref, recv1, rdec,
                 win, out3, recv3, full, parts, gather1, gather2, send1, rsem1, send2, rsem2, send3, rsem3,
-                local, dsend, drecv, hsend1, hrecv1, hsend2, hrecv2):
+                local, dsend, drecv, hsend1, hrecv1, hsend2, hrecv2, sc_ref, pdec_ref):
     me = lax.axis_index("seq")
     col = lax.axis_index("head")
     c = me % width
@@ -34,7 +34,8 @@
     piece = recv1.shape[1] // 2
     spans = [1, 2, 3, 4]
 
-    length = sc_ref.shape[0]
+    length = x_ref.shape[0]
+    pdec_ref[...] = jnp.broadcast_to(dcol_ref[...], pdec_ref.shape)
     later = lax.broadcasted_iota(jnp.int32, (length, length), 1) >= lax.broadcasted_iota(
         jnp.int32, (length, length), 0)
     run_ref[...] = jnp.zeros(run_ref.shape, run_ref.dtype)
@@ -82,6 +83,7 @@
     peers = width - 1 + groups - 1
     for d in spans:
         peers = peers + ((rows_n - 1 - y) // d + rows_n - 1) // rows_n + (y // d + rows_n - 1) // rows_n
+    sc_ref[...] = nt_dot(b_ref[...], c_ref[...])
     heads(2)
     pl.semaphore_wait(barrier, peers)
 
@@ -287,7 +289,7 @@
     sum_ref[...] = gather2[...]
 
 
-def exclusive_scans(count, groups, decay_cols, forward, backward, x, dy, scores_t, cumulative,
+def exclusive_scans(count, groups, decay_cols, forward, backward, x, dy, cumulative,
                     into_end, from_start, b_inputs, c_inputs):
     s, w = forward.shape
     width = 8 if count % 8 == 0 else 1
@@ -297,8 +299,7 @@
     pack = jnp.concatenate(
         [forward.reshape(width, piece, w), backward.reshape(width, piece, w)], axis=1
     ).astype(jnp.bfloat16)
-    decay_rows = jnp.broadcast_to(decay_cols, (8, w))
-    length = scores_t.shape[0]
+    length = x.shape[0]
     chunk_rows = 2 * length // groups
     columns = jnp.concatenate([cumulative, into_end, from_start], axis=0).T
     grad_values, sums = pl.pallas_call(
@@ -307,7 +308,7 @@
             jax.ShapeDtypeStruct(x.shape, jnp.bfloat16),
             jax.ShapeDtypeStruct((groups, chunk_rows, s), jnp.bfloat16),
         ),
-        in_specs=[pl.BlockSpec(memory_space=pltpu.VMEM)] * 9,
+        in_specs=[pl.BlockSpec(memory_space=pltpu.VMEM)] * 8,
         out_specs=(pl.BlockSpec(memory_space=pltpu.VMEM),) * 2,
         scratch_shapes=[
             pltpu.VMEM((length, length), jnp.float32),
@@ -336,9 +337,11 @@
             pltpu.SemaphoreType.DMA((groups,)),
             pltpu.SemaphoreType.DMA((groups,)),
             pltpu.SemaphoreType.DMA((groups,)),
+            pltpu.VMEM((length, length), jnp.float32),
+            pltpu.VMEM((8, w), jnp.float32),
         ],
         compiler_params=pltpu.CompilerParams(collective_id=1, has_side_effects=True),
-    )(pack, decay_rows, x, dy, scores_t, cumulative, columns, b_inputs, c_inputs)
+    )(pack, decay_cols, x, dy, cumulative, columns, b_inputs, c_inputs)
     sums = sums.reshape(2 * length, s)
     return grad_values, sums[:length], sums[length:]
 
@@ -368,11 +371,8 @@
         "hsn,shp->nhp", decayed_c, dy_heads, preferred_element_type=jnp.float32
     ).reshape(state_size, heads_here * head_dim)
     decay_cols = jnp.repeat(block_decay, head_dim)[None, :]
-    scores_t = lax.dot_general(
-        b_inputs, c_inputs, (((1,), (1,)), ((), ())), preferred_element_type=jnp.float32
-    )
     grad_values, grad_b, grad_c = exclusive_scans(
-        count, groups, decay_cols, state_local, adjoint_local, token_values, grad_out, scores_t,
+        count, groups, decay_cols, state_local, adjoint_local, token_values, grad_out,
         cumulative, into_end, from_start, b_inputs, c_inputs,
     )
     return grad_values, grad_b, grad_c

time: 69.4 us -> 69.2 us (level)
  matrix products: 2.51 us -> 1.46 us
  local copies, waits for them, and re-layouts: 6.73 us -> 7.71 us
    dot_general x1 -> x0, matrix products: 1.07 us -> none  [shards(): lax.dot_general(b_inputs, c_inputs, (((1,), (1,)), ((), ())), preferred_e...]
    unnamed x17 -> x15, local copies, waits for them, and re-layouts: 2.45 us -> 3.48 us
    broadcast_in_dim x2 -> x0, local copies, waits for them, and re-layouts: 0.7 us -> none  [exclusive_scans(): decay_rows = jnp.broadcast_to(decay_cols, (8, w))]
where the time goes in v13:
time: 69.2 us; the launch traced here: 69 us
  Pallas kernels  58.2 us (84%)
  local copies, waits for them, and re-layouts  7.71 us (11%)
  matrix products  1.46 us (2%)
  other arithmetic  0.83 us (1%)
  between operations  0.75 us (1%)
    pallas_call x1, Pallas kernels, exclusive_scans(): pl.pallas_call(functools.partial(scan_kernel, rows_n, width, groups), out...  58.2 us
    unnamed x15, local copies, waits for them, and re-layouts  3.48 us
    slice x1, local copies, waits for them, and re-layouts, exclusive_scans(): return (grad_values, sums[:length], sums[length:])  1.68 us

profile of v13, /device:TPU:16, one launch (start us, length us, event | category | flops | bytes accessed | tf_op | source)
XLA Modules:
  0.0 69.0 jit_solution(7923137962488381511)
XLA Ops:
  0.6 0.0 copy-start
  0.6 0.0 copy-start.3
  0.7 1.2 %copy.31 = bf16[384,512]{0,1:T(8,128)(2,1)S(1)} copy(bf16[384,512]{1,0:T(8,128)(2,1)} %dy_ref.1) | data formatting | bytes 786432 | tf_op args[4]
  1.9 0.0 copy-done.3
  1.9 0.0 copy-done
  2.0 0.2 convolution_bitcast_fusion.cr_ref
  2.2 0.0 copy-start.5
  2.2 0.2 slice_reduce_fusion
  2.4 0.1 subtract_exponential_fusion
  2.4 0.6 fusion.1
  3.1 0.0 copy-start.1
  3.1 0.2 copy.32
  3.3 0.2 reshape_reshape.9
  3.5 0.6 copy-done.1
  4.1 0.0 copy-start.4
  4.1 0.2 copy.29
  4.3 0.7 copy-done.4
  5.0 0.6 fusion
  5.6 0.2 copy.30
  5.8 0.2 reshape_reshape.8
  6.0 0.7 %pad_maximum_fusion.pack_ref = bf16[8,32,512]{2,1,0:T(8,128)(2,1)} fusion(bf16[8,16,512]{2,1,0:T(8,128)(2,1)S(1)} %reshape_reshape.9, bf16[8,16,512]{2,1,0:T(8,128)(2,1)S(1)} %reshape_reshape.8), kind=kLoop, calls=%fused_computation.12 | loop fusion | flops 524288 | bytes 524288 | tf_op jit(solution)/shard_map/concatenate | solution.py:299
  6.8 0.1 broadcast_in_dim.2
  6.8 0.7 broadcast_in_dim_reshape.3.dcol_ref
  7.5 0.0 copy-done.5
  7.5 0.8 %copy.33 = f32[24,384]{0,1:T(8,128)} copy(f32[24,384]{1,0:T(8,128)S(1)} %pad_maximum_fusion.1) | data formatting | bytes 73728 | tf_op jit(solution)/shard_map/concatenate | solution.py:304
  8.3 58.2 %shard_map.76 = (bf16[384,512]{1,0:T(8,128)(2,1)}, bf16[8,96,128]{2,1,0:T(8,128)(2,1)}) custom-call(bf16[8,32,512]{2,1,0:T(8,128)(2,1)} %pad_maximum_fusion.pack_ref, f32[1,512]{1,0:T(1,128)} %broadcast_in_dim_reshape.3.dcol_ref, bf16[384,512]{1,0:T(8,128)(2,1)} %x_ref.1, bf16[384,512]{1,0:T(8,128)(2,1)} %dy_ref.1, f32[8,384]{1,0:T(8,128)} %copy-done.5, ...), custom_call_target="tpu_custom_call" | custom-call | tf_op jit(solution)/shard_map/pallas_call | solution.py:305
  66.5 0.0 copy-start.2
  66.5 1.7 %fusion.6 = (bf16[4,96,128]{2,1,0:T(8,128)(2,1)}, bf16[4,96,128]{2,1,0:T(8,128)(2,1)}) fusion(bf16[8,96,128]{2,1,0:T(8,128)(2,1)} %get-tuple-element.6), kind=kLoop, calls=%fused_computation.16 | loop fusion | bytes 393216 | tf_op jit(solution)/shard_map/slice | solution.py:346
  68.2 0.0 copy-done.2
  68.2 0.7 %copy.35 = bf16[384,512]{1,0:T(8,128)(2,1)} copy(bf16[384,512]{1,0:T(8,128)(2,1)S(1)} %copy-done.2) | data formatting | bytes 786432
  (4 shorter events, 0.0 us)
Async XLA Ops:
  0.6 1.3 %copy-start = (f32[8,384]{1,0:T(8,128)S(1)}, f32[8,384]{1,0:T(8,128)}, u32[]{:S(2)}) copy-start(f32[8,384]{1,0:T(8,128)} %param.8) | copy-start | bytes 36868
  0.6 1.3 %copy-start.3 = (bf16[384,128]{1,0:T(8,128)(2,1)S(1)}, bf16[384,128]{1,0:T(8,128)(2,1)}, u32[]{:S(2)}) copy-start(bf16[384,128]{1,0:T(8,128)(2,1)} %c_ref.1) | copy-start | bytes 294916
  2.2 5.3 %copy-start.5 = (f32[8,384]{1,0:T(8,128)}, f32[8,384]{1,0:T(8,128)S(1)}, u32[]{:S(2)}) copy-start(f32[8,384]{1,0:T(8,128)S(1)} %convolution_bitcast_fusion.cr_ref) | copy-start | bytes 36868
  3.1 1.0 %copy-start.1 = (bf16[384,512]{1,0:T(8,128)(2,1)S(1)}, bf16[384,512]{1,0:T(8,128)(2,1)}, u32[]{:S(2)}) copy-start(bf16[384,512]{1,0:T(8,128)(2,1)} %x_ref.1) | copy-start | bytes 1179652
  4.1 0.9 %copy-start.4 = (bf16[384,128]{1,0:T(8,128)(2,1)S(1)}, bf16[384,128]{1,0:T(8,128)(2,1)}, u32[]{:S(2)}) copy-start(bf16[384,128]{1,0:T(8,128)(2,1)} %b_ref.1) | copy-start | bytes 294916
  66.5 1.7 %copy-start.2 = (bf16[384,512]{1,0:T(8,128)(2,1)S(1)}, bf16[384,512]{1,0:T(8,128)(2,1)}, u32[]{:S(2)}) copy-start(bf16[384,512]{1,0:T(8,128)(2,1)} %get-tuple-element.14) | copy-start | bytes 1179652

commit v14 on v13

--- a/solution.py
+++ b/solution.py
@@ -26,7 +26,8 @@
 def scan_kernel(rows_n, width, groups, pack_ref, dcol_ref, x_ref, dy_ref, cr_ref, cc_ref,
                 b_ref, c_ref, gv_ref, sum_ref, run_ref, dx_ref, xs_ref, ds_ref, recv1, rdec,
                 win, out3, recv3, full, parts, gather1, gather2, send1, rsem1, send2, rsem2, send3, rsem3,
-                local, dsend, drecv, hsend1, hrecv1, hsend2, hrecv2, sc_ref, pdec_ref):
+                local, dsend, drecv, hsend1, hrecv1, hsend2, hrecv2, sc_ref, pdec_ref,
+                early):
     me = lax.axis_index("seq")
     col = lax.axis_index("head")
     c = me % width
@@ -217,6 +218,10 @@
             recv_sem=rsem3.at[off], device_id=(y * width + k, col), device_id_type=MESH)
         cp.start()
         sends.append(cp)
+    weighted = run_ref[...].astype(jnp.bfloat16)
+    early[0] = jnp.dot(weighted, c_ref[...], preferred_element_type=jnp.float32)
+    early[1] = lax.dot_general(
+        weighted, b_ref[...], (((0,), (0,)), ((), ())), preferred_element_type=jnp.float32)
     for off in range(1, width):
         k = (c + width - off) % width
         pltpu.make_async_remote_copy(
@@ -230,12 +235,8 @@
     for k in range(width):
         full[0, k * piece:(k + 1) * piece, :] = recv3[k, :piece, :].astype(jnp.float32)
         full[1, k * piece:(k + 1) * piece, :] = recv3[k, piece:, :].astype(jnp.float32)
-    weighted = run_ref[...].astype(jnp.bfloat16)
-    part_b = jnp.dot(weighted, c_ref[...], preferred_element_type=jnp.float32) + nt_dot_f32(
-        xs_ref[...], full[1])
-    part_c = lax.dot_general(
-        weighted, b_ref[...], (((0,), (0,)), ((), ())), preferred_element_type=jnp.float32
-    ) + nt_dot_f32(ds_ref[...], full[0])
+    part_b = early[0] + nt_dot_f32(xs_ref[...], full[1])
+    part_c = early[1] + nt_dot_f32(ds_ref[...], full[0])
     n_rows = part_b.shape[0]
     parts[:n_rows, :] = part_b.astype(parts.dtype)
     parts[n_rows:, :] = part_c.astype(parts.dtype)
@@ -339,6 +340,7 @@
             pltpu.SemaphoreType.DMA((groups,)),
             pltpu.VMEM((length, length), jnp.float32),
             pltpu.VMEM((8, w), jnp.float32),
+            pltpu.VMEM((2, length, s), jnp.float32),
         ],
         compiler_params=pltpu.CompilerParams(collective_id=1, has_side_effects=True),
     )(pack, decay_cols, x, dy, cumulative, columns, b_inputs, c_inputs)

time: 69.2 us -> 69 us (level)
  no operation moved by 1% of the time
where the time goes in v14:
time: 69 us; the launch traced here: 68.8 us
  Pallas kernels  58 us (84%)
  local copies, waits for them, and re-layouts  7.71 us (11%)
  matrix products  1.46 us (2%)
  other arithmetic  0.83 us (1%)
  between operations  0.75 us (1%)
    pallas_call x1, Pallas kernels, exclusive_scans(): pl.pallas_call(functools.partial(scan_kernel, rows_n, width, groups), out...  58 us
    unnamed x15, local copies, waits for them, and re-layouts  3.48 us
    slice x1, local copies, waits for them, and re-layouts, exclusive_scans(): return (grad_values, sums[:length], sums[length:])  1.68 us

profile of v14, /device:TPU:16, one launch (start us, length us, event | category | flops | bytes accessed | tf_op | source)
XLA Modules:
  0.0 68.8 jit_solution(4042628597374770413)
XLA Ops:
  0.6 0.0 copy-start
  0.6 0.0 copy-start.3
  0.7 1.2 %copy.31 = bf16[384,512]{0,1:T(8,128)(2,1)S(1)} copy(bf16[384,512]{1,0:T(8,128)(2,1)} %dy_ref.1) | data formatting | bytes 786432 | tf_op args[4]
  1.9 0.0 copy-done.3
  1.9 0.0 copy-done
  2.0 0.2 convolution_bitcast_fusion.cr_ref
  2.2 0.0 copy-start.5
  2.2 0.2 slice_reduce_fusion
  2.4 0.1 subtract_exponential_fusion
  2.4 0.6 fusion.1
  3.1 0.0 copy-start.1
  3.1 0.2 copy.32
  3.3 0.2 reshape_reshape.9
  3.5 0.6 copy-done.1
  4.1 0.0 copy-start.4
  4.1 0.2 copy.29
  4.3 0.7 copy-done.4
  5.0 0.6 fusion
  5.6 0.2 copy.30
  5.8 0.2 reshape_reshape.8
  6.0 0.7 %pad_maximum_fusion.pack_ref = bf16[8,32,512]{2,1,0:T(8,128)(2,1)} fusion(bf16[8,16,512]{2,1,0:T(8,128)(2,1)S(1)} %reshape_reshape.9, bf16[8,16,512]{2,1,0:T(8,128)(2,1)S(1)} %reshape_reshape.8), kind=kLoop, calls=%fused_computation.12 | loop fusion | flops 524288 | bytes 524288 | tf_op jit(solution)/shard_map/concatenate | solution.py:300
  6.8 0.1 broadcast_in_dim.2
  6.8 0.7 broadcast_in_dim_reshape.3.dcol_ref
  7.5 0.0 copy-done.5
  7.5 0.8 %copy.33 = f32[24,384]{0,1:T(8,128)} copy(f32[24,384]{1,0:T(8,128)S(1)} %pad_maximum_fusion.1) | data formatting | bytes 73728 | tf_op jit(solution)/shard_map/concatenate | solution.py:305
  8.3 58.0 %shard_map.76 = (bf16[384,512]{1,0:T(8,128)(2,1)}, bf16[8,96,128]{2,1,0:T(8,128)(2,1)}) custom-call(bf16[8,32,512]{2,1,0:T(8,128)(2,1)} %pad_maximum_fusion.pack_ref, f32[1,512]{1,0:T(1,128)} %broadcast_in_dim_reshape.3.dcol_ref, bf16[384,512]{1,0:T(8,128)(2,1)} %x_ref.1, bf16[384,512]{1,0:T(8,128)(2,1)} %dy_ref.1, f32[8,384]{1,0:T(8,128)} %copy-done.5, ...), custom_call_target="tpu_custom_call" | custom-call | tf_op jit(solution)/shard_map/pallas_call | solution.py:306
  66.3 0.0 copy-start.2
  66.4 1.7 %fusion.6 = (bf16[4,96,128]{2,1,0:T(8,128)(2,1)}, bf16[4,96,128]{2,1,0:T(8,128)(2,1)}) fusion(bf16[8,96,128]{2,1,0:T(8,128)(2,1)} %get-tuple-element.6), kind=kLoop, calls=%fused_computation.16 | loop fusion | bytes 393216 | tf_op jit(solution)/shard_map/slice | solution.py:348
  68.0 0.0 copy-done.2
  68.0 0.7 %copy.35 = bf16[384,512]{1,0:T(8,128)(2,1)} copy(bf16[384,512]{1,0:T(8,128)(2,1)S(1)} %copy-done.2) | data formatting | bytes 786432
  (4 shorter events, 0.0 us)
Async XLA Ops:
  0.6 1.3 %copy-start = (f32[8,384]{1,0:T(8,128)S(1)}, f32[8,384]{1,0:T(8,128)}, u32[]{:S(2)}) copy-start(f32[8,384]{1,0:T(8,128)} %param.8) | copy-start | bytes 36868
  0.6 1.3 %copy-start.3 = (bf16[384,128]{1,0:T(8,128)(2,1)S(1)}, bf16[384,128]{1,0:T(8,128)(2,1)}, u32[]{:S(2)}) copy-start(bf16[384,128]{1,0:T(8,128)(2,1)} %c_ref.1) | copy-start | bytes 294916
  2.2 5.3 %copy-start.5 = (f32[8,384]{1,0:T(8,128)}, f32[8,384]{1,0:T(8,128)S(1)}, u32[]{:S(2)}) copy-start(f32[8,384]{1,0:T(8,128)S(1)} %convolution_bitcast_fusion.cr_ref) | copy-start | bytes 36868
  3.1 1.0 %copy-start.1 = (bf16[384,512]{1,0:T(8,128)(2,1)S(1)}, bf16[384,512]{1,0:T(8,128)(2,1)}, u32[]{:S(2)}) copy-start(bf16[384,512]{1,0:T(8,128)(2,1)} %x_ref.1) | copy-start | bytes 1179652
  4.1 0.9 %copy-start.4 = (bf16[384,128]{1,0:T(8,128)(2,1)S(1)}, bf16[384,128]{1,0:T(8,128)(2,1)}, u32[]{:S(2)}) copy-start(bf16[384,128]{1,0:T(8,128)(2,1)} %b_ref.1) | copy-start | bytes 294916
  66.3 1.7 %copy-start.2 = (bf16[384,512]{1,0:T(8,128)(2,1)S(1)}, bf16[384,512]{1,0:T(8,128)(2,1)}, u32[]{:S(2)}) copy-start(bf16[384,512]{1,0:T(8,128)(2,1)} %get-tuple-element.14) | copy-start | bytes 1179652

commit v15 on v14

--- a/solution.py
+++ b/solution.py
@@ -23,11 +23,11 @@
     return nt_dot(ph, qh) + (nt_dot(ph, ql) + nt_dot(pl_, qh))
 
 
-def scan_kernel(rows_n, width, groups, pack_ref, dcol_ref, x_ref, dy_ref, cr_ref, cc_ref,
+def scan_kernel(rows_n, width, groups, fwd_ref, bwd_ref, x_ref, dy_ref, cr_ref, cc_ref,
                 b_ref, c_ref, gv_ref, sum_ref, run_ref, dx_ref, xs_ref, ds_ref, recv1, rdec,
                 win, out3, recv3, full, parts, gather1, gather2, send1, rsem1, send2, rsem2, send3, rsem3,
                 local, dsend, drecv, hsend1, hrecv1, hsend2, hrecv2, sc_ref, pdec_ref,
-                early):
+                early, pack_ref):
     me = lax.axis_index("seq")
     col = lax.axis_index("head")
     c = me % width
@@ -36,7 +36,6 @@
     spans = [1, 2, 3, 4]
 
     length = x_ref.shape[0]
-    pdec_ref[...] = jnp.broadcast_to(dcol_ref[...], pdec_ref.shape)
     later = lax.broadcasted_iota(jnp.int32, (length, length), 1) >= lax.broadcasted_iota(
         jnp.int32, (length, length), 0)
     run_ref[...] = jnp.zeros(run_ref.shape, run_ref.dtype)
@@ -59,6 +58,13 @@
     nh = cr_ref.shape[0]
     heads_left = list(range(nh))
     hd = x_ref.shape[1] // cr_ref.shape[0]
+    for h in range(nh):
+        pdec_ref[:, h * hd:(h + 1) * hd] = jnp.broadcast_to(
+            jnp.exp(cc_ref[length - 1:length, h:h + 1]), (pdec_ref.shape[0], hd))
+    span = pack_ref.shape[1] // 2
+    for k in range(pack_ref.shape[0]):
+        pack_ref[k, :span, :] = fwd_ref[k * span:(k + 1) * span, :].astype(pack_ref.dtype)
+        pack_ref[k, span:, :] = bwd_ref[k * span:(k + 1) * span, :].astype(pack_ref.dtype)
 
     def heads(k):
         for _ in range(k):
@@ -297,9 +303,6 @@
     rows_n = count // width
     piece = s // width
     assert rows_n <= 8
-    pack = jnp.concatenate(
-        [forward.reshape(width, piece, w), backward.reshape(width, piece, w)], axis=1
-    ).astype(jnp.bfloat16)
     length = x.shape[0]
     chunk_rows = 2 * length // groups
     columns = jnp.concatenate([cumulative, into_end, from_start], axis=0).T
@@ -341,9 +344,10 @@
             pltpu.VMEM((length, length), jnp.float32),
             pltpu.VMEM((8, w), jnp.float32),
             pltpu.VMEM((2, length, s), jnp.float32),
+            pltpu.VMEM((width, 2 * piece, w), jnp.bfloat16),
         ],
         compiler_params=pltpu.CompilerParams(collective_id=1, has_side_effects=True),
-    )(pack, decay_cols, x, dy, cumulative, columns, b_inputs, c_inputs)
+    )(forward, backward, x, dy, cumulative, columns, b_inputs, c_inputs)
     sums = sums.reshape(2 * length, s)
     return grad_values, sums[:length], sums[length:]
 

time: 69 us -> 68.2 us (0.988)
  other arithmetic: 0.83 us -> 0.11 us
    reshape x0 -> x2, local copies, waits for them, and re-layouts: none -> 1.68 us  [the longest x1 0.84 us: shards(): adjoint_local = jnp.einsum('hsn,shp->nhp', decayed_c, dy_heads, preferred...]
    another operation x3 -> x0, local copies, waits for them, and re-layouts: 1.08 us -> none  [the longest x1 0.66 us: shards(): decay_cols = jnp.repeat(block_decay, head_dim)[None, :]]
    concatenate x1 -> x0, other arithmetic: 0.72 us -> none  [exclusive_scans(): jnp.concatenate([forward.reshape(width, piece, w), backward.reshape(width...]
where the time goes in v15:
time: 68.2 us; the launch traced here: 67.9 us
  Pallas kernels  58.2 us (85%)
  local copies, waits for them, and re-layouts  7.41 us (11%)
  matrix products  1.47 us (2%)
  between operations  0.74 us (1%)
    pallas_call x1, Pallas kernels, exclusive_scans(): pl.pallas_call(functools.partial(scan_kernel, rows_n, width, groups), out...  58.2 us
    unnamed x15, local copies, waits for them, and re-layouts  3.06 us
    slice x1, local copies, waits for them, and re-layouts, exclusive_scans(): return (grad_values, sums[:length], sums[length:])  1.68 us

profile of v15, /device:TPU:16, one launch (start us, length us, event | category | flops | bytes accessed | tf_op | source)
XLA Modules:
  0.0 67.9 jit_solution(1018216571458742108)
XLA Ops:
  0.6 0.0 copy-start
  0.6 0.0 copy-start.3
  0.7 1.2 %copy.29 = bf16[384,512]{0,1:T(8,128)(2,1)S(1)} copy(bf16[384,512]{1,0:T(8,128)(2,1)} %x_ref.1) | data formatting | bytes 786432 | tf_op args[0]
  1.9 0.0 copy-done.3
  1.9 0.0 copy-done
  2.0 0.2 convolution_bitcast_fusion.cr_ref
  2.2 0.0 copy-start.5
  2.2 0.2 slice_reduce_fusion
  2.4 0.1 fusion.7
  2.4 0.6 fusion
  3.1 0.0 copy-start.1
  3.1 0.8 %copy.32.fwd_ref = f32[128,512]{1,0:T(8,128)} copy(f32[128,512]{0,1:T(8,128)S(1)} %bitcast.19) | data formatting | bytes 524288 | tf_op jit(solution)/shard_map/reshape | solution.py:375
  3.9 0.1 copy-done.1
  4.1 0.0 copy-start.4
  4.1 0.2 copy.30
  4.3 0.7 copy-done.4
  5.0 0.6 fusion.1
  5.6 0.8 %copy.33.bwd_ref = f32[128,512]{1,0:T(8,128)} copy(f32[128,512]{0,1:T(8,128)S(1)} %bitcast.20) | data formatting | bytes 524288 | tf_op jit(solution)/shard_map/reshape | solution.py:378
  6.5 0.0 copy-done.5
  6.5 0.8 %copy.31 = f32[24,384]{0,1:T(8,128)} copy(f32[24,384]{1,0:T(8,128)S(1)} %pad_maximum_fusion) | data formatting | bytes 73728 | tf_op jit(solution)/shard_map/concatenate | solution.py:308
  7.3 58.2 %shard_map.76 = (bf16[384,512]{1,0:T(8,128)(2,1)}, bf16[8,96,128]{2,1,0:T(8,128)(2,1)}) custom-call(f32[128,512]{1,0:T(8,128)} %copy.32.fwd_ref, f32[128,512]{1,0:T(8,128)} %copy.33.bwd_ref, bf16[384,512]{1,0:T(8,128)(2,1)} %x_ref.1, bf16[384,512]{1,0:T(8,128)(2,1)} %dy_ref.1, f32[8,384]{1,0:T(8,128)} %copy-done.5, f32[384,24]{1,0:T(8,128)} %bitcast.16, ...), custom_call_target="tpu_custom_call" | custom-call | tf_op jit(solution)/shard_map/pallas_call | solution.py:309
  65.5 0.0 copy-start.2
  65.5 1.7 %fusion.6 = (bf16[4,96,128]{2,1,0:T(8,128)(2,1)}, bf16[4,96,128]{2,1,0:T(8,128)(2,1)}) fusion(bf16[8,96,128]{2,1,0:T(8,128)(2,1)} %get-tuple-element.6), kind=kLoop, calls=%fused_computation.13 | loop fusion | bytes 393216 | tf_op jit(solution)/shard_map/slice | solution.py:352
  67.2 0.0 copy-done.2
  67.2 0.7 %copy.35 = bf16[384,512]{1,0:T(8,128)(2,1)} copy(bf16[384,512]{1,0:T(8,128)(2,1)S(1)} %copy-done.2) | data formatting | bytes 786432
  (3 shorter events, 0.0 us)
Async XLA Ops:
  0.6 1.3 %copy-start = (f32[8,384]{1,0:T(8,128)S(1)}, f32[8,384]{1,0:T(8,128)}, u32[]{:S(2)}) copy-start(f32[8,384]{1,0:T(8,128)} %param.8) | copy-start | bytes 36868
  0.6 1.3 %copy-start.3 = (bf16[384,128]{1,0:T(8,128)(2,1)S(1)}, bf16[384,128]{1,0:T(8,128)(2,1)}, u32[]{:S(2)}) copy-start(bf16[384,128]{1,0:T(8,128)(2,1)} %b_ref.1) | copy-start | bytes 294916
  2.2 4.3 %copy-start.5 = (f32[8,384]{1,0:T(8,128)}, f32[8,384]{1,0:T(8,128)S(1)}, u32[]{:S(2)}) copy-start(f32[8,384]{1,0:T(8,128)S(1)} %convolution_bitcast_fusion.cr_ref) | copy-start | bytes 36868
  3.1 1.0 %copy-start.1 = (bf16[384,512]{1,0:T(8,128)(2,1)S(1)}, bf16[384,512]{1,0:T(8,128)(2,1)}, u32[]{:S(2)}) copy-start(bf16[384,512]{1,0:T(8,128)(2,1)} %dy_ref.1) | copy-start | bytes 1179652
  4.1 0.9 %copy-start.4 = (bf16[384,128]{1,0:T(8,128)(2,1)S(1)}, bf16[384,128]{1,0:T(8,128)(2,1)}, u32[]{:S(2)}) copy-start(bf16[384,128]{1,0:T(8,128)(2,1)} %c_ref.1) | copy-start | bytes 294916
  65.5 1.7 %copy-start.2 = (bf16[384,512]{1,0:T(8,128)(2,1)S(1)}, bf16[384,512]{1,0:T(8,128)(2,1)}, u32[]{:S(2)}) copy-start(bf16[384,512]{1,0:T(8,128)(2,1)} %get-tuple-element.14) | copy-start | bytes 1179652

commit v16 on v15

--- a/solution.py
+++ b/solution.py
@@ -23,11 +23,11 @@
     return nt_dot(ph, qh) + (nt_dot(ph, ql) + nt_dot(pl_, qh))
 
 
-def scan_kernel(rows_n, width, groups, fwd_ref, bwd_ref, x_ref, dy_ref, cr_ref, cc_ref,
+def scan_kernel(rows_n, width, groups, x_ref, dy_ref, cr_ref, cc_ref,
                 b_ref, c_ref, gv_ref, sum_ref, run_ref, dx_ref, xs_ref, ds_ref, recv1, rdec,
                 win, out3, recv3, full, parts, gather1, gather2, send1, rsem1, send2, rsem2, send3, rsem3,
                 local, dsend, drecv, hsend1, hrecv1, hsend2, hrecv2, sc_ref, pdec_ref,
-                early, pack_ref):
+                early, pack_ref, local_ref):
     me = lax.axis_index("seq")
     col = lax.axis_index("head")
     c = me % width
@@ -61,10 +61,20 @@
     for h in range(nh):
         pdec_ref[:, h * hd:(h + 1) * hd] = jnp.broadcast_to(
             jnp.exp(cc_ref[length - 1:length, h:h + 1]), (pdec_ref.shape[0], hd))
+    b_all = b_ref[...].astype(jnp.float32)
+    c_all = c_ref[...].astype(jnp.float32)
+    for h in range(nh):
+        lanes = slice(h * hd, (h + 1) * hd)
+        decayed_b = (cc_ref[:, nh + h:nh + h + 1] * b_all).astype(jnp.bfloat16)
+        decayed_c = (cc_ref[:, 2 * nh + h:2 * nh + h + 1] * c_all).astype(jnp.bfloat16)
+        local_ref[0, :, lanes] = lax.dot_general(
+            decayed_b, x_ref[:, lanes], (((0,), (0,)), ((), ())), preferred_element_type=jnp.float32)
+        local_ref[1, :, lanes] = lax.dot_general(
+            decayed_c, dy_ref[:, lanes], (((0,), (0,)), ((), ())), preferred_element_type=jnp.float32)
     span = pack_ref.shape[1] // 2
     for k in range(pack_ref.shape[0]):
-        pack_ref[k, :span, :] = fwd_ref[k * span:(k + 1) * span, :].astype(pack_ref.dtype)
-        pack_ref[k, span:, :] = bwd_ref[k * span:(k + 1) * span, :].astype(pack_ref.dtype)
+        pack_ref[k, :span, :] = local_ref[0, k * span:(k + 1) * span, :].astype(pack_ref.dtype)
+        pack_ref[k, span:, :] = local_ref[1, k * span:(k + 1) * span, :].astype(pack_ref.dtype)
 
     def heads(k):
         for _ in range(k):
@@ -312,7 +322,7 @@
             jax.ShapeDtypeStruct(x.shape, jnp.bfloat16),
             jax.ShapeDtypeStruct((groups, chunk_rows, s), jnp.bfloat16),
         ),
-        in_specs=[pl.BlockSpec(memory_space=pltpu.VMEM)] * 8,
+        in_specs=[pl.BlockSpec(memory_space=pltpu.VMEM)] * 6,
         out_specs=(pl.BlockSpec(memory_space=pltpu.VMEM),) * 2,
         scratch_shapes=[
             pltpu.VMEM((length, length), jnp.float32),
@@ -345,9 +355,10 @@
             pltpu.VMEM((8, w), jnp.float32),
             pltpu.VMEM((2, length, s), jnp.float32),
             pltpu.VMEM((width, 2 * piece, w), jnp.bfloat16),
+            pltpu.VMEM((2, s, w), jnp.float32),
         ],
         compiler_params=pltpu.CompilerParams(collective_id=1, has_side_effects=True),
-    )(forward, backward, x, dy, cumulative, columns, b_inputs, c_inputs)
+    )(x, dy, cumulative, columns, b_inputs, c_inputs)
     sums = sums.reshape(2 * length, s)
     return grad_values, sums[:length], sums[length:]
 

time: 68.2 us -> 67 us (0.982)
  Pallas kernels: 58.2 us -> 61.4 us
  local copies, waits for them, and re-layouts: 7.41 us -> 4.48 us
  matrix products: 1.47 us -> 0.21 us
    pallas_call x1, Pallas kernels: 58.2 us -> 61.4 us  [exclusive_scans(): pl.pallas_call(functools.partial(scan_kernel, rows_n, width, groups), out...]
    reshape x2 -> x0, local copies, waits for them, and re-layouts: 1.68 us -> none  [the longest x1 0.84 us: shards(): adjoint_local = jnp.einsum('hsn,shp->nhp', decayed_c, dy_heads, preferred...]
    dot_general x2 -> x0, matrix products: 1.25 us -> none  [the longest x1 0.64 us: shards(): jnp.einsum('htn,thp->nhp', decayed_b, x_heads, preferred_element_type=jnp...]
    unnamed x15 -> x7, local copies, waits for them, and re-layouts: 3.06 us -> 1.8 us
where the time goes in v16:
time: 67 us; the launch traced here: 66.8 us
  Pallas kernels  61.4 us (92%)
  local copies, waits for them, and re-layouts  4.48 us (7%)
    pallas_call x1, Pallas kernels, exclusive_scans(): pl.pallas_call(functools.partial(scan_kernel, rows_n, width, groups), out...  61.4 us
    unnamed x7, local copies, waits for them, and re-layouts  1.8 us
    slice x1, local copies, waits for them, and re-layouts, exclusive_scans(): return (grad_values, sums[:length], sums[length:])  1.68 us

profile of v16, /device:TPU:16, one launch (start us, length us, event | category | flops | bytes accessed | tf_op | source)
XLA Modules:
  0.0 66.8 jit_solution(15061914270370799524)
XLA Ops:
  0.6 0.0 copy-start
  0.6 0.7 %copy-done = f32[8,384]{1,0:T(8,128)S(1)} copy-done((f32[8,384]{1,0:T(8,128)S(1)}, f32[8,384]{1,0:T(8,128)}, u32[]{:S(2)}) %copy-start) | copy-done | bytes 12312
  1.3 0.2 convolution_bitcast_fusion.cr_ref
  1.6 0.0 copy-start.2
  1.6 0.2 slice_reduce_fusion
  1.8 0.1 subtract_exponential_fusion
  1.8 0.3 copy-done.2
  2.2 0.8 %copy.11 = f32[24,384]{0,1:T(8,128)} copy(f32[24,384]{1,0:T(8,128)S(1)} %pad_maximum_fusion) | data formatting | bytes 73728 | tf_op jit(solution)/shard_map/concatenate | solution.py:318
  3.0 61.4 %shard_map.76 = (bf16[384,512]{1,0:T(8,128)(2,1)}, bf16[8,96,128]{2,1,0:T(8,128)(2,1)}) custom-call(bf16[384,512]{1,0:T(8,128)(2,1)} %x_ref.1, bf16[384,512]{1,0:T(8,128)(2,1)} %dy_ref.1, f32[8,384]{1,0:T(8,128)} %copy-done.2, f32[384,24]{1,0:T(8,128)} %bitcast.6, bf16[384,128]{1,0:T(8,128)(2,1)} %b_ref.1, bf16[384,128]{1,0:T(8,128)(2,1)} %c_ref.1), custom_call_target="tpu_custom_call" | custom-call | tf_op jit(solution)/shard_map/pallas_call | solution.py:319
  64.4 0.0 copy-start.1
  64.4 1.7 %fusion = (bf16[4,96,128]{2,1,0:T(8,128)(2,1)}, bf16[4,96,128]{2,1,0:T(8,128)(2,1)}) fusion(bf16[8,96,128]{2,1,0:T(8,128)(2,1)} %get-tuple-element.6), kind=kLoop, calls=%fused_computation.5 | loop fusion | bytes 393216 | tf_op jit(solution)/shard_map/slice | solution.py:363
  66.1 0.0 copy-done.1
  66.1 0.7 %copy.13 = bf16[384,512]{1,0:T(8,128)(2,1)} copy(bf16[384,512]{1,0:T(8,128)(2,1)S(1)} %copy-done.1) | data formatting | bytes 786432
  (1 shorter events, 0.0 us)
Async XLA Ops:
  0.6 0.7 %copy-start = (f32[8,384]{1,0:T(8,128)S(1)}, f32[8,384]{1,0:T(8,128)}, u32[]{:S(2)}) copy-start(f32[8,384]{1,0:T(8,128)} %param.8) | copy-start | bytes 36868
  1.6 0.6 copy-start.2
  64.4 1.7 %copy-start.1 = (bf16[384,512]{1,0:T(8,128)(2,1)S(1)}, bf16[384,512]{1,0:T(8,128)(2,1)}, u32[]{:S(2)}) copy-start(bf16[384,512]{1,0:T(8,128)(2,1)} %get-tuple-element.14) | copy-start | bytes 1179652

commit v17 on v16

--- a/solution.py
+++ b/solution.py
@@ -23,11 +23,11 @@
     return nt_dot(ph, qh) + (nt_dot(ph, ql) + nt_dot(pl_, qh))
 
 
-def scan_kernel(rows_n, width, groups, x_ref, dy_ref, cr_ref, cc_ref,
+def scan_kernel(rows_n, width, groups, x_ref, dy_ref, cr_ref,
                 b_ref, c_ref, gv_ref, sum_ref, run_ref, dx_ref, xs_ref, ds_ref, recv1, rdec,
                 win, out3, recv3, full, parts, gather1, gather2, send1, rsem1, send2, rsem2, send3, rsem3,
                 local, dsend, drecv, hsend1, hrecv1, hsend2, hrecv2, sc_ref, pdec_ref,
-                early, pack_ref, local_ref):
+                early, pack_ref, local_ref, cc_ref):
     me = lax.axis_index("seq")
     col = lax.axis_index("head")
     c = me % width
@@ -36,6 +36,7 @@
     spans = [1, 2, 3, 4]
 
     length = x_ref.shape[0]
+    cc_ref[...] = cr_ref[...].T
     later = lax.broadcasted_iota(jnp.int32, (length, length), 1) >= lax.broadcasted_iota(
         jnp.int32, (length, length), 0)
     run_ref[...] = jnp.zeros(run_ref.shape, run_ref.dtype)
@@ -55,9 +56,9 @@
             x_h, dy_h, (((1,), (1,)), ((), ())), preferred_element_type=jnp.float32)
         run_ref[...] += dec * pairs
 
-    nh = cr_ref.shape[0]
+    nh = cr_ref.shape[0] // 3
     heads_left = list(range(nh))
-    hd = x_ref.shape[1] // cr_ref.shape[0]
+    hd = x_ref.shape[1] // nh
     for h in range(nh):
         pdec_ref[:, h * hd:(h + 1) * hd] = jnp.broadcast_to(
             jnp.exp(cc_ref[length - 1:length, h:h + 1]), (pdec_ref.shape[0], hd))
@@ -274,7 +275,7 @@
     adj_lo = (adj - adj_hi.astype(jnp.float32)).astype(jnp.bfloat16)
     b_adj = jnp.dot(b_ref[...], adj_hi, preferred_element_type=jnp.float32) + jnp.dot(
         b_ref[...], adj_lo, preferred_element_type=jnp.float32)
-    for h in range(cr_ref.shape[0]):
+    for h in range(nh):
         lanes = slice(h * hd, (h + 1) * hd)
         gv_ref[:, lanes] = (dx_ref[:, lanes] + cc_ref[:, nh + h:nh + h + 1] * b_adj[:, lanes]).astype(
             gv_ref.dtype)
@@ -315,14 +316,14 @@
     assert rows_n <= 8
     length = x.shape[0]
     chunk_rows = 2 * length // groups
-    columns = jnp.concatenate([cumulative, into_end, from_start], axis=0).T
+    stacked = jnp.concatenate([cumulative, into_end, from_start], axis=0)
     grad_values, sums = pl.pallas_call(
         functools.partial(scan_kernel, rows_n, width, groups),
         out_shape=(
             jax.ShapeDtypeStruct(x.shape, jnp.bfloat16),
             jax.ShapeDtypeStruct((groups, chunk_rows, s), jnp.bfloat16),
         ),
-        in_specs=[pl.BlockSpec(memory_space=pltpu.VMEM)] * 6,
+        in_specs=[pl.BlockSpec(memory_space=pltpu.VMEM)] * 5,
         out_specs=(pl.BlockSpec(memory_space=pltpu.VMEM),) * 2,
         scratch_shapes=[
             pltpu.VMEM((length, length), jnp.float32),
@@ -356,9 +357,10 @@
             pltpu.VMEM((2, length, s), jnp.float32),
             pltpu.VMEM((width, 2 * piece, w), jnp.bfloat16),
             pltpu.VMEM((2, s, w), jnp.float32),
+            pltpu.VMEM((length, 3 * cumulative.shape[0]), jnp.float32),
         ],
         compiler_params=pltpu.CompilerParams(collective_id=1, has_side_effects=True),
-    )(x, dy, cumulative, columns, b_inputs, c_inputs)
+    )(x, dy, stacked, b_inputs, c_inputs)
     sums = sums.reshape(2 * length, s)
     return grad_values, sums[:length], sums[length:]
 

time: 67 us -> 66.6 us (level)
  local copies, waits for them, and re-layouts: 4.48 us -> 3.32 us
    concatenate x1 -> x0, local copies, waits for them, and re-layouts: 0.81 us -> none  [exclusive_scans(): columns = jnp.concatenate([cumulative, into_end, from_start], axis=0).T]
    unnamed x7 -> x5, local copies, waits for them, and re-layouts: 1.8 us -> 1.46 us
where the time goes in v17:
time: 66.6 us; the launch traced here: 66.4 us
  Pallas kernels  61.5 us (92%)
  local copies, waits for them, and re-layouts  3.32 us (5%)
  other arithmetic  0.71 us (1%)
    pallas_call x1, Pallas kernels, exclusive_scans(): pl.pallas_call(functools.partial(scan_kernel, rows_n, width, groups), out...  61.5 us
    slice x1, local copies, waits for them, and re-layouts, exclusive_scans(): return (grad_values, sums[:length], sums[length:])  1.68 us
    unnamed x5, local copies, waits for them, and re-layouts  1.46 us

profile of v17, /device:TPU:16, one launch (start us, length us, event | category | flops | bytes accessed | tf_op | source)
XLA Modules:
  0.0 66.4 jit_solution(14820678640226721654)
XLA Ops:
  0.6 0.0 copy-start
  0.6 0.7 %copy-done = f32[8,384]{1,0:T(8,128)S(1)} copy-done((f32[8,384]{1,0:T(8,128)S(1)}, f32[8,384]{1,0:T(8,128)}, u32[]{:S(2)}) %copy-start) | copy-done | bytes 12312
  1.3 0.2 convolution_bitcast_fusion
  1.6 0.2 slice_reduce_fusion
  1.7 0.1 subtract_exponential_fusion
  1.8 0.6 pad_maximum_fusion.cr_ref
  2.5 61.5 %shard_map.76 = (bf16[384,512]{1,0:T(8,128)(2,1)}, bf16[8,96,128]{2,1,0:T(8,128)(2,1)}) custom-call(bf16[384,512]{1,0:T(8,128)(2,1)} %x_ref.1, bf16[384,512]{1,0:T(8,128)(2,1)} %dy_ref.1, f32[24,384]{1,0:T(8,128)} %pad_maximum_fusion.cr_ref, bf16[384,128]{1,0:T(8,128)(2,1)} %b_ref.1, bf16[384,128]{1,0:T(8,128)(2,1)} %c_ref.1), custom_call_target="tpu_custom_call" | custom-call | tf_op jit(solution)/shard_map/pallas_call | solution.py:320
  63.9 0.0 copy-start.1
  64.0 1.7 %fusion = (bf16[4,96,128]{2,1,0:T(8,128)(2,1)}, bf16[4,96,128]{2,1,0:T(8,128)(2,1)}) fusion(bf16[8,96,128]{2,1,0:T(8,128)(2,1)} %get-tuple-element.6), kind=kLoop, calls=%fused_computation.5 | loop fusion | bytes 393216 | tf_op jit(solution)/shard_map/slice | solution.py:365
  65.6 0.0 copy-done.1
  65.6 0.7 %copy.9 = bf16[384,512]{1,0:T(8,128)(2,1)} copy(bf16[384,512]{1,0:T(8,128)(2,1)S(1)} %copy-done.1) | data formatting | bytes 786432
Async XLA Ops:
  0.6 0.7 %copy-start = (f32[8,384]{1,0:T(8,128)S(1)}, f32[8,384]{1,0:T(8,128)}, u32[]{:S(2)}) copy-start(f32[8,384]{1,0:T(8,128)} %param.8) | copy-start | bytes 36868
  63.9 1.7 %copy-start.1 = (bf16[384,512]{1,0:T(8,128)(2,1)S(1)}, bf16[384,512]{1,0:T(8,128)(2,1)}, u32[]{:S(2)}) copy-start(bf16[384,512]{1,0:T(8,128)(2,1)} %get-tuple-element.14) | copy-start | bytes 1179652

commit v18 on v17

--- a/solution.py
+++ b/solution.py
@@ -102,7 +102,7 @@
     for d in spans:
         peers = peers + ((rows_n - 1 - y) // d + rows_n - 1) // rows_n + (y // d + rows_n - 1) // rows_n
     sc_ref[...] = nt_dot(b_ref[...], c_ref[...])
-    heads(2)
+    heads(1)
     pl.semaphore_wait(barrier, peers)
 
     own = pltpu.make_async_copy(pack_ref.at[c], recv1.at[c], local.at[0])

time: 66.6 us -> 66.6 us (level)
  no operation moved by 1% of the time
where the time goes in v18:
time: 66.6 us; the launch traced here: 66.4 us
  Pallas kernels  61.5 us (92%)
  local copies, waits for them, and re-layouts  3.32 us (5%)
  other arithmetic  0.71 us (1%)
    pallas_call x1, Pallas kernels, exclusive_scans(): pl.pallas_call(functools.partial(scan_kernel, rows_n, width, groups), out...  61.5 us
    slice x1, local copies, waits for them, and re-layouts, exclusive_scans(): return (grad_values, sums[:length], sums[length:])  1.68 us
    unnamed x5, local copies, waits for them, and re-layouts  1.46 us

profile of v18, /device:TPU:16, one launch (start us, length us, event | category | flops | bytes accessed | tf_op | source)
XLA Modules:
  0.0 66.4 jit_solution(1997608907350660101)
XLA Ops:
  0.6 0.0 copy-start
  0.6 0.7 %copy-done = f32[8,384]{1,0:T(8,128)S(1)} copy-done((f32[8,384]{1,0:T(8,128)S(1)}, f32[8,384]{1,0:T(8,128)}, u32[]{:S(2)}) %copy-start) | copy-done | bytes 12312
  1.3 0.2 convolution_bitcast_fusion
  1.6 0.2 slice_reduce_fusion
  1.7 0.1 subtract_exponential_fusion
  1.8 0.6 pad_maximum_fusion.cr_ref
  2.5 61.5 %shard_map.76 = (bf16[384,512]{1,0:T(8,128)(2,1)}, bf16[8,96,128]{2,1,0:T(8,128)(2,1)}) custom-call(bf16[384,512]{1,0:T(8,128)(2,1)} %x_ref.1, bf16[384,512]{1,0:T(8,128)(2,1)} %dy_ref.1, f32[24,384]{1,0:T(8,128)} %pad_maximum_fusion.cr_ref, bf16[384,128]{1,0:T(8,128)(2,1)} %b_ref.1, bf16[384,128]{1,0:T(8,128)(2,1)} %c_ref.1), custom_call_target="tpu_custom_call" | custom-call | tf_op jit(solution)/shard_map/pallas_call | solution.py:320
  63.9 0.0 copy-start.1
  64.0 1.7 %fusion = (bf16[4,96,128]{2,1,0:T(8,128)(2,1)}, bf16[4,96,128]{2,1,0:T(8,128)(2,1)}) fusion(bf16[8,96,128]{2,1,0:T(8,128)(2,1)} %get-tuple-element.6), kind=kLoop, calls=%fused_computation.5 | loop fusion | bytes 393216 | tf_op jit(solution)/shard_map/slice | solution.py:365
  65.6 0.0 copy-done.1
  65.6 0.7 %copy.9 = bf16[384,512]{1,0:T(8,128)(2,1)} copy(bf16[384,512]{1,0:T(8,128)(2,1)S(1)} %copy-done.1) | data formatting | bytes 786432
Async XLA Ops:
  0.6 0.7 %copy-start = (f32[8,384]{1,0:T(8,128)S(1)}, f32[8,384]{1,0:T(8,128)}, u32[]{:S(2)}) copy-start(f32[8,384]{1,0:T(8,128)} %param.8) | copy-start | bytes 36868
  63.9 1.7 %copy-start.1 = (bf16[384,512]{1,0:T(8,128)(2,1)S(1)}, bf16[384,512]{1,0:T(8,128)(2,1)}, u32[]{:S(2)}) copy-start(bf16[384,512]{1,0:T(8,128)(2,1)} %get-tuple-element.14) | copy-start | bytes 1179652

commit v19 on v18

--- a/solution.py
+++ b/solution.py
@@ -102,7 +102,7 @@
     for d in spans:
         peers = peers + ((rows_n - 1 - y) // d + rows_n - 1) // rows_n + (y // d + rows_n - 1) // rows_n
     sc_ref[...] = nt_dot(b_ref[...], c_ref[...])
-    heads(1)
+    heads(0)
     pl.semaphore_wait(barrier, peers)
 
     own = pltpu.make_async_copy(pack_ref.at[c], recv1.at[c], local.at[0])

time: 66.6 us -> 66.6 us (level)
  no operation moved by 1% of the time
where the time goes in v19:
time: 66.6 us; the launch traced here: 66.4 us
  Pallas kernels  61.5 us (92%)
  local copies, waits for them, and re-layouts  3.32 us (5%)
  other arithmetic  0.71 us (1%)
    pallas_call x1, Pallas kernels, exclusive_scans(): pl.pallas_call(functools.partial(scan_kernel, rows_n, width, groups), out...  61.5 us
    slice x1, local copies, waits for them, and re-layouts, exclusive_scans(): return (grad_values, sums[:length], sums[length:])  1.68 us
    unnamed x5, local copies, waits for them, and re-layouts  1.46 us

profile of v19, /device:TPU:16, one launch (start us, length us, event | category | flops | bytes accessed | tf_op | source)
XLA Modules:
  0.0 66.4 jit_solution(4871114639552205894)
XLA Ops:
  0.6 0.0 copy-start
  0.6 0.7 %copy-done = f32[8,384]{1,0:T(8,128)S(1)} copy-done((f32[8,384]{1,0:T(8,128)S(1)}, f32[8,384]{1,0:T(8,128)}, u32[]{:S(2)}) %copy-start) | copy-done | bytes 12312
  1.3 0.2 convolution_bitcast_fusion
  1.6 0.2 slice_reduce_fusion
  1.7 0.1 subtract_exponential_fusion
  1.8 0.6 pad_maximum_fusion.cr_ref
  2.5 61.5 %shard_map.76 = (bf16[384,512]{1,0:T(8,128)(2,1)}, bf16[8,96,128]{2,1,0:T(8,128)(2,1)}) custom-call(bf16[384,512]{1,0:T(8,128)(2,1)} %x_ref.1, bf16[384,512]{1,0:T(8,128)(2,1)} %dy_ref.1, f32[24,384]{1,0:T(8,128)} %pad_maximum_fusion.cr_ref, bf16[384,128]{1,0:T(8,128)(2,1)} %b_ref.1, bf16[384,128]{1,0:T(8,128)(2,1)} %c_ref.1), custom_call_target="tpu_custom_call" | custom-call | tf_op jit(solution)/shard_map/pallas_call | solution.py:320
  63.9 0.0 copy-start.1
  64.0 1.7 %fusion = (bf16[4,96,128]{2,1,0:T(8,128)(2,1)}, bf16[4,96,128]{2,1,0:T(8,128)(2,1)}) fusion(bf16[8,96,128]{2,1,0:T(8,128)(2,1)} %get-tuple-element.6), kind=kLoop, calls=%fused_computation.5 | loop fusion | bytes 393216 | tf_op jit(solution)/shard_map/slice | solution.py:365
  65.6 0.0 copy-done.1
  65.6 0.7 %copy.9 = bf16[384,512]{1,0:T(8,128)(2,1)} copy(bf16[384,512]{1,0:T(8,128)(2,1)S(1)} %copy-done.1) | data formatting | bytes 786432
Async XLA Ops:
  0.6 0.7 %copy-start = (f32[8,384]{1,0:T(8,128)S(1)}, f32[8,384]{1,0:T(8,128)}, u32[]{:S(2)}) copy-start(f32[8,384]{1,0:T(8,128)} %param.8) | copy-start | bytes 36868
  63.9 1.7 %copy-start.1 = (bf16[384,512]{1,0:T(8,128)(2,1)S(1)}, bf16[384,512]{1,0:T(8,128)(2,1)}, u32[]{:S(2)}) copy-start(bf16[384,512]{1,0:T(8,128)(2,1)} %get-tuple-element.14) | copy-start | bytes 1179652

commit v20 on v18

--- a/solution.py
+++ b/solution.py
@@ -122,7 +122,7 @@
             recv_sem=drecv.at[off], device_id=(y * width + k, col), device_id_type=MESH)
         cp.start()
         sends.append(cp)
-    heads(3)
+    heads(4)
     for off in range(1, width):
         k = (c + width - off) % width
         pltpu.make_async_remote_copy(

time: 66.6 us -> 66.6 us (level)
  no operation moved by 1% of the time
where the time goes in v20:
time: 66.6 us; the launch traced here: 66.4 us
  Pallas kernels  61.5 us (92%)
  local copies, waits for them, and re-layouts  3.32 us (5%)
  other arithmetic  0.71 us (1%)
    pallas_call x1, Pallas kernels, exclusive_scans(): pl.pallas_call(functools.partial(scan_kernel, rows_n, width, groups), out...  61.5 us
    slice x1, local copies, waits for them, and re-layouts, exclusive_scans(): return (grad_values, sums[:length], sums[length:])  1.68 us
    unnamed x5, local copies, waits for them, and re-layouts  1.46 us

profile of v20, /device:TPU:16, one launch (start us, length us, event | category | flops | bytes accessed | tf_op | source)
XLA Modules:
  0.0 66.4 jit_solution(436993538359420006)
XLA Ops:
  0.6 0.0 copy-start
  0.6 0.7 %copy-done = f32[8,384]{1,0:T(8,128)S(1)} copy-done((f32[8,384]{1,0:T(8,128)S(1)}, f32[8,384]{1,0:T(8,128)}, u32[]{:S(2)}) %copy-start) | copy-done | bytes 12312
  1.3 0.2 convolution_bitcast_fusion
  1.6 0.2 slice_reduce_fusion
  1.7 0.1 subtract_exponential_fusion
  1.8 0.6 pad_maximum_fusion.cr_ref
  2.5 61.5 %shard_map.76 = (bf16[384,512]{1,0:T(8,128)(2,1)}, bf16[8,96,128]{2,1,0:T(8,128)(2,1)}) custom-call(bf16[384,512]{1,0:T(8,128)(2,1)} %x_ref.1, bf16[384,512]{1,0:T(8,128)(2,1)} %dy_ref.1, f32[24,384]{1,0:T(8,128)} %pad_maximum_fusion.cr_ref, bf16[384,128]{1,0:T(8,128)(2,1)} %b_ref.1, bf16[384,128]{1,0:T(8,128)(2,1)} %c_ref.1), custom_call_target="tpu_custom_call" | custom-call | tf_op jit(solution)/shard_map/pallas_call | solution.py:320
  63.9 0.0 copy-start.1
  64.0 1.7 %fusion = (bf16[4,96,128]{2,1,0:T(8,128)(2,1)}, bf16[4,96,128]{2,1,0:T(8,128)(2,1)}) fusion(bf16[8,96,128]{2,1,0:T(8,128)(2,1)} %get-tuple-element.6), kind=kLoop, calls=%fused_computation.5 | loop fusion | bytes 393216 | tf_op jit(solution)/shard_map/slice | solution.py:365
  65.6 0.0 copy-done.1
  65.6 0.7 %copy.9 = bf16[384,512]{1,0:T(8,128)(2,1)} copy(bf16[384,512]{1,0:T(8,128)(2,1)S(1)} %copy-done.1) | data formatting | bytes 786432
Async XLA Ops:
  0.6 0.7 %copy-start = (f32[8,384]{1,0:T(8,128)S(1)}, f32[8,384]{1,0:T(8,128)}, u32[]{:S(2)}) copy-start(f32[8,384]{1,0:T(8,128)} %param.8) | copy-start | bytes 36868
  63.9 1.7 %copy-start.1 = (bf16[384,512]{1,0:T(8,128)(2,1)S(1)}, bf16[384,512]{1,0:T(8,128)(2,1)}, u32[]{:S(2)}) copy-start(bf16[384,512]{1,0:T(8,128)(2,1)} %get-tuple-element.14) | copy-start | bytes 1179652
